TPU v7x, 32 devices: a whole 2x2x4 slice. The times are simulated.
32 devices in a mesh: dp: 4 (over z), row: 2 (over x), col: 4 (over y, core).
Axes of the slice: x: 2, y: 2, z: 4, core: 2. Of those that a mesh axis runs over, the one named last changes fastest.
Arguments:
- layer_input: bfloat16 [16384, 2048], P(('dp', 'row'), 'col'), may hold values from -6 to 6
- norm1_gain: float32 [2048], P('col'), may hold values from 0.5 to 1.5
- norm1_shift: float32 [2048], P('col'), may hold values from -3 to 3
- w_query: bfloat16 [2048, 2048], P('col', 'row'), may hold values from -0.125 to 0.125
- b_query: float32 [2048], P('row'), may hold values from -3 to 3
- w_keyval: bfloat16 [2048, 256], P('col'), may hold values from -0.125 to 0.125
- b_value: float32 [128], replicated, may hold values from -3 to 3
- w_attn_out: bfloat16 [2048, 2048], P('row', 'col'), may hold values from -3 to 3
- b_attn_out: float32 [2048], P('col'), may hold values from -3 to 3
- norm2_gain: float32 [2048], P('col'), may hold values from 0.5 to 1.5
- norm2_shift: float32 [2048], P('col'), may hold values from -3 to 3
- w_fc_in: bfloat16 [2048, 8192], P('col', 'row'), may hold values from -0.125 to 0.125
- b_fc_in: float32 [8192], P('row'), may hold values from -3 to 3
- w_fc_out: bfloat16 [8192, 2048], P('row', 'col'), may hold values from -0.125 to 0.125
- b_fc_out: float32 [2048], P('col'), may hold values from -3 to 3
- valid_mask: int32 [4, 4096], P('dp'), may hold values from 0 to 1, as said below
- block_ids: int32 [4, 4096], P('dp'), may hold values from 0 to 31, never falling along the last dimension, each value on 1 to 256 neighbouring positions
- teacher: bfloat16 [16384, 2048], P(('dp', 'row'), 'col'), may hold values from -6 to 6
- out_cotangent: bfloat16 [16384, 2048], P(('dp', 'row'), 'col'), may hold values from -6 to 6
Outputs:
- layer_output: float32 [16384, 2048], P(('dp', 'row'), 'col')
- loss_value: float32 [], replicated
- input_grad: float32 [16384, 2048], P(('dp', 'row'), 'col')
- grad_norm1_gain: float32 [2048], P('col')
- grad_norm1_shift: float32 [2048], P('col')
- grad_w_query: float32 [2048, 2048], P('col', 'row')
- grad_b_query: float32 [2048], P('row')
- grad_w_keyval: float32 [2048, 256], P('col')
- grad_b_value: float32 [128], replicated
- grad_w_attn_out: float32 [2048, 2048], P('row', 'col')
- grad_b_attn_out: float32 [2048], P('col')
- grad_norm2_gain: float32 [2048], P('col')
- grad_norm2_shift: float32 [2048], P('col')
- grad_w_fc_in: float32 [2048, 8192], P('col', 'row')
- grad_b_fc_in: float32 [8192], P('row')
- grad_w_fc_out: float32 [8192, 2048], P('row', 'col')
- grad_b_fc_out: float32 [2048], P('col')
Inputs may be any that keep to these rules, and one draw needn't show every extreme that they name: `valid_mask`: in each sequence the ones form a prefix of 1024 to 4096 positions and zeros follow; the first sequence has no padding. `block_ids`: within each sequence block numbers never fall along positions; each block holds 1 to 256 positions.
All inputs are finite; a program needn't handle non-finite values.
Results may differ from a plain program's by a relative error of at most 0.0034.
Values may be sent and summed in bfloat16 or wider, within the bound.
No kernel may reach another device: no remote copies, remote signals or barrier semaphores. Data moves between devices by JAX's collectives and lax.ppermute only.
A program may use at most 448 MiB of HBM per device.

v0:
```python
import jax
import jax.numpy as jnp
from jax import lax
from jax.sharding import PartitionSpec as P

D = 2048
HEAD = 128
SEQ = 4096
QROWS = 512


epsilon = 1e-05
gelu_coeff = 0.7978845608028654


def gelu_tanh(values):
    return (
        0.5 * values * (1.0 + jnp.tanh(gelu_coeff * (values + 0.044715 * values * values * values)))
    )


def feature_sums(first_term, second_term):
    return lax.psum((jnp.sum(first_term, 1), jnp.sum(second_term, 1)), "col")


def norm_forward(values, gain, shift):
    totals, squares = feature_sums(values, values * values)
    means = totals / D
    inverse = lax.rsqrt(squares / D - means * means + epsilon)
    normal = (values - means[:, None]) * inverse[:, None]
    return (normal, inverse, normal * gain + shift)


def norm_backward(grad, normal, inverse, gain):
    scaled = grad * gain
    totals, mixed_sums = feature_sums(scaled, scaled * normal)
    return inverse[:, None] * (scaled - totals[:, None] / D - normal * mixed_sums[:, None] / D)


def product_term(whole, weight, transposed):
    if transposed:
        return lax.dot_general(
            whole, weight, (((1,), (1,)), ((), ())), preferred_element_type=jnp.float32
        )
    return jnp.dot(whole, weight, preferred_element_type=jnp.float32)


def rows_gather(part):
    return lax.all_gather(part, "row", axis=0, tiled=True)


def cols_gather(part):
    return lax.all_gather(part, "col", axis=0, tiled=True)


def cols_scatter(whole, weight):
    return lax.psum_scatter(
        product_term(whole, weight, False), "col", scatter_dimension=0, tiled=True
    )


def rows_scatter(whole, weight):
    return lax.psum_scatter(
        product_term(whole, weight, False), "row", scatter_dimension=0, tiled=True
    )


def back_rows_gather(part):
    return lax.all_gather(part, "row", axis=0, tiled=True)


def back_cols_gather(part):
    return lax.all_gather(part, "col", axis=0, tiled=True)


def back_cols_scatter(whole, weight):
    return lax.psum_scatter(
        product_term(whole, weight, True), "col", scatter_dimension=0, tiled=True
    )


def back_rows_scatter(whole, weight):
    return lax.psum_scatter(
        product_term(whole, weight, True), "row", scatter_dimension=0, tiled=True
    )


def weight_product(left, right):
    return lax.dot_general(
        left, right, (((0,), (0,)), ((), ())), preferred_element_type=jnp.float32
    )


def allowed_pairs(valid_flat, block_flat, query_start):
    query_ids = lax.dynamic_slice_in_dim(block_flat, query_start, QROWS, 0)
    return (block_flat[None, :] <= query_ids[:, None]) & (valid_flat[None, :] > 0)


def block_operands(query_low, key_low, value_low, valid_flat, block_flat, first_row, block_index):
    heads_here = query_low.shape[1] // HEAD
    offset = block_index * QROWS
    query_start = first_row + offset
    key_start = query_start // SEQ * SEQ
    query_block = lax.dynamic_slice_in_dim(query_low, offset, QROWS, 0).reshape(
        QROWS, heads_here, HEAD
    )
    allowed = allowed_pairs(valid_flat, block_flat, query_start)
    scores = jnp.einsum(
        "qhd,kd->hqk", query_block, key_low, preferred_element_type=jnp.float32
    ) * HEAD ** (-0.5)
    scores = jnp.where(allowed[None], scores, -1e30)
    return (offset, key_start, query_block, key_low, value_low, allowed, scores)


def attend_forward(query_low, key_low, value_low, valid_flat, block_flat, first_row):
    count_blocks = query_low.shape[0] // QROWS

    def one_block(block_index):
        offset, key_start, query_block, key_block, value_block, allowed, scores = block_operands(
            query_low, key_low, value_low, valid_flat, block_flat, first_row, block_index
        )
        maxima = jnp.max(scores, -1, keepdims=True)
        exp_scores = jnp.where(allowed[None], jnp.exp(scores - maxima), 0.0)
        totals = jnp.sum(exp_scores, -1, keepdims=True)
        probs = (exp_scores / totals).astype(jnp.bfloat16)
        attended = jnp.einsum("hqk,kd->qhd", probs, value_block, preferred_element_type=jnp.float32)
        return (attended.reshape(QROWS, query_low.shape[1]), maxima + jnp.log(totals))

    attended, log_totals = lax.map(one_block, jnp.arange(count_blocks, dtype=jnp.int32))
    return (attended.reshape(-1, query_low.shape[1]), log_totals)


def attend_backward(
    query_low,
    key_low,
    value_low,
    grad_low,
    log_totals,
    valid_flat,
    block_flat,
    first_row,
    tok_group,
):
    count_blocks = query_low.shape[0] // QROWS
    heads_here = query_low.shape[1] // HEAD

    def one_block(carry, operands):
        block_index, block_lse = operands
        offset, key_start, query_block, key_block, value_block, allowed, scores = block_operands(
            query_low, key_low, value_low, valid_flat, block_flat, first_row, block_index
        )
        probs = jnp.where(allowed[None], jnp.exp(scores - block_lse), 0.0)
        grad_block = lax.dynamic_slice_in_dim(grad_low, offset, QROWS, 0).reshape(
            QROWS, heads_here, HEAD
        )
        grad_probs = jnp.einsum(
            "qhd,kd->hqk", grad_block, value_block, preferred_element_type=jnp.float32
        )
        centers = jnp.sum(probs * grad_probs, -1, keepdims=True)
        grad_scores = (probs * (grad_probs - centers) * HEAD ** (-0.5)).astype(jnp.bfloat16)
        grad_queries = jnp.einsum(
            "hqk,kd->qhd", grad_scores, key_block, preferred_element_type=jnp.float32
        )
        grad_keys = jnp.einsum(
            "hqk,qhd->kd", grad_scores, query_block, preferred_element_type=jnp.float32
        )
        grad_values = jnp.einsum(
            "hqk,qhd->kd",
            probs.astype(jnp.bfloat16),
            grad_block,
            preferred_element_type=jnp.float32,
        )
        current = carry
        carry = current + jnp.concatenate([grad_keys, grad_values], 1)
        return (carry, grad_queries.reshape(QROWS, heads_here * HEAD))

    initial = jnp.zeros((tok_group, 2 * HEAD), jnp.float32)
    grad_keyval, grad_queries = lax.scan(
        one_block, initial, (jnp.arange(count_blocks, dtype=jnp.int32), log_totals)
    )
    return (grad_queries.reshape(-1, heads_here * HEAD), grad_keyval)


def per_device(
    layer_input,
    norm1_gain,
    norm1_shift,
    w_query,
    b_query,
    w_keyval,
    b_value,
    w_attn_out,
    b_attn_out,
    norm2_gain,
    norm2_shift,
    w_fc_in,
    b_fc_in,
    w_fc_out,
    b_fc_out,
    valid_mask,
    block_ids,
    teacher,
    out_cotangent,
):
    count_row = lax.axis_size("row")
    count_col = lax.axis_size("col")
    rows_a = layer_input.shape[0]
    tok_group = rows_a * count_row
    rows_b = tok_group // count_col
    own_start = lax.axis_index("row") * rows_a
    first_row = lax.axis_index("col") * rows_b
    valid_flat = valid_mask.reshape(-1)
    block_flat = block_ids.reshape(-1)
    residual = layer_input.astype(jnp.float32)
    normal1, inverse1, normed1 = norm_forward(residual, norm1_gain, norm1_shift)
    normed1_low = normed1.astype(jnp.bfloat16)
    gathered1 = rows_gather(normed1_low)
    query_low = (cols_scatter(gathered1, w_query) + b_query).astype(jnp.bfloat16)
    keyval = lax.psum(jnp.dot(gathered1, w_keyval, preferred_element_type=jnp.float32), "col")
    key_low = keyval[:, :HEAD].astype(jnp.bfloat16)
    value_low = (keyval[:, HEAD:] + b_value).astype(jnp.bfloat16)
    attended, log_totals = attend_forward(
        query_low, key_low, value_low, valid_flat, block_flat, first_row
    )
    attended_low = attended.astype(jnp.bfloat16)
    attended_all = cols_gather(attended_low)
    middle = residual + rows_scatter(attended_all, w_attn_out) + b_attn_out
    normal2, inverse2, normed2 = norm_forward(middle, norm2_gain, norm2_shift)
    normed2_low = normed2.astype(jnp.bfloat16)
    gathered2 = rows_gather(normed2_low)
    pre_act = cols_scatter(gathered2, w_fc_in) + b_fc_in
    act_value, gelu_back = jax.vjp(gelu_tanh, pre_act)
    act_low = act_value.astype(jnp.bfloat16)
    act_all = cols_gather(act_low)
    layer_output = middle + rows_scatter(act_all, w_fc_out) + b_fc_out
    own_valid = lax.dynamic_slice_in_dim(valid_flat, own_start, rows_a, 0).astype(jnp.float32)
    errors = layer_output - teacher.astype(jnp.float32)
    loss_terms = lax.psum(
        (jnp.sum(own_valid), jnp.sum(own_valid[:, None] * errors * errors)), ("dp", "row", "col")
    )
    valid_count = loss_terms[0] / count_col
    loss_value = loss_terms[1] / (valid_count * D)
    ratio = tok_group * lax.axis_size("dp") / valid_count
    grad_out = out_cotangent.astype(jnp.float32) + ratio * own_valid[:, None] * errors
    grad_mlp_all = back_rows_gather(grad_out.astype(jnp.bfloat16))
    grad_fc_out = weight_product(act_all, grad_mlp_all)
    grad_fc_out_bias = jnp.sum(grad_mlp_all, 0, dtype=jnp.float32)
    grad_act = back_cols_scatter(grad_mlp_all, w_fc_out)
    grad_pre_low = gelu_back(grad_act)[0].astype(jnp.bfloat16)
    grad_pre_all = back_cols_gather(grad_pre_low)
    grad_fc_in = weight_product(gathered2, grad_pre_all)
    grad_fc_in_bias = jnp.sum(grad_pre_all, 0, dtype=jnp.float32)
    grad_normed2 = back_rows_scatter(grad_pre_all, w_fc_in)
    gain2_part = jnp.sum(grad_normed2 * normal2, 0)
    shift2_part = jnp.sum(grad_normed2, 0)
    grad_middle = grad_out + norm_backward(grad_normed2, normal2, inverse2, norm2_gain)
    grad_attn_all = back_rows_gather(grad_middle.astype(jnp.bfloat16))
    grad_attn_out = weight_product(attended_all, grad_attn_all)
    grad_attn_bias = jnp.sum(grad_attn_all, 0, dtype=jnp.float32)
    grad_attended_low = back_cols_scatter(grad_attn_all, w_attn_out).astype(jnp.bfloat16)
    grad_queries, grad_keyval = attend_backward(
        query_low,
        key_low,
        value_low,
        grad_attended_low,
        log_totals,
        valid_flat,
        block_flat,
        first_row,
        tok_group,
    )
    grad_keyval_low = lax.psum(grad_keyval, ("row", "col")).astype(jnp.bfloat16)
    grad_value_bias = jnp.sum(grad_keyval_low[:, HEAD:], 0, dtype=jnp.float32)
    grad_query_all = back_cols_gather(grad_queries.astype(jnp.bfloat16))
    grad_query_w = weight_product(gathered1, grad_query_all)
    grad_query_bias = jnp.sum(grad_query_all, 0, dtype=jnp.float32)
    grad_keyval_w = weight_product(gathered1, grad_keyval_low)
    own_keyval = lax.dynamic_slice_in_dim(grad_keyval_low, own_start, rows_a, 0)
    grad_normed1 = back_rows_scatter(grad_query_all, w_query) + lax.dot_general(
        own_keyval, w_keyval, (((1,), (1,)), ((), ())), preferred_element_type=jnp.float32
    )
    gain1_part = jnp.sum(grad_normed1 * normal1, 0)
    shift1_part = jnp.sum(grad_normed1, 0)
    input_grad = grad_middle + norm_backward(grad_normed1, normal1, inverse1, norm1_gain)
    gain1_sum, shift1_sum, gain2_sum, shift2_sum = lax.psum(
        (gain1_part, shift1_part, gain2_part, shift2_part), ("dp", "row")
    )
    summed = lax.psum(
        (
            grad_query_w,
            grad_query_bias,
            grad_keyval_w,
            grad_value_bias,
            grad_attn_out,
            grad_attn_bias,
            grad_fc_in,
            grad_fc_in_bias,
            grad_fc_out,
            grad_fc_out_bias,
        ),
        "dp",
    )
    return (
        layer_output,
        loss_value,
        input_grad,
        gain1_sum,
        shift1_sum,
        summed[0],
        summed[1],
        summed[2],
        summed[3],
        summed[4],
        summed[5],
        gain2_sum,
        shift2_sum,
        summed[6],
        summed[7],
        summed[8],
        summed[9],
    )


def solution(mesh):
    placed = (
        P(("dp", "row"), "col"),
        P("col"),
        P("col"),
        P("col", "row"),
        P("row"),
        P("col", None),
        P(),
        P("row", "col"),
        P("col"),
        P("col"),
        P("col"),
        P("col", "row"),
        P("row"),
        P("row", "col"),
        P("col"),
        P("dp", None),
        P("dp", None),
        P(("dp", "row"), "col"),
        P(("dp", "row"), "col"),
    )
    return jax.shard_map(
        per_device,
        mesh=mesh,
        in_specs=placed,
        out_specs=(
            P(("dp", "row"), "col"),
            P(),
            P(("dp", "row"), "col"),
            P("col"),
            P("col"),
            P("col", "row"),
            P("row"),
            P("col", None),
            P(),
            P("row", "col"),
            P("col"),
            P("col"),
            P("col"),
            P("col", "row"),
            P("row"),
            P("row", "col"),
            P("col"),
        ),
        check_vma=False,
    )
```

profile of v0, /device:TPU:0, one launch (start us, length us, event | category | flops | bytes accessed | tf_op | source)
XLA Modules:
  0.0 4217.3 jit_solution(16304057358142107234)
XLA Ops:
  26.1 57.1 %all-gather.9.cloned.1.call-done = bf16[4096,512]{1,0:T(8,128)(2,1)} async-done(((bf16[2048,512]{1,0:T(8,128)(2,1)}), bf16[4096,512]{1,0:T(8,128)(2,1)}) %all-gather.9.cloned.1.call-update) | async-done | bytes 4194320 | tf_op jit(solution)/shard_map/all_gather | solution.py:49
  100.4 74.0 %all-reduce.14.cloned.1.call-done = f32[4096,256]{1,0:T(8,128)} async-done(((f32[4096,256]{1,0:T(8,128)}), f32[4096,256]{1,0:T(8,128)}) %all-reduce.14.cloned.1.call-update) | async-done | bytes 4194320 | tf_op jit(solution)/shard_map/psum | solution.py:219
  180.1 122.0 %reduce-scatter.13.cloned.1.call-done = f32[1024,1024]{1,0:T(8,128)} async-done(((f32[4096,1024]{1,0:T(8,128)}), f32[1024,1024]{1,0:T(8,128)}) %reduce-scatter.13.cloned.1.call-update) | async-done | bytes 4194320 | tf_op jit(solution)/shard_map/reduce_scatter | solution.py:57
  311.8 180.2 %while.25 = (s32[]{:T(128)}, bf16[2,512,1024]{2,1,0:T(8,128)(2,1)}, f32[2,8,512,1]{2,1,3,0:T(8,128)}, s32[1,4096]{1,0:T(1,128)S(1)}, s32[2]{0:T(128)S(1)}, /*ind...) while((s32[]{:T(128)}, bf16[2,512,1024]{2,1,0:T(8,128)(2,1)}, ...), condition=%wide.region_9.10_spmd, body=%wide.region_6.9_spmd.sunk | while | flops 8829009920 | bytes 220772896 | solution.py:129
  317.2 28.2 bitcast_reduce_fusion.2
  369.4 29.8 fusion.131
  407.0 28.2 bitcast_reduce_fusion.2
  459.2 29.8 fusion.131
  492.1 58.4 %all-gather.11.cloned.1.call-done = bf16[4096,1024]{1,0:T(8,128)(2,1)} async-done(((bf16[1024,1024]{1,0:T(8,128)(2,1)}), bf16[4096,1024]{1,0:T(8,128)(2,1)}) %all-gather.11.cloned.1.call-update) | async-done | bytes 8388624 | tf_op jit(solution)/shard_map/all_gather | solution.py:53
  560.7 99.4 %reduce-scatter.15.cloned.1.call-done = f32[2048,512]{1,0:T(8,128)} async-done(((f32[4096,512]{1,0:T(8,128)}), f32[2048,512]{1,0:T(8,128)}) %reduce-scatter.15.cloned.1.call-update) | async-done | bytes 4194320 | tf_op jit(solution)/shard_map/reduce_scatter | solution.py:63
  679.8 56.3 %all-gather.13.cloned.1.call-done = bf16[4096,512]{1,0:T(8,128)(2,1)} async-done(((bf16[2048,512]{1,0:T(8,128)(2,1)}), bf16[4096,512]{1,0:T(8,128)(2,1)}) %all-gather.13.cloned.1.call-update) | async-done | bytes 4194320 | tf_op jit(solution)/shard_map/all_gather | solution.py:49
  736.2 30.0 fusion.66
  766.2 447.0 %reduce-scatter.25.cloned.1.call-done = f32[1024,4096]{1,0:T(8,128)} async-done(((f32[4096,4096]{1,0:T(8,128)}), f32[1024,4096]{1,0:T(8,128)}) %reduce-scatter.25.cloned.1.call-update) | async-done | bytes 16777232
  1224.8 201.6 %all-gather.15.cloned.1.call-done = bf16[4096,4096]{1,0:T(8,128)(2,1)} async-done(((bf16[1024,4096]{1,0:T(8,128)(2,1)}), bf16[4096,4096]{1,0:T(8,128)(2,1)}) %all-gather.15.cloned.1.call-update) | async-done | bytes 33554448 | tf_op jit(solution)/shard_map/all_gather | solution.py:53
  1452.8 98.2 %reduce-scatter.17.cloned.1.call-done = f32[2048,512]{1,0:T(8,128)} async-done(((f32[4096,512]{1,0:T(8,128)}), f32[2048,512]{1,0:T(8,128)}) %reduce-scatter.17.cloned.1.call-update) | async-done | bytes 4194320 | tf_op jit(solution)/shard_map/reduce_scatter | solution.py:63
  1556.9 39.5 all-reduce.2
  1602.2 57.7 %all-gather.17.cloned.1.call-done = bf16[4096,512]{1,0:T(8,128)(2,1)} async-done(((bf16[2048,512]{1,0:T(8,128)(2,1)}), bf16[4096,512]{1,0:T(8,128)(2,1)}) %all-gather.17.cloned.1.call-update) | async-done | bytes 4194320 | tf_op jit(solution)/shard_map/all_gather | solution.py:69
  1659.9 30.0 fusion.68
  1690.0 447.0 %reduce-scatter.27.cloned.1.call-done = f32[1024,4096]{1,0:T(8,128)} async-done(((f32[4096,4096]{1,0:T(8,128)}), f32[1024,4096]{1,0:T(8,128)}) %reduce-scatter.27.cloned.1.call-update) | async-done | bytes 16777232
  2157.2 201.6 %all-gather.19.cloned.1.call-done = bf16[4096,4096]{1,0:T(8,128)(2,1)} async-done(((bf16[1024,4096]{1,0:T(8,128)(2,1)}), bf16[4096,4096]{1,0:T(8,128)(2,1)}) %all-gather.19.cloned.1.call-update) | async-done | bytes 33554448 | tf_op jit(solution)/shard_map/all_gather | solution.py:73
  2383.9 99.4 %reduce-scatter.19.cloned.1.call-done = f32[2048,512]{1,0:T(8,128)} async-done(((f32[4096,512]{1,0:T(8,128)}), f32[2048,512]{1,0:T(8,128)}) %reduce-scatter.19.cloned.1.call-update) | async-done | bytes 4194320 | tf_op jit(solution)/shard_map/reduce_scatter | solution.py:83
  2508.5 56.3 %all-gather.21.cloned.1.call-done = bf16[4096,512]{1,0:T(8,128)(2,1)} async-done(((bf16[2048,512]{1,0:T(8,128)(2,1)}), bf16[4096,512]{1,0:T(8,128)(2,1)}) %all-gather.21.cloned.1.call-update) | async-done | bytes 4194320 | tf_op jit(solution)/shard_map/all_gather | solution.py:69
  2576.9 123.5 %reduce-scatter.21.cloned.1.call-done = f32[1024,1024]{1,0:T(8,128)} async-done(((f32[4096,1024]{1,0:T(8,128)}), f32[1024,1024]{1,0:T(8,128)}) %reduce-scatter.21.cloned.1.call-update) | async-done | bytes 4194320 | tf_op jit(solution)/shard_map/reduce_scatter | solution.py:77
  2705.8 528.1 %while.26 = (s32[]{:T(128)}, f32[4096,256]{0,1:T(8,128)}, bf16[2,512,1024]{2,1,0:T(8,128)(2,1)}, s32[1,4096]{1,0:T(1,128)S(1)}, s32[2]{0:T(128)S(1)}, /*index=5*...) while((s32[]{:T(128)}, f32[4096,256]{0,1:T(8,128)}, ...), condition=%wide.region_30.31_spmd.clone, body=%wide.region_28.30_spmd.clone.sunk | while | flops 21733855232 | bytes 526481792 | solution.py:178
  2712.2 28.2 fusion.140
  2787.1 82.5 %fusion.144 = bf16[8,512,128]{1,2,0:T(8,128)(2,1)} fusion(f32[8,512,4096]{2,1,0:T(8,128)} %fusion.140, f32[512,8,4096]{2,0,1:T(8,128)} %fusion.142, bf16[4096,128]{0,1:T(8,128)(2,1)} %copy-done.20), kind=kOutput, calls=%fused_computation.31.clone.1 | convolution fusion | flops 4378861568 | bytes 136314880 | tf_op jit(solution)/shard_map/while/body/eval_jaxpr/hqk,kd->qhd/dot_general | solution.py:161
  2869.6 92.8 %fusion.143 = f32[4096,128]{0,1:T(8,128)} fusion(bf16[512,8,128]{0,2,1:T(8,128)(2,1)S(1)} %bitcast.184, f32[8,512,4096]{2,1,0:T(8,128)} %fusion.140, f32[512,8,4096]{2,0,1:T(8,128)} %fusion.142), kind=kOutput, calls=%fused_computation.35.clone.1 | convolution fusion | flops 4378861568 | bytes 137363456 | tf_op jit(solution)/shard_map/while/body/eval_jaxpr/hqk,qhd->kd/dot_general | solution.py:164
  3050.3 82.5 %fusion.144 = bf16[8,512,128]{1,2,0:T(8,128)(2,1)} fusion(f32[8,512,4096]{2,1,0:T(8,128)} %fusion.140, f32[512,8,4096]{2,0,1:T(8,128)} %fusion.142, bf16[4096,128]{0,1:T(8,128)(2,1)} %copy-done.20), kind=kOutput, calls=%fused_computation.31.clone.1 | convolution fusion | flops 4378861568 | bytes 136314880 | tf_op jit(solution)/shard_map/while/body/eval_jaxpr/hqk,kd->qhd/dot_general | solution.py:161
  3132.8 92.8 %fusion.143 = f32[4096,128]{0,1:T(8,128)} fusion(bf16[512,8,128]{0,2,1:T(8,128)(2,1)S(1)} %bitcast.184, f32[8,512,4096]{2,1,0:T(8,128)} %fusion.140, f32[512,8,4096]{2,0,1:T(8,128)} %fusion.142), kind=kOutput, calls=%fused_computation.35.clone.1 | convolution fusion | flops 4378861568 | bytes 137363456 | tf_op jit(solution)/shard_map/while/body/eval_jaxpr/hqk,qhd->kd/dot_general | solution.py:164
  3234.1 58.4 %all-gather.23.cloned.1.call-done = bf16[4096,1024]{1,0:T(8,128)(2,1)} async-done(((bf16[1024,1024]{1,0:T(8,128)(2,1)}), bf16[4096,1024]{1,0:T(8,128)(2,1)}) %all-gather.23.cloned.1.call-update) | async-done | bytes 8388624 | tf_op jit(solution)/shard_map/all_gather | solution.py:73
  3361.4 99.9 %all-reduce.17 = bf16[4096,256]{0,1:T(8,128)(2,1)S(1)} all-reduce(f32[4096,256]{0,1:T(8,128)} %get-tuple-element.146), channel_id=1, replica_groups=mesh['dp'=4,'row'=2,'col'=4] {'row','col'}, use_global_device_ids=true, to_apply=%region_32.33 | all-reduce | flops 1048576 | bytes 6291456 | tf_op jit(solution)/shard_map/psum | solution.py:272
  3566.2 627.0 %all-reduce.16.cloned.1.call-done = (f32[512,1024]{1,0:T(8,128)}, f32[512,256]{1,0:T(8,128)}, f32[1024,512]{1,0:T(8,128)}, f32[512,4096]{1,0:T(8,128)}, f32[4096,512]{1,0:T(8,128)}) async-done(((f32[512,1024]{1,0:T(8,128)}, f32[512,256]{1,0:T(8,128)}, f32[1024,512]{1,0:T(8,128)}, f32[512,4096]{1,0:T(8,128)}, f32[4096,512]{1,0:T(8,128)}), (f32[512,1024]{1,0:T(8,128)}, f32[512,256]{1,0:T(8,128)}, ...) | async-done | bytes 21495824 | tf_op jit(solution)/shard_map/psum | solution.py:288
  (273 shorter events, 616.2 us)
Async XLA Ops:
  7.2 543.3 %copy-start = (bf16[1024,512]{1,0:T(8,128)(2,1)S(1)}, bf16[1024,512]{1,0:T(8,128)(2,1)}, u32[]{:S(2)}) copy-start(bf16[1024,512]{1,0:T(8,128)(2,1)} %param.30) | copy-start | bytes 3145732
  7.2 76.0 %all-gather.9.cloned.1.call-start = ((), (), s32[]{:S(2)}) async-start(), calls=%async_computation.8 | async-start | bytes 6291456 | tf_op jit(solution)/shard_map/all_gather | solution.py:49
  26.1 148.3 %all-reduce.14.cloned.1.call-start = ((), (), s32[]{:S(2)}) async-start(), calls=%async_computation.10 | async-start | bytes 8388608 | tf_op jit(solution)/shard_map/psum | solution.py:219
  88.7 213.4 %reduce-scatter.13.cloned.1.call-start = ((), (), s32[]{:S(2)}) async-start(), calls=%async_computation.9 | async-start | bytes 20971520 | tf_op jit(solution)/shard_map/reduce_scatter | solution.py:57
  100.3 201.9 %copy-start.42 = (f32[1024]{0:T(1024)S(1)}, f32[1024]{0:T(1024)}, u32[]{:S(2)}) copy-start(f32[1024]{0:T(1024)} %param.27) | copy-start | bytes 12292
  100.3 450.2 %all-gather.11.cloned.1.call-start = ((), (), s32[]{:S(2)}) async-start(), calls=%async_computation.11 | async-start | bytes 10485760 | tf_op jit(solution)/shard_map/all_gather | solution.py:53
  176.1 130.2 %copy-start.2 = (bf16[4096,128]{1,0:T(8,128)(2,1)}, bf16[4096,128]{1,0:T(8,128)(2,1)S(1)}, u32[]{:S(2)}) copy-start(bf16[4096,128]{1,0:T(8,128)(2,1)S(1)} %fusion.55) | copy-start | bytes 3145732
  492.0 168.0 %reduce-scatter.15.cloned.1.call-start = ((), (), s32[]{:S(2)}) async-start(), calls=%async_computation.12 | async-start | bytes 12582912 | tf_op jit(solution)/shard_map/reduce_scatter | solution.py:63
  560.6 99.5 %copy-start.45 = (f32[512]{0:T(512)S(1)}, f32[512]{0:T(512)}, u32[]{:S(2)}) copy-start(f32[512]{0:T(512)} %param.31) | copy-start | bytes 6148
  560.6 115.6 %copy-start.37 = (f32[512]{0:T(512)S(1)}, f32[512]{0:T(512)}, u32[]{:S(2)}) copy-start(f32[512]{0:T(512)} %param.32) | copy-start | bytes 6148
  560.6 115.6 %copy-start.43 = (f32[512]{0:T(512)S(1)}, f32[512]{0:T(512)}, u32[]{:S(2)}) copy-start(f32[512]{0:T(512)} %param.33) | copy-start | bytes 6148
  560.6 175.6 %all-gather.13.cloned.1.call-start = ((), (), s32[]{:S(2)}) async-start(), calls=%async_computation.13 | async-start | bytes 6291456 | tf_op jit(solution)/shard_map/all_gather | solution.py:49
  679.8 533.4 %reduce-scatter.25.cloned.1.call-start = ((), (), s32[]{:S(2)}) async-start(), calls=%async_computation.23 | async-start | bytes 83886080
  766.1 447.1 %copy-start.36 = (f32[4096]{0:T(1024)S(1)}, f32[4096]{0:T(1024)}, u32[]{:S(2)}) copy-start(f32[4096]{0:T(1024)} %param.35) | copy-start | bytes 49156
  766.2 660.2 %all-gather.15.cloned.1.call-start = ((), (), s32[]{:S(2)}) async-start(), calls=%async_computation.14 | async-start | bytes 41943040 | tf_op jit(solution)/shard_map/all_gather | solution.py:53
  1224.7 326.2 %reduce-scatter.17.cloned.1.call-start = ((), (), s32[]{:S(2)}) async-start(), calls=%async_computation.15 | async-start | bytes 12582912 | tf_op jit(solution)/shard_map/reduce_scatter | solution.py:63
  1451.5 99.5 %copy-start.7 = (bf16[2048,512]{1,0:T(8,128)(2,1)S(1)}, bf16[2048,512]{1,0:T(8,128)(2,1)}, u32[]{:S(2)}) copy-start(bf16[2048,512]{1,0:T(8,128)(2,1)} %param.40) | copy-start | bytes 6291460
  1451.5 99.5 %copy-start.44 = (f32[512]{0:T(512)S(1)}, f32[512]{0:T(512)}, u32[]{:S(2)}) copy-start(f32[512]{0:T(512)} %param.37) | copy-start | bytes 6148
  1451.5 208.5 %all-gather.17.cloned.1.call-start = ((), (), s32[]{:S(2)}) async-start(), calls=%async_computation.16 | async-start | bytes 6291456 | tf_op jit(solution)/shard_map/all_gather | solution.py:69
  1602.2 534.8 %reduce-scatter.27.cloned.1.call-start = ((), (), s32[]{:S(2)}) async-start(), calls=%async_computation.24 | async-start | bytes 83886080
  1690.0 668.8 %all-gather.19.cloned.1.call-start = ((), (), s32[]{:S(2)}) async-start(), calls=%async_computation.17 | async-start | bytes 41943040 | tf_op jit(solution)/shard_map/all_gather | solution.py:73
  2157.1 326.2 %reduce-scatter.19.cloned.1.call-start = ((), (), s32[]{:S(2)}) async-start(), calls=%async_computation.18 | async-start | bytes 12582912 | tf_op jit(solution)/shard_map/reduce_scatter | solution.py:83
  2383.8 99.5 %copy-start.29 = (f32[2048]{0:T(1024)S(1)}, f32[2048]{0:T(1024)}, u32[]{:S(2)}) copy-start(f32[2048]{0:T(1024)} %copy-done.28) | copy-start | bytes 24580
  2383.8 99.5 %copy-start.31 = (f32[2048]{0:T(1024)S(1)}, f32[2048]{0:T(1024)}, u32[]{:S(2)}) copy-start(f32[2048]{0:T(1024)} %copy-done.30) | copy-start | bytes 24580
  2383.8 99.5 %copy-start.38 = (f32[512]{0:T(512)S(1)}, f32[512]{0:T(512)}, u32[]{:S(2)}) copy-start(f32[512]{0:T(512)} %param.32) | copy-start | bytes 6148
  2383.8 181.0 %all-gather.21.cloned.1.call-start = ((), (), s32[]{:S(2)}) async-start(), calls=%async_computation.19 | async-start | bytes 6291456 | tf_op jit(solution)/shard_map/all_gather | solution.py:69
  2508.4 192.0 %reduce-scatter.21.cloned.1.call-start = ((), (), s32[]{:S(2)}) async-start(), calls=%async_computation.20 | async-start | bytes 20971520 | tf_op jit(solution)/shard_map/reduce_scatter | solution.py:77
  2575.2 717.2 %all-gather.23.cloned.1.call-start = ((), (), s32[]{:S(2)}) async-start(), calls=%async_computation.21 | async-start | bytes 10485760 | tf_op jit(solution)/shard_map/all_gather | solution.py:73
  2576.9 128.9 %copy-start.16 = (s32[1,4096]{1,0:T(1,128)S(1)}, s32[1,4096]{1,0:T(1,128)}, u32[]{:S(2)}) copy-start(s32[1,4096]{1,0:T(1,128)} %param.39) | copy-start | bytes 49156
  2576.9 128.9 %copy-start.27 = (f32[2,8,512,1]{2,1,3,0:T(8,128)S(1)}, f32[2,8,512,1]{2,1,3,0:T(8,128)}, u32[]{:S(2)}) copy-start(f32[2,8,512,1]{2,1,3,0:T(8,128)} %get-tuple-element.728) | copy-start | bytes 98308
  3234.0 285.2 %reduce-scatter.23.cloned.1.call-start = ((), (), s32[]{:S(2)}) async-start(), calls=%async_computation.22 | async-start | bytes 12582912 | tf_op jit(solution)/shard_map/reduce_scatter | solution.py:83
  3304.0 889.1 %all-reduce.16.cloned.1.call-start = ((), (), s32[]{:S(2)}) async-start(), calls=%async_computation.25 | async-start | bytes 42991616 | tf_op jit(solution)/shard_map/psum | solution.py:288
  (51 other events, 838.7 us)
Sparse Core Ops, SparseCore 0:
  26.2 57.0 all-gather.8
  88.9 85.4 all-reduce.13
  177.0 125.1 reduce-scatter.12
  492.2 58.2 all-gather.10
  560.7 99.2 reduce-scatter.14
  679.9 56.2 all-gather.12
  766.3 446.8 reduce-scatter.24
  1224.8 201.5 all-gather.14
  1451.6 99.2 reduce-scatter.16
  1602.3 57.6 all-gather.16
  1690.1 446.8 reduce-scatter.26
  2157.2 201.5 all-gather.18
  2384.0 99.3 reduce-scatter.18
  2508.6 56.2 all-gather.20
  2575.3 125.0 reduce-scatter.20
  3234.1 58.2 all-gather.22
  3304.2 116.4 reduce-scatter.22
  3474.9 718.2 all-reduce.15
where the time goes:
time: 4220 us
  waiting for transfers between devices  2890 us (68%)
  matrix products  852 us (20%)
  blocking collectives  232 us (5%)
  other arithmetic  169 us (4%)
  local copies, waits for them, and re-layouts  56.8 us (1%)
    unnamed x20, waiting for transfers between devices  894 us
    psum x1, waiting for transfers between devices, per_device(): lax.psum((grad_query_w, grad_query_bias, grad_keyval_w, grad_value_bias,...  627 us
    all_gather x2, waiting for transfers between devices, cols_gather(): return lax.all_gather(part, 'col', axis=0, tiled=True)  260 us
    all_gather x2, waiting for transfers between devices, back_cols_gather(): return lax.all_gather(part, 'col', axis=0, tiled=True)  260 us
    reduce_scatter x2, waiting for transfers between devices, rows_scatter(): lax.psum_scatter(product_term(whole, weight, False), 'row', scatter_dimen...  198 us
    dot_general x2, matrix products, one_block(): jnp.einsum('hqk,qhd->kd', grad_scores, query_block, preferred_element_typ...  186 us
    dot_general x2, matrix products, one_block(): jnp.einsum('hqk,kd->qhd', grad_scores, key_block, preferred_element_type=...  165 us
    reduce_scatter x1, waiting for transfers between devices, back_cols_scatter(): lax.psum_scatter(product_term(whole, weight, True), 'col', scatter_dimens...  123 us
  transfers between devices with their start and end apart: 18, of which 17 were waited for; matrix products, arithmetic and copies ran while one was open for 3% of the time, Pallas kernels for 0%

commit v1 on v0

v1 whole, which is shorter than its diff:
```python
import functools
import jax, jax.numpy as jnp
from jax import lax
from jax.experimental import pallas as pl
from jax.experimental.pallas import tpu as pltpu
from jax.sharding import PartitionSpec as P

D = 2048
HEAD = 128
SCALE = HEAD**-0.5
SC = SCALE * 1.4426950408889634
NT = (((1,), (1,)), ((), ()))
NN = (((1,), (0,)), ((), ()))
TN = (((0,), (0,)), ((), ()))
f32 = jnp.float32
bf16 = jnp.bfloat16


def stack_heads(ref, heads):
    return jnp.concatenate([ref[:, h * HEAD : (h + 1) * HEAD] for h in range(heads)], axis=0)


def key_rows(ref, slot_ref, block, per_block, chunk):
    parts = [
        ref[pl.ds(pl.multiple_of(slot_ref[block * per_block + s] * chunk, chunk), chunk), :]
        for s in range(per_block)
    ]
    return parts[0] if per_block == 1 else jnp.concatenate(parts, axis=0)


def fwd_kernel(
    full_ref, count_ref, slot_ref, q_ref, k_ref, v_ref, lim_ref, o_ref, lse_ref, acc, top, tot,
    *, heads, tq, chunk, per_block
):
    t = pl.program_id(0)
    bk = chunk * per_block
    q = stack_heads(q_ref, heads)
    acc[...] = jnp.zeros_like(acc)
    top[...] = jnp.full_like(top, -1e30)
    tot[...] = jnp.zeros_like(tot)

    def step(block, masked):
        kk = key_rows(k_ref, slot_ref, block, per_block, chunk)
        vv = key_rows(v_ref, slot_ref, block, per_block, chunk)
        s = lax.dot_general(kk, q, NT, preferred_element_type=f32)
        if masked:
            ids = lax.broadcasted_iota(jnp.int32, (bk, heads * tq), 0) + block * bk
            lim = jnp.concatenate([lim_ref[:1, :]] * heads, axis=1)
            s = jnp.where(ids < lim, s, -1e30)
        before = top[...]
        now = jnp.maximum(before, jnp.max(s, axis=0, keepdims=True))
        p = jnp.exp2(s * SC - now * SC)
        top[...] = now
        a = jnp.exp2((before - now) * SC)
        tot[...] = tot[...] * a + jnp.sum(p, axis=0, keepdims=True)
        acc[...] = acc[...] * a + lax.dot_general(
            vv, p.astype(bf16), TN, preferred_element_type=f32
        )

    lax.fori_loop(0, full_ref[t], lambda b, c: (step(b, False), c)[1], 0)
    lax.fori_loop(full_ref[t], count_ref[t], lambda b, c: (step(b, True), c)[1], 0)
    o = acc[...] * (1.0 / tot[...])
    lse = top[...] * SC + jnp.log2(tot[...])
    for h in range(heads):
        o_ref[:, h * HEAD : (h + 1) * HEAD] = jnp.transpose(o[:, h * tq : (h + 1) * tq]).astype(bf16)
        lse_ref[h : h + 1, :] = lse[:, h * tq : (h + 1) * tq]


def bwd_kernel(
    full_ref, count_ref, slot_ref, q_ref, do_ref, k_ref, v_ref, lim_ref, lse_ref, dl_ref,
    dq_ref, dk_ref, dv_ref, dqa, *, heads, tq, chunk, per_block
):
    t = pl.program_id(0)
    bk = chunk * per_block

    @pl.when((t == 0) & (pl.program_id(1) == 0))
    def _():
        dk_ref[...] = jnp.zeros_like(dk_ref)
        dv_ref[...] = jnp.zeros_like(dv_ref)

    q = stack_heads(q_ref, heads)
    do = stack_heads(do_ref, heads)
    lse = jnp.concatenate([lse_ref[h : h + 1, :] for h in range(heads)], axis=1)
    dl = jnp.concatenate([dl_ref[h : h + 1, :] for h in range(heads)], axis=1)
    dqa[...] = jnp.zeros_like(dqa)

    def step(block, masked):
        kk = key_rows(k_ref, slot_ref, block, per_block, chunk)
        vv = key_rows(v_ref, slot_ref, block, per_block, chunk)
        s = lax.dot_general(kk, q, NT, preferred_element_type=f32)
        p = jnp.exp2(s * SC - lse)
        if masked:
            ids = lax.broadcasted_iota(jnp.int32, (bk, heads * tq), 0) + block * bk
            lim = jnp.concatenate([lim_ref[:1, :]] * heads, axis=1)
            p = jnp.where(ids < lim, p, 0.0)
        dp = lax.dot_general(vv, do, NT, preferred_element_type=f32)
        ds = (p * (dp - dl)).astype(bf16)
        dv = lax.dot_general(p.astype(bf16), do, NN, preferred_element_type=f32)
        dk = lax.dot_general(ds, q, NN, preferred_element_type=f32)
        dqa[...] += lax.dot_general(ds, kk, TN, preferred_element_type=f32)
        for s in range(per_block):
            off = pl.multiple_of(slot_ref[block * per_block + s] * chunk, chunk)
            dk_ref[pl.ds(off, chunk), :] += dk[s * chunk : (s + 1) * chunk]
            dv_ref[pl.ds(off, chunk), :] += dv[s * chunk : (s + 1) * chunk]

    lax.fori_loop(0, full_ref[t], lambda b, c: (step(b, False), c)[1], 0)
    lax.fori_loop(full_ref[t], count_ref[t], lambda b, c: (step(b, True), c)[1], 0)
    dq = (dqa[...] * HEAD**-0.5).astype(bf16)
    for h in range(heads):
        dq_ref[:, h * HEAD : (h + 1) * HEAD] = dq[h * tq : (h + 1) * tq]

    @pl.when((t == pl.num_programs(0) - 1) & (pl.program_id(1) == pl.num_programs(1) - 1))
    def _():
        dk_ref[...] = dk_ref[...] * HEAD**-0.5


def block_counts(limits, tq, bk):
    tiles = limits.reshape(-1, tq)
    return jnp.min(tiles, 1) // bk, (jnp.max(tiles, 1) + bk - 1) // bk


def attend_forward(q, k, v, limits, slots, chunk, tq=128, heads=16, bk=256):
    n, hq = q.shape
    total = hq // HEAD
    per_block = max(1, bk // chunk)
    full, count = block_counts(limits, tq, chunk * per_block)
    rows = k.shape[0]
    grid = pltpu.PrefetchScalarGridSpec(
        num_scalar_prefetch=3,
        grid=(n // tq, total // heads),
        in_specs=[
            pl.BlockSpec((tq, heads * HEAD), lambda t, g, *_: (t, g)),
            pl.BlockSpec((rows, HEAD), lambda t, g, *_: (0, 0)),
            pl.BlockSpec((rows, HEAD), lambda t, g, *_: (0, 0)),
            pl.BlockSpec((8, tq), lambda t, g, *_: (0, t)),
        ],
        out_specs=[
            pl.BlockSpec((tq, heads * HEAD), lambda t, g, *_: (t, g)),
            pl.BlockSpec((heads, tq), lambda t, g, *_: (g, t)),
        ],
        scratch_shapes=[
            pltpu.VMEM((HEAD, heads * tq), f32),
            pltpu.VMEM((1, heads * tq), f32),
            pltpu.VMEM((1, heads * tq), f32),
        ],
    )
    return pl.pallas_call(
        functools.partial(fwd_kernel, heads=heads, tq=tq, chunk=chunk, per_block=per_block),
        grid_spec=grid,
        out_shape=(jax.ShapeDtypeStruct((n, hq), bf16), jax.ShapeDtypeStruct((total, n), f32)),
        name="attend_forward",
        compiler_params=pltpu.CompilerParams(vmem_limit_bytes=48 << 20),
    )(full, count, slots, q, k, v, jnp.broadcast_to(limits[None, :], (8, n)))


def attend_backward(q, do, k, v, limits, slots, lse, delta, chunk, tq=128, heads=16, bk=256):
    n, hq = q.shape
    total = hq // HEAD
    per_block = max(1, bk // chunk)
    full, count = block_counts(limits, tq, chunk * per_block)
    rows = k.shape[0]
    token_block = pl.BlockSpec((tq, heads * HEAD), lambda t, g, *_: (t, g))
    key_block = pl.BlockSpec((rows, HEAD), lambda t, g, *_: (0, 0))
    head_block = pl.BlockSpec((heads, tq), lambda t, g, *_: (g, t))
    grid = pltpu.PrefetchScalarGridSpec(
        num_scalar_prefetch=3,
        grid=(n // tq, total // heads),
        in_specs=[
            token_block, token_block, key_block, key_block,
            pl.BlockSpec((8, tq), lambda t, g, *_: (0, t)),
            head_block, head_block,
        ],
        out_specs=[token_block, key_block, key_block],
        scratch_shapes=[pltpu.VMEM((heads * tq, HEAD), f32)],
    )
    return pl.pallas_call(
        functools.partial(bwd_kernel, heads=heads, tq=tq, chunk=chunk, per_block=per_block),
        grid_spec=grid,
        out_shape=(
            jax.ShapeDtypeStruct((n, hq), bf16),
            jax.ShapeDtypeStruct((rows, HEAD), f32),
            jax.ShapeDtypeStruct((rows, HEAD), f32),
        ),
        name="attend_backward",
        compiler_params=pltpu.CompilerParams(vmem_limit_bytes=48 << 20),
    )(full, count, slots, q, do, k, v, jnp.broadcast_to(limits[None, :], (8, n)), lse, delta)


epsilon = 1e-05
gelu_coeff = 0.7978845608028654


def send(x, axis, mask):
    size = lax.axis_size(axis)
    return lax.ppermute(x, axis, [(i, i ^ mask) for i in range(size)])


def send_pair(x, i, j):
    count_row, count_col = lax.axis_size("row"), lax.axis_size("col")
    pairs = [
        (a * count_col + b, (a ^ i) * count_col + (b ^ j))
        for a in range(count_row)
        for b in range(count_col)
    ]
    return lax.ppermute(x, ("row", "col"), pairs)


def masks_of(axis):
    size = lax.axis_size(axis)
    return [1 << k for k in reversed(range(size.bit_length() - 1))]


def other_key(key, axis, mask):
    return (key[0] ^ mask, key[1]) if axis == "row" else (key[0], key[1] ^ mask)


def gather_pieces(x, steps):
    pieces = {(0, 0): x}
    for axis, mask in steps:
        for key in list(pieces):
            pieces[other_key(key, axis, mask)] = send(pieces[key], axis, mask)
    return pieces


def reduce_pieces(pieces, steps, wire):
    pieces = dict(pieces)
    for axis, mask in steps:
        at = 0 if axis == "row" else 1
        for key in [key for key in pieces if key[at] & mask]:
            arrived = send(pieces.pop(key).astype(wire), axis, mask)
            home = other_key(key, axis, mask)
            pieces[home] = pieces[home].astype(f32) + arrived.astype(f32)
    return pieces[(0, 0)]


def join(pieces, rows, cols):
    strips = [
        jnp.concatenate([pieces[(i, j)] for i in range(rows)], 1) if rows > 1 else pieces[(0, j)]
        for j in range(cols)
    ]
    return jnp.concatenate(strips, 0) if cols > 1 else strips[0]


def everywhere(x, axes):
    for axis in axes:
        for mask in masks_of(axis):
            x = x + send(x, axis, mask)
    return x


def gelu_tanh(values):
    return (
        0.5 * values * (1.0 + jnp.tanh(gelu_coeff * (values + 0.044715 * values * values * values)))
    )


def gelu_slope(values):
    square = values * values
    curve = jnp.tanh(gelu_coeff * values * (1.0 + 0.044715 * square))
    return 0.5 * (1.0 + curve) + 0.5 * values * (1.0 - curve * curve) * gelu_coeff * (
        1.0 + 3.0 * 0.044715 * square
    )


def norm_forward(values, gain, shift):
    means = jnp.mean(values, 1, keepdims=True)
    squares = jnp.mean(values * values, 1, keepdims=True)
    inverse = lax.rsqrt(squares - means * means + epsilon)
    normal = (values - means) * inverse
    return (normal, inverse, (normal * gain + shift).astype(bf16))


def norm_backward(grad, normal, inverse, gain):
    scaled = grad * gain
    return inverse * (
        scaled
        - jnp.mean(scaled, 1, keepdims=True)
        - normal * jnp.mean(scaled * normal, 1, keepdims=True)
    )


def dot_nn(a, b):
    return lax.dot_general(a, b, NN, preferred_element_type=f32)


def dot_nt(a, b):
    return lax.dot_general(a, b, NT, preferred_element_type=f32)


def dot_tn(a, b):
    return lax.dot_general(a, b, TN, preferred_element_type=f32)


def chunk_rows(chunk, i, j):
    count_row, count_col = lax.axis_size("row"), lax.axis_size("col")
    r, c = lax.axis_index("row"), lax.axis_index("col") ^ j
    if count_row == 2:
        owner = (r ^ i) * count_col + c
        return jnp.where(r == 0, owner, 2 * count_col - 1 - owner) * chunk
    return (c if i == 0 else 2 * count_col - 1 - c) * chunk


def chunk_send(x, i, j):
    if lax.axis_size("row") == 2:
        return send_pair(x, i, j) if i or j else x
    return send(x, "col", j) if j else x


def to_tokens(block, chunk):
    count_col = lax.axis_size("col")
    return [
        [
            chunk_send(lax.dynamic_slice_in_dim(block, chunk_rows(chunk, i, j), chunk, 0), i, j)
            for j in range(count_col)
        ]
        for i in range(2)
    ]


def assemble(pieces):
    return jnp.concatenate([jnp.concatenate(strip, 1) for strip in pieces], 0)


def from_tokens(tokens, chunk, width, rows):
    out = jnp.zeros((rows, width), f32)
    low = tokens.astype(bf16)
    for i in range(2):
        for j in range(lax.axis_size("col")):
            part = low[i * chunk : (i + 1) * chunk, j * width : (j + 1) * width]
            out = lax.dynamic_update_slice_in_dim(
                out, chunk_send(part, i, j).astype(f32), chunk_rows(chunk, i, j), 0
            )
    return out


def token_starts(chunk):
    count_row, count_col = lax.axis_size("row"), lax.axis_size("col")
    r, c = lax.axis_index("row"), lax.axis_index("col")
    if count_row == 2:
        own = r * count_col + c
        low, high = own * chunk, (4 * count_col - 1 - own) * chunk
        return [jnp.where(r == 0, low, high), jnp.where(r == 0, high, low)]
    return [(r * 2 * count_col + c) * chunk, (r * 2 * count_col + 2 * count_col - 1 - c) * chunk]


def key_slots():
    count_row, count_col = lax.axis_size("row"), lax.axis_size("col")
    r, c = lax.axis_index("row"), lax.axis_index("col")
    group = jnp.arange(2 * count_row * count_col, dtype=jnp.int32)
    half = group // (2 * count_col)
    if count_row == 2:
        owner = jnp.where(half == 0, group, 4 * count_col - 1 - group)
        owner_row, owner_col = owner // count_col, owner % count_col
        which = owner_row ^ half
    else:
        local = group % (2 * count_col)
        owner_row = half
        which = (local >= count_col).astype(jnp.int32)
        owner_col = jnp.where(which == 0, local, 2 * count_col - 1 - local)
    return ((owner_row ^ r) * count_col + (owner_col ^ c)) * 2 + which


def over_dp(total, wire):
    size = lax.axis_size("dp")
    if size != 4:
        return everywhere(total, ["dp"])
    z = lax.axis_index("dp")
    half = total.shape[0] // 2
    total = total + lax.ppermute(total.astype(wire), "dp", [(0, 1), (3, 2)]).astype(f32)
    own_at = jnp.where(z < 2, 0, half)
    far_at = half - own_at
    middle = [(1, 2), (2, 1)]
    outward = [(1, 0), (2, 3)]
    far = lax.dynamic_slice_in_dim(total, far_at, half, 0).astype(wire)
    own = lax.dynamic_slice_in_dim(total, own_at, half, 0)
    own = (own + lax.ppermute(far, "dp", middle).astype(f32)).astype(wire)
    far = lax.ppermute(own, "dp", middle)
    own_out = lax.ppermute(own, "dp", outward)
    far_out = lax.ppermute(far, "dp", outward)
    inside = (z == 1) | (z == 2)
    own = jnp.where(inside, own, own_out).astype(f32)
    far = jnp.where(inside, far, far_out).astype(f32)
    first = jnp.where(z < 2, own, far)
    second = jnp.where(z < 2, far, own)
    return jnp.concatenate([first, second], 0)


def per_device(
    layer_input,
    norm1_gain,
    norm1_shift,
    w_query,
    b_query,
    w_keyval,
    b_value,
    w_attn_out,
    b_attn_out,
    norm2_gain,
    norm2_shift,
    w_fc_in,
    b_fc_in,
    w_fc_out,
    b_fc_out,
    valid_mask,
    block_ids,
    teacher,
    out_cotangent,
):
    count_row = lax.axis_size("row")
    count_col = lax.axis_size("col")
    count_dp = lax.axis_size("dp")
    rows_a, width = layer_input.shape
    wide = w_query.shape[1]
    chunk = rows_a // (2 * count_col)
    col_in = [("col", m) for m in masks_of("col")]
    row_in = [("row", m) for m in masks_of("row")]
    col_out, row_out = col_in[::-1], row_in[::-1]
    near, across = col_in[-1:], col_in[:-1]
    all_in = across + row_in + near
    all_out = near + row_out + across[::-1]
    valid_flat = valid_mask.reshape(-1)
    block_flat = block_ids.reshape(-1)

    x_pieces = to_tokens(layer_input, chunk)
    vectors = gather_pieces(
        jnp.stack([norm1_gain, norm1_shift, b_attn_out, norm2_gain, norm2_shift, b_fc_out]), col_in
    )
    vectors = jnp.concatenate([vectors[(0, j)] for j in range(count_col)], 1)
    gain1, shift1, bias_o, gain2, shift2, bias_out = [vectors[k : k + 1] for k in range(6)]
    bias_q = gather_pieces(b_query[None, :], row_in)
    bias_q = jnp.concatenate([bias_q[(i, 0)] for i in range(count_row)], 1)
    keyval_w = join(gather_pieces(w_keyval, col_in), 1, count_col)
    query_w = join(gather_pieces(w_query, all_in), count_row, count_col)
    attn_pieces = gather_pieces(w_attn_out, all_in)
    attn_w = jnp.concatenate(
        [
            jnp.concatenate([attn_pieces[(i, j)] for j in range(count_col)], 1)
            for i in range(count_row)
        ],
        0,
    )
    fc_in_pieces = gather_pieces(w_fc_in, col_in)
    fc_in_w = jnp.concatenate([fc_in_pieces[(0, j)] for j in range(count_col)], 0)
    fc_out_pieces = gather_pieces(w_fc_out, col_in)
    fc_out_w = jnp.concatenate([fc_out_pieces[(0, j)] for j in range(count_col)], 1)
    late_pieces = [
        [
            chunk_send(
                jnp.concatenate(
                    [
                        lax.dynamic_slice_in_dim(block, chunk_rows(chunk, i, j), chunk, 0)
                        for block in (teacher, out_cotangent)
                    ],
                    0,
                ),
                i,
                j,
            )
            for j in range(count_col)
        ]
        for i in range(2)
    ]
    target = assemble([[piece[:chunk] for piece in strip] for strip in late_pieces])
    cotangent = assemble([[piece[chunk:] for piece in strip] for strip in late_pieces])

    starts = token_starts(chunk)
    block_own = jnp.concatenate(
        [lax.dynamic_slice_in_dim(block_flat, start, chunk, 0) for start in starts]
    )
    valid_own = jnp.concatenate(
        [lax.dynamic_slice_in_dim(valid_flat, start, chunk, 0) for start in starts]
    ).astype(f32)[:, None]
    valid_length = jnp.sum(valid_flat)
    reach = jnp.sum((block_flat[None, :] <= block_own[:, None]).astype(jnp.int32), 1)
    limits = jnp.minimum(reach, valid_length)
    slots = key_slots()
    valid_count = everywhere(jnp.full((8, 128), valid_length.astype(f32)), ["dp"])[0, 0]

    residual = assemble(x_pieces).astype(f32)
    normal1, inverse1, normed1 = norm_forward(residual, gain1, shift1)
    keyval = dot_nn(normed1, keyval_w)
    keyval = jnp.concatenate(
        [keyval[:, :HEAD].astype(bf16), (keyval[:, HEAD:] + b_value).astype(bf16)], 1
    )
    keyval_pieces = gather_pieces(keyval, all_in)
    keyval_all = jnp.concatenate(
        [keyval_pieces[(i, j)] for i in range(count_row) for j in range(count_col)], 0
    )
    keys, values = keyval_all[:, :HEAD], keyval_all[:, HEAD:]
    queries = (dot_nn(normed1, query_w) + bias_q).astype(bf16)
    attended, log_totals = attend_forward(queries, keys, values, limits, slots, chunk)
    middle = residual + (dot_nn(attended, attn_w) + bias_o)
    normal2, inverse2, normed2 = norm_forward(middle, gain2, shift2)
    own = normed2.shape[0]

    def row_gather(x):
        pieces = gather_pieces(x, row_in)
        return jnp.concatenate([pieces[(i, 0)] for i in range(count_row)], 0)

    def row_sum(x):
        pieces = {(i, 0): x[i * own : (i + 1) * own] for i in range(count_row)}
        return reduce_pieces(pieces, row_out, bf16)

    normed2_all = row_gather(normed2)
    pre_act = dot_nn(normed2_all, fc_in_w) + b_fc_in
    act = gelu_tanh(pre_act).astype(bf16)
    layer_output = middle + (row_sum(dot_nn(act, fc_out_w)) + bias_out)
    errors = layer_output - target.astype(f32)
    loss_part = jnp.sum(valid_own * errors * errors)
    ratio = rows_a * count_row * count_dp / valid_count
    grad_out = cotangent.astype(f32) + ratio * valid_own * errors
    output_block = from_tokens(layer_output, chunk, width, rows_a)
    grad_mlp = grad_out.astype(bf16)
    grad_fc_out_bias = jnp.sum(grad_mlp, 0, dtype=f32)
    grad_mlp_all = row_gather(grad_mlp)

    parts = 2
    hidden = act.shape[1] // parts
    fc_out_grads = []
    for f in range(parts):
        pieces = {
            (0, j): dot_tn(
                act[:, f * hidden : (f + 1) * hidden],
                grad_mlp_all[:, j * width : (j + 1) * width],
            )
            for j in range(count_col)
        }
        fc_out_grads.append(over_dp(reduce_pieces(pieces, col_out, bf16), bf16))
    grad_fc_out = jnp.concatenate(fc_out_grads, 0)

    grad_pre = (dot_nt(grad_mlp_all, fc_out_w) * gelu_slope(pre_act)).astype(bf16)
    grad_fc_in_bias = jnp.sum(grad_pre, 0, dtype=f32)
    grad_normed2 = row_sum(dot_nt(grad_pre, fc_in_w))
    fc_in_grads = []
    for f in range(parts):
        pieces = {
            (0, j): dot_tn(
                normed2_all[:, j * width : (j + 1) * width],
                grad_pre[:, f * hidden : (f + 1) * hidden],
            )
            for j in range(count_col)
        }
        fc_in_grads.append(over_dp(reduce_pieces(pieces, col_out, bf16), bf16))
    grad_fc_in = jnp.concatenate(fc_in_grads, 1)

    gain2_part = jnp.sum(grad_normed2 * normal2, 0)
    shift2_part = jnp.sum(grad_normed2, 0)
    grad_middle = grad_out + norm_backward(grad_normed2, normal2, inverse2, gain2)
    grad_attn = grad_middle.astype(bf16)
    grad_attn_bias = jnp.sum(grad_attn, 0, dtype=f32)
    pieces = {
        (i, j): dot_tn(
            attended[:, i * wide : (i + 1) * wide], grad_attn[:, j * width : (j + 1) * width]
        )
        for i in range(count_row)
        for j in range(count_col)
    }
    grad_attn_out = over_dp(reduce_pieces(pieces, all_out, bf16), bf16)
    grad_attended = dot_nt(grad_attn, attn_w).astype(bf16)

    heads = queries.shape[1] // HEAD
    delta = jnp.sum(
        (attended.astype(f32) * grad_attended.astype(f32)).reshape(own, heads, HEAD), -1
    ).T
    grad_queries, grad_keys, grad_values = attend_backward(
        queries, grad_attended, keys, values, limits, slots, log_totals, delta, chunk
    )
    grad_keyval = jnp.concatenate([grad_keys, grad_values], 1)
    pieces = {
        (i, j): grad_keyval[(i * count_col + j) * own : (i * count_col + j + 1) * own]
        for i in range(count_row)
        for j in range(count_col)
    }
    grad_keyval_low = reduce_pieces(pieces, all_out, f32).astype(bf16)
    grad_value_bias = jnp.sum(grad_keyval_low[:, HEAD:], 0, dtype=f32)
    grad_query_bias = jnp.sum(grad_queries, 0, dtype=f32)
    pieces = {
        (i, j): dot_tn(
            normed1[:, j * width : (j + 1) * width], grad_queries[:, i * wide : (i + 1) * wide]
        )
        for i in range(count_row)
        for j in range(count_col)
    }
    grad_query_w = over_dp(reduce_pieces(pieces, all_out, bf16), bf16)
    pieces = {
        (0, j): dot_tn(normed1[:, j * width : (j + 1) * width], grad_keyval_low)
        for j in range(count_col)
    }
    grad_keyval_w = everywhere(reduce_pieces(pieces, col_out, f32), ["row", "dp"])
    grad_normed1 = dot_nt(grad_queries, query_w) + dot_nt(grad_keyval_low, keyval_w)
    gain1_part = jnp.sum(grad_normed1 * normal1, 0)
    shift1_part = jnp.sum(grad_normed1, 0)
    input_grad = grad_middle + norm_backward(grad_normed1, normal1, inverse1, gain1)
    input_block = from_tokens(input_grad, chunk, width, rows_a)

    def feature_sums(parts_list):
        stacked = jnp.stack(parts_list)
        pieces = {(0, j): stacked[:, j * width : (j + 1) * width] for j in range(count_col)}
        return everywhere(reduce_pieces(pieces, col_out, f32), ["row", "dp"])

    early = feature_sums([gain2_part, shift2_part, grad_fc_out_bias, grad_attn_bias])
    late = feature_sums([gain1_part, shift1_part])
    loss_sum = everywhere(jnp.full((8, 128), loss_part), ["row", "col", "dp"])[0, 0]
    fc_in_bias_sum = everywhere(grad_fc_in_bias[None, :], ["col", "dp"])[0]
    pieces = {(i, 0): grad_query_bias[None, i * wide : (i + 1) * wide] for i in range(count_row)}
    query_bias_sum = everywhere(reduce_pieces(pieces, row_out, f32), ["col", "dp"])[0]
    value_bias_sum = everywhere(grad_value_bias[None, :], ["row", "col", "dp"])[0]
    return (
        output_block,
        loss_sum / (valid_count * D),
        input_block,
        late[0],
        late[1],
        grad_query_w,
        query_bias_sum,
        grad_keyval_w,
        value_bias_sum,
        grad_attn_out,
        early[3],
        early[0],
        early[1],
        grad_fc_in,
        fc_in_bias_sum,
        grad_fc_out,
        early[2],
    )


def solution(mesh):
    placed = (
        P(("dp", "row"), "col"),
        P("col"),
        P("col"),
        P("col", "row"),
        P("row"),
        P("col", None),
        P(),
        P("row", "col"),
        P("col"),
        P("col"),
        P("col"),
        P("col", "row"),
        P("row"),
        P("row", "col"),
        P("col"),
        P("dp", None),
        P("dp", None),
        P(("dp", "row"), "col"),
        P(("dp", "row"), "col"),
    )
    return jax.shard_map(
        per_device,
        mesh=mesh,
        in_specs=placed,
        out_specs=(
            P(("dp", "row"), "col"),
            P(),
            P(("dp", "row"), "col"),
            P("col"),
            P("col"),
            P("col", "row"),
            P("row"),
            P("col", None),
            P(),
            P("row", "col"),
            P("col"),
            P("col"),
            P("col"),
            P("col", "row"),
            P("row"),
            P("row", "col"),
            P("col"),
        ),
        check_vma=False,
    )
```

time: 4220 us -> 1760 us (0.42)
  waiting for transfers between devices: 2890 us -> 987 us
  matrix products: 852 us -> 287 us
  blocking collectives: 232 us -> 0 us
  starting transfers between devices: 0.75 us -> 156 us
  Pallas kernels: 0 us -> 98.9 us
    ppermute x0 -> x168, waiting for transfers between devices: none -> 987 us  [the longest x110 440 us: send(): return lax.ppermute(x, axis, [(i, i ^ mask) for i in range(size)])]
    unnamed x20 -> x0, waiting for transfers between devices: 894 us -> none
    all_gather x8 -> x0, waiting for transfers between devices: 748 us -> none  [the longest x2 260 us: cols_gather(): return lax.all_gather(part, 'col', axis=0, tiled=True)]
    psum x2 -> x0, waiting for transfers between devices: 701 us -> none  [the longest x1 627 us: per_device(): lax.psum((grad_query_w, grad_query_bias, grad_keyval_w, grad_value_bias,...]
    dot_general x29 -> x46, matrix products: 852 us -> 287 us  [the longest x36 127 us: dot_tn(): return lax.dot_general(a, b, TN, preferred_element_type=f32)]
    reduce_scatter x6 -> x0, waiting for transfers between devices: 542 us -> none  [the longest x2 198 us: rows_scatter(): lax.psum_scatter(product_term(whole, weight, False), 'row', scatter_dimen...]
    psum x8 -> x0, blocking collectives: 232 us -> none  [the longest x1 99.9 us: per_device(): grad_keyval_low = lax.psum(grad_keyval, ('row', 'col')).astype(jnp.bfloat16)]
    ppermute x0 -> x168, starting transfers between devices: none -> 156 us  [the longest x110 85.9 us: send(): return lax.ppermute(x, axis, [(i, i ^ mask) for i in range(size)])]
  transfers between devices with their start and end apart: 18 -> 168, of which waited for: 17 -> 67; matrix products, arithmetic and copies ran while one was open for 3% -> 25% of each run, Pallas kernels for 0% -> 6%
where the time goes in v1:
time: 1760 us; the launch traced here: 1750 us
  waiting for transfers between devices  987 us (56%)
  matrix products  287 us (16%)
  starting transfers between devices  156 us (9%)
  other arithmetic  151 us (9%)
  Pallas kernels  98.9 us (6%)
  local copies, waits for them, and re-layouts  65.9 us (4%)
    ppermute x110, waiting for transfers between devices, send(): return lax.ppermute(x, axis, [(i, i ^ mask) for i in range(size)])  440 us
    ppermute x28, waiting for transfers between devices, send_pair(): return lax.ppermute(x, ('row', 'col'), pairs)  203 us
    dot_general x36, matrix products, dot_tn(): return lax.dot_general(a, b, TN, preferred_element_type=f32)  127 us
    ppermute x6, waiting for transfers between devices, over_dp(): far_out = lax.ppermute(far, 'dp', outward)  125 us
    ppermute x6, waiting for transfers between devices, over_dp(): own_out = lax.ppermute(own, 'dp', outward)  119 us
    ppermute x6, waiting for transfers between devices, over_dp(): lax.ppermute(total.astype(wire), 'dp', [(0, 1), (3, 2)]).astype(f32)  101 us
    dot_general x5, matrix products, dot_nt(): return lax.dot_general(a, b, NT, preferred_element_type=f32)  87.9 us
    ppermute x110, starting transfers between devices, send(): return lax.ppermute(x, axis, [(i, i ^ mask) for i in range(size)])  85.9 us
  transfers between devices with their start and end apart: 168, of which 67 were waited for; matrix products, arithmetic and copies ran while one was open for 25% of the time, Pallas kernels for 6%

profile of v1, /device:TPU:0, one launch (start us, length us, event | category | flops | bytes accessed | tf_op | source)
XLA Modules:
  0.0 1753.5 jit_solution(15549097361634830480)
XLA Ops:
  78.5 23.9 %collective-permute-done.26 = bf16[512,256]{1,0:T(8,128)(2,1)S(1)} collective-permute-done((bf16[512,256]{1,0:T(8,128)(2,1)S(1)}, bf16[512,256]{1,0:T(8,128)(2,1)S(1)}, u32[]{:S(2)}, u32[]{:S(2)}) %collective-permute-start.26) | collective-permute-done | bytes 262176 | tf_op jit(solution)/shard_map/ppermute | solution.py:195
  130.5 20.5 %collective-permute-done.14 = bf16[512,1024]{1,0:T(8,128)(2,1)S(1)} collective-permute-done((bf16[512,1024]{1,0:T(8,128)(2,1)S(1)}, bf16[512,1024]{1,0:T(8,128)(2,1)S(1)}, u32[]{:S(2)}, u32[]{:S(2)}) %collective-permute-start.14) | collective-permute-done | bytes 1048608 | tf_op jit(solution)/shard_map/ppermute | solution.py:195
  154.2 17.7 %collective-permute-done.33 = bf16[1024,512]{1,0:T(8,128)(2,1)} collective-permute-done((bf16[1024,512]{1,0:T(8,128)(2,1)S(1)}, bf16[1024,512]{1,0:T(8,128)(2,1)}, u32[]{:S(2)}, u32[]{:S(2)}) %collective-permute-start.33) | collective-permute-done | bytes 1048608 | tf_op jit(solution)/shard_map/ppermute | solution.py:195
  189.5 17.3 maximum_maximum_fusion.1
  206.9 39.7 %attend_forward.1 = (bf16[512,2048]{1,0:T(8,128)(2,1)S(1)}, f32[16,512]{1,0:T(8,128)S(1)}) custom-call(s32[4]{0:T(128)S(1)} %get-tuple-element.171.full_ref, s32[4]{0:T(128)S(1)} %get-tuple-element.170.count_ref, s32[16]{0:T(128)S(1)} %xor_add_fusion.slot_ref, bf16[512,2048]{1,0:T(8,128)(2,1)} %add_convert_fusion.5.q_ref, ...), custom_call_target="tpu_custom_call" | custom-call | tf_op jit(solution)/shard_map/attend_forward/pallas_call | solution.py:147
  250.2 84.0 %collective-permute-done.40 = bf16[4096,512]{1,0:T(8,128)(2,1)} collective-permute-done((bf16[4096,512]{1,0:T(8,128)(2,1)}, bf16[4096,512]{1,0:T(8,128)(2,1)}, u32[]{:S(2)}, u32[]{:S(2)}) %collective-permute-start.40) | collective-permute-done | bytes 4194336 | tf_op jit(solution)/shard_map/ppermute | solution.py:195
  371.5 30.3 %collective-permute-done.35 = bf16[512,2048]{1,0:T(8,128)(2,1)S(1)} collective-permute-done((bf16[512,2048]{1,0:T(8,128)(2,1)S(1)}, bf16[512,2048]{1,0:T(8,128)(2,1)S(1)}, u32[]{:S(2)}, u32[]{:S(2)}) %collective-permute-start.35) | collective-permute-done | bytes 2097184 | tf_op jit(solution)/shard_map/ppermute | solution.py:195
  401.8 27.0 %fusion.4 = (bf16[1024,4096]{1,0:T(8,128)(2,1)}, f32[1024,4096]{1,0:T(8,128)}) fusion(f32[4096]{0:T(1024)S(1)} %copy-done.116, bf16[2048,4096]{1,0:T(8,128)(2,1)} %constant_dynamic-update-slice_fusion.12, bf16[512,2048]{1,0:T(8,128)(2,1)S(1)} %collective-permute-done.35, bf16[512,2048]{1,0:T(8,128)(2,1)S(1)} %add_convert_fusion.4), kind=kOutput, calls=%fused_computation.5 | convolution fusion | flops 17230200832 | bytes 46153728 | tf_op jit(solution)/shard_map/dot_general | solution.py:283
  428.8 21.6 %fusion.167 = f32[1024,2048]{1,0:T(8,128)S(1)} fusion(bf16[1024,4096]{1,0:T(8,128)(2,1)} %get-tuple-element.153, bf16[4096,2048]{1,0:T(8,128)(2,1)} %constant_dynamic-update-slice_fusion.16), kind=kOutput, calls=%fused_computation.408 | convolution fusion | flops 17179869184 | bytes 33554432 | tf_op jit(solution)/shard_map/dot_general | solution.py:283
  461.6 49.0 %collective-permute-done.53 = bf16[512,512]{1,0:T(8,128)(2,1)S(1)} collective-permute-done((bf16[512,512]{1,0:T(8,128)(2,1)S(1)}, bf16[512,512]{1,0:T(8,128)(2,1)S(1)}, u32[]{:S(2)}, u32[]{:S(2)}) %collective-permute-start.53) | collective-permute-done | bytes 524320 | tf_op jit(solution)/shard_map/ppermute | solution.py:205
  543.4 17.9 %convert_reduce_fusion.4 = (f32[2048]{0:T(1024)}, bf16[512,2048]{1,0:T(8,128)(2,1)}, f32[512,2048]{1,0:T(8,128)}, f32[512,2048]{1,0:T(8,128)S(1)}) fusion(bf16[256,512]{1,0:T(8,128)(2,1)S(1)} %get-tuple-element.123, bf16[256,512]{1,0:T(8,128)(2,1)S(1)} %get-tuple-element.121, bf16[256,512]{1,0:T(8,128)(2,1)S(1)} %get-tuple-element.119, ...), kind=kLoop, calls=%fused_computation.71 | loop fusion | flops 44038144 | bytes 25184256 | tf_op jit(solution)/shard_map/reduce_sum | solution.py:514
  607.1 24.7 %collective-permute-done.46 = bf16[256,512]{1,0:T(8,128)(2,1)S(1)} collective-permute-done((bf16[256,512]{1,0:T(8,128)(2,1)S(1)}, bf16[256,512]{1,0:T(8,128)(2,1)S(1)}, u32[]{:S(2)}, u32[]{:S(2)}) %collective-permute-start.46) | collective-permute-done | bytes 262176 | tf_op jit(solution)/shard_map/ppermute | solution.py:205
  662.8 35.7 %convert_reduce_fusion = (f32[4096]{0:T(1024)S(1)}, bf16[1024,4096]{1,0:T(8,128)(2,1)}) fusion(f32[1024,4096]{1,0:T(8,128)} %get-tuple-element.154, f32[4096]{0:T(1024)S(1)} %copy-done.116, bf16[4096,2048]{1,0:T(8,128)(2,1)} %constant_dynamic-update-slice_fusion.16, bf16[512,2048]{1,0:T(8,128)(2,1)} %collective-permute-done.64, ...), kind=kOutput, calls=%fused_computation.6 | convolution fusion | flops 17276334080 | bytes 46170112 | tf_op jit(solution)/shard_map/dot_general | solution.py:287
  699.1 21.5 %fusion.168 = f32[1024,2048]{1,0:T(8,128)S(1)} fusion(bf16[1024,4096]{1,0:T(8,128)(2,1)} %get-tuple-element.165, bf16[2048,4096]{1,0:T(8,128)(2,1)} %constant_dynamic-update-slice_fusion.12), kind=kOutput, calls=%fused_computation.409 | convolution fusion | flops 17179869184 | bytes 33554432 | tf_op jit(solution)/shard_map/dot_general | solution.py:287
  753.5 19.4 %collective-permute-done.65 = bf16[512,2048]{1,0:T(8,128)(2,1)S(1)} collective-permute-done((bf16[512,2048]{1,0:T(8,128)(2,1)S(1)}, bf16[512,2048]{1,0:T(8,128)(2,1)S(1)}, u32[]{:S(2)}, u32[]{:S(2)}) %collective-permute-start.65) | collective-permute-done | bytes 2097184 | tf_op jit(solution)/shard_map/ppermute | solution.py:195
  801.4 59.2 %attend_backward.1 = (bf16[512,2048]{1,0:T(8,128)(2,1)S(1)}, f32[4096,128]{1,0:T(8,128)}, f32[4096,128]{1,0:T(8,128)}) custom-call(s32[4]{0:T(128)S(1)} %copy-done.11, s32[4]{0:T(128)S(1)} %copy-done.9, s32[16]{0:T(128)S(1)} %copy-done.13, bf16[512,2048]{1,0:T(8,128)(2,1)} %add_convert_fusion.5.q_ref, bf16[512,2048]{1,0:T(8,128)(2,1)} %copy-done.41, ...), custom_call_target="tpu_custom_call" | custom-call | tf_op jit(solution)/shard_map/attend_backward/pallas_call | solution.py:176
  951.7 19.7 %fusion.19 = (f32[2048]{0:T(1024)S(1)}, f32[512]{0:T(512)S(1)}, f32[512]{0:T(512)S(1)}, f32[2048]{0:T(1024)S(1)}, f32[512,2048]{1,0:T(8,128)}) fusion(bf16[512,2048]{1,0:T(8,128)(2,1)} %copy-done.25, f32[512]{0:T(512)S(1)} %copy-done.98, f32[512]{0:T(512)S(1)} %copy-done.96, f32[2048]{0:T(1024)S(1)} %bitcast.79, f32[512,2048]{1,0:T(8,128)} %fusion.169, ...), kind=kOutput, calls=%fused_computation.50 | convolution fusion | flops 4373605376 | bytes 21004288 | tf_op jit(solution)/shard_map/dot_general | solution.py:287
  998.3 47.1 %collective-permute-done.74 = bf16[256,512]{1,0:T(8,128)(2,1)S(1)} collective-permute-done((bf16[256,512]{1,0:T(8,128)(2,1)S(1)}, bf16[256,512]{1,0:T(8,128)(2,1)S(1)}, u32[]{:S(2)}, u32[]{:S(2)}) %collective-permute-start.74) | collective-permute-done | bytes 262176 | tf_op jit(solution)/shard_map/ppermute | solution.py:205
  1081.3 25.7 %collective-permute-done.162 = bf16[2048,512]{1,0:T(8,128)(2,1)S(1)} collective-permute-done((bf16[2048,512]{1,0:T(8,128)(2,1)}, bf16[2048,512]{1,0:T(8,128)(2,1)S(1)}, u32[]{:S(2)}, u32[]{:S(2)}) %collective-permute-start.162) | collective-permute-done | bytes 2097184 | tf_op jit(solution)/shard_map/ppermute | solution.py:195
  1116.6 35.4 %collective-permute-done.134 = bf16[512,2048]{1,0:T(8,128)(2,1)S(1)} collective-permute-done((bf16[512,2048]{1,0:T(8,128)(2,1)S(1)}, bf16[512,2048]{1,0:T(8,128)(2,1)S(1)}, u32[]{:S(2)}, u32[]{:S(2)}) %collective-permute-start.134) | collective-permute-done | bytes 2097184 | tf_op jit(solution)/shard_map/ppermute | solution.py:195
  1154.0 51.6 %collective-permute-done.105 = f32[512,256]{1,0:T(8,128)} collective-permute-done((f32[512,256]{1,0:T(8,128)S(1)}, f32[512,256]{1,0:T(8,128)}, u32[]{:S(2)}, u32[]{:S(2)}) %collective-permute-start.105) | collective-permute-done | bytes 524320 | tf_op jit(solution)/shard_map/ppermute | solution.py:195
  1287.3 30.3 %collective-permute-done.107 = f32[512,256]{1,0:T(8,128)S(1)} collective-permute-done((f32[512,256]{1,0:T(8,128)S(1)}, f32[512,256]{1,0:T(8,128)S(1)}, u32[]{:S(2)}, u32[]{:S(2)}) %collective-permute-start.107) | collective-permute-done | bytes 524320 | tf_op jit(solution)/shard_map/ppermute | solution.py:195
  1338.1 24.6 %collective-permute-done.135 = bf16[512,2048]{1,0:T(8,128)(2,1)} collective-permute-done((bf16[512,2048]{1,0:T(8,128)(2,1)}, bf16[512,2048]{1,0:T(8,128)(2,1)}, u32[]{:S(2)}, u32[]{:S(2)}) %collective-permute-start.135) | collective-permute-done | bytes 2097184 | tf_op jit(solution)/shard_map/ppermute | solution.py:369
  1368.4 39.2 %collective-permute-done.143 = bf16[512,2048]{1,0:T(8,128)(2,1)} collective-permute-done((bf16[512,2048]{1,0:T(8,128)(2,1)}, bf16[512,2048]{1,0:T(8,128)(2,1)}, u32[]{:S(2)}, u32[]{:S(2)}) %collective-permute-start.143) | collective-permute-done | bytes 2097184 | tf_op jit(solution)/shard_map/ppermute | solution.py:369
  1432.5 20.1 %collective-permute-done.93 = bf16[512,1024]{1,0:T(8,128)(2,1)} collective-permute-done((bf16[512,1024]{1,0:T(8,128)(2,1)}, bf16[512,1024]{1,0:T(8,128)(2,1)}, u32[]{:S(2)}, u32[]{:S(2)}) %collective-permute-start.93) | collective-permute-done | bytes 1048608 | tf_op jit(solution)/shard_map/ppermute | solution.py:369
  1472.5 47.7 %collective-permute-done.123 = bf16[512,512]{1,0:T(8,128)(2,1)S(1)} collective-permute-done((bf16[512,512]{1,0:T(8,128)(2,1)S(1)}, bf16[512,512]{1,0:T(8,128)(2,1)S(1)}, u32[]{:S(2)}, u32[]{:S(2)}) %collective-permute-start.123) | collective-permute-done | bytes 524320 | tf_op jit(solution)/shard_map/ppermute | solution.py:378
  1522.6 28.6 %collective-permute-done.125 = bf16[512,512]{1,0:T(8,128)(2,1)S(1)} collective-permute-done((bf16[512,512]{1,0:T(8,128)(2,1)S(1)}, bf16[512,512]{1,0:T(8,128)(2,1)S(1)}, u32[]{:S(2)}, u32[]{:S(2)}) %collective-permute-start.125) | collective-permute-done | bytes 524320 | tf_op jit(solution)/shard_map/ppermute | solution.py:379
  1554.4 32.5 %collective-permute-done.95 = bf16[256,1024]{1,0:T(8,128)(2,1)S(1)} collective-permute-done((bf16[256,1024]{1,0:T(8,128)(2,1)S(1)}, bf16[256,1024]{1,0:T(8,128)(2,1)S(1)}, u32[]{:S(2)}, u32[]{:S(2)}) %collective-permute-start.95) | collective-permute-done | bytes 524320 | tf_op jit(solution)/shard_map/ppermute | solution.py:378
  1622.5 20.5 %collective-permute-done.165 = bf16[1024,512]{1,0:T(8,128)(2,1)S(1)} collective-permute-done((bf16[1024,512]{1,0:T(8,128)(2,1)S(1)}, bf16[1024,512]{1,0:T(8,128)(2,1)S(1)}, u32[]{:S(2)}, u32[]{:S(2)}) %collective-permute-start.165) | collective-permute-done | bytes 1048608 | tf_op jit(solution)/shard_map/ppermute | solution.py:378
  1647.1 18.4 %collective-permute-done.167 = bf16[1024,512]{1,0:T(8,128)(2,1)S(1)} collective-permute-done((bf16[1024,512]{1,0:T(8,128)(2,1)S(1)}, bf16[1024,512]{1,0:T(8,128)(2,1)S(1)}, u32[]{:S(2)}, u32[]{:S(2)}) %collective-permute-start.167) | collective-permute-done | bytes 1048608 | tf_op jit(solution)/shard_map/ppermute | solution.py:379
  1670.1 17.9 %collective-permute-done.137 = bf16[256,2048]{1,0:T(8,128)(2,1)S(1)} collective-permute-done((bf16[256,2048]{1,0:T(8,128)(2,1)S(1)}, bf16[256,2048]{1,0:T(8,128)(2,1)S(1)}, u32[]{:S(2)}, u32[]{:S(2)}) %collective-permute-start.137) | collective-permute-done | bytes 1048608 | tf_op jit(solution)/shard_map/ppermute | solution.py:378
  1688.0 42.9 %collective-permute-done.139 = bf16[256,2048]{1,0:T(8,128)(2,1)S(1)} collective-permute-done((bf16[256,2048]{1,0:T(8,128)(2,1)S(1)}, bf16[256,2048]{1,0:T(8,128)(2,1)S(1)}, u32[]{:S(2)}, u32[]{:S(2)}) %collective-permute-start.139) | collective-permute-done | bytes 1048608 | tf_op jit(solution)/shard_map/ppermute | solution.py:379
  (787 shorter events, 734.7 us)
Async XLA Ops:
  151.0 95.7 %collective-permute-start.37 = (bf16[512,4096]{1,0:T(8,128)(2,1)}, bf16[512,4096]{1,0:T(8,128)(2,1)}, u32[]{:S(2)}, u32[]{:S(2)}) collective-permute-start(bf16[512,4096]{1,0:T(8,128)(2,1)} %param.30), channel_id=1, source_target_pairs={{0,2},{1,3},{2,0},{3,1},{4,6},{5,7},{6,4},{7,5},{8,10},{9,11},{10,... | collective-permute-start | bytes 12582920 | tf_op jit(solution)/shard_map/ppermute | solution.py:195
  152.6 181.6 %collective-permute-start.40 = (bf16[4096,512]{1,0:T(8,128)(2,1)}, bf16[4096,512]{1,0:T(8,128)(2,1)}, u32[]{:S(2)}, u32[]{:S(2)}) collective-permute-start(bf16[4096,512]{1,0:T(8,128)(2,1)} %param.32), channel_id=1, source_target_pairs={{0,2},{1,3},{2,0},{3,1},{4,6},{5,7},{6,4},{7,5},{8,10},{9,11},{10,... | collective-permute-start | bytes 12582920 | tf_op jit(solution)/shard_map/ppermute | solution.py:195
  171.9 171.1 %collective-permute-start.36 = (bf16[512,4096]{1,0:T(8,128)(2,1)}, bf16[512,4096]{1,0:T(8,128)(2,1)}, u32[]{:S(2)}, u32[]{:S(2)}) collective-permute-start(bf16[512,4096]{1,0:T(8,128)(2,1)} %param.30), channel_id=1, source_target_pairs={{0,1},{1,0},{2,3},{3,2},{4,5},{5,4},{6,7},{7,6},{8,9},{9,8},{10,11... | collective-permute-start | bytes 12582920 | tf_op jit(solution)/shard_map/ppermute | solution.py:195
  189.0 164.8 %collective-permute-start.39 = (bf16[4096,512]{1,0:T(8,128)(2,1)}, bf16[4096,512]{1,0:T(8,128)(2,1)S(1)}, u32[]{:S(2)}, u32[]{:S(2)}) collective-permute-start(bf16[4096,512]{1,0:T(8,128)(2,1)} %param.32), channel_id=1, source_target_pairs={{0,1},{1,0},{2,3},{3,2},{4,5},{5,4},{6,7},{7,6},{8,9},{9,8},{10,11... | collective-permute-start | bytes 12582920 | tf_op jit(solution)/shard_map/ppermute | solution.py:195
  189.0 265.6 %collective-permute-start.50 = (bf16[512,512]{1,0:T(8,128)(2,1)}, bf16[512,512]{1,0:T(8,128)(2,1)}, u32[]{:S(2)}, u32[]{:S(2)}) collective-permute-start(bf16[512,512]{1,0:T(8,128)(2,1)} %pad_maximum_fusion.7), channel_id=1, source_target_pairs={{0,1},{1,0},{2,3},{3,2},{4,5},{5,4},{6,7},{7,6},{8,9},{9,8},{10,11... | collective-permute-start | bytes 1572872 | tf_op jit(solution)/shard_map/ppermute | solution.py:205
  246.7 115.4 %collective-permute-start.38 = (bf16[512,4096]{1,0:T(8,128)(2,1)}, bf16[512,4096]{1,0:T(8,128)(2,1)}, u32[]{:S(2)}, u32[]{:S(2)}) collective-permute-start(bf16[512,4096]{1,0:T(8,128)(2,1)} %collective-permute-done.37), channel_id=1, source_target_pairs={{0,1},{1,0},{2,3},{3,2},{4,5},{5,4},{6,7},{7,6},{8,9},{9,8},{10,11... | collective-permute-start | bytes 12582920 | tf_op jit(solution)/shard_map/ppermute | solution.py:195
  343.7 112.8 %collective-permute-start.51 = (bf16[512,512]{1,0:T(8,128)(2,1)S(1)}, bf16[512,512]{1,0:T(8,128)(2,1)S(1)}, u32[]{:S(2)}, u32[]{:S(2)}) collective-permute-start(bf16[512,512]{1,0:T(8,128)(2,1)S(1)} %copy-done.77), channel_id=1, source_target_pairs={{0,2},{1,3},{2,0},{3,1},{4,6},{5,7},{6,4},{7,5},{8,10},{9,11},{10,... | collective-permute-start | bytes 1572872 | tf_op jit(solution)/shard_map/ppermute | solution.py:205
  362.1 96.8 %collective-permute-start.52 = (bf16[512,512]{1,0:T(8,128)(2,1)S(1)}, bf16[512,512]{1,0:T(8,128)(2,1)S(1)}, u32[]{:S(2)}, u32[]{:S(2)}) collective-permute-start(bf16[512,512]{1,0:T(8,128)(2,1)S(1)} %copy-done.78), channel_id=1, source_target_pairs={{0,3},{1,2},{2,1},{3,0},{4,7},{5,6},{6,5},{7,4},{8,11},{9,10},{10,... | collective-permute-start | bytes 1572872 | tf_op jit(solution)/shard_map/ppermute | solution.py:205
  367.6 84.7 %collective-permute-start.63 = (f32[8,128]{1,0:T(8,128)S(1)}, f32[8,128]{1,0:T(8,128)S(1)}, u32[]{:S(2)}, u32[]{:S(2)}) collective-permute-start(f32[8,128]{1,0:T(8,128)S(1)} %broadcast_add_fusion), channel_id=1, source_target_pairs={{0,8},{8,0},{16,24},{24,16},{1,9},{9,1},{17,25},{25,17},{2,10},{10... | collective-permute-start | bytes 12296 | tf_op jit(solution)/shard_map/ppermute | solution.py:195
  450.8 91.2 %collective-permute-start.42 = (bf16[512,2048]{1,0:T(8,128)(2,1)S(1)}, bf16[512,2048]{1,0:T(8,128)(2,1)S(1)}, u32[]{:S(2)}, u32[]{:S(2)}) collective-permute-start(bf16[512,2048]{1,0:T(8,128)(2,1)S(1)} %slice.788), channel_id=1, source_target_pairs={{0,4},{4,0},{1,5},{5,1},{2,6},{6,2},{3,7},{7,3},{8,12},{12,8},{9,1... | collective-permute-start | bytes 6291464 | tf_op jit(solution)/shard_map/ppermute | solution.py:195
  657.4 220.7 %collective-permute-start.153 = (bf16[2048,512]{1,0:T(8,128)(2,1)}, bf16[2048,512]{1,0:T(8,128)(2,1)}, u32[]{:S(2)}, u32[]{:S(2)}) collective-permute-start(bf16[2048,512]{1,0:T(8,128)(2,1)} %convolution_convert_fusion.2), channel_id=1, source_target_pairs={{0,1},{1,0},{2,3},{3,2},{4,5},{5,4},{6,7},{7,6},{8,9},{9,8},{10,11... | collective-permute-start | bytes 6291464 | tf_op jit(solution)/shard_map/ppermute | solution.py:195
  662.4 224.0 %collective-permute-start.161 = (bf16[2048,512]{1,0:T(8,128)(2,1)}, bf16[2048,512]{1,0:T(8,128)(2,1)}, u32[]{:S(2)}, u32[]{:S(2)}) collective-permute-start(bf16[2048,512]{1,0:T(8,128)(2,1)} %convolution_convert_fusion), channel_id=1, source_target_pairs={{0,1},{1,0},{2,3},{3,2},{4,5},{5,4},{6,7},{7,6},{8,9},{9,8},{10,11... | collective-permute-start | bytes 6291464 | tf_op jit(solution)/shard_map/ppermute | solution.py:195
  724.4 143.1 %collective-permute-start.133 = (bf16[512,2048]{1,0:T(8,128)(2,1)}, bf16[512,2048]{1,0:T(8,128)(2,1)}, u32[]{:S(2)}, u32[]{:S(2)}) collective-permute-start(bf16[512,2048]{1,0:T(8,128)(2,1)} %convolution_convert_fusion.6), channel_id=1, source_target_pairs={{0,1},{1,0},{2,3},{3,2},{4,5},{5,4},{6,7},{7,6},{8,9},{9,8},{10,11... | collective-permute-start | bytes 6291464 | tf_op jit(solution)/shard_map/ppermute | solution.py:195
  752.8 140.5 %collective-permute-start.141 = (bf16[512,2048]{1,0:T(8,128)(2,1)}, bf16[512,2048]{1,0:T(8,128)(2,1)}, u32[]{:S(2)}, u32[]{:S(2)}) collective-permute-start(bf16[512,2048]{1,0:T(8,128)(2,1)} %convolution_convert_fusion.4), channel_id=1, source_target_pairs={{0,1},{1,0},{2,3},{3,2},{4,5},{5,4},{6,7},{7,6},{8,9},{9,8},{10,11... | collective-permute-start | bytes 6291464 | tf_op jit(solution)/shard_map/ppermute | solution.py:195
  793.7 109.3 %collective-permute-start.127 = (f32[4,512]{1,0:T(4,128)S(1)}, f32[4,512]{1,0:T(4,128)S(1)}, u32[]{:S(2)}, u32[]{:S(2)}) collective-permute-start(f32[4,512]{1,0:T(4,128)S(1)} %get-tuple-element.133), channel_id=1, source_target_pairs={{0,1},{1,0},{2,3},{3,2},{4,5},{5,4},{6,7},{7,6},{8,9},{9,8},{10,11... | collective-permute-start | bytes 24584 | tf_op jit(solution)/shard_map/ppermute | solution.py:195
  980.4 88.2 %collective-permute-start.132 = (bf16[512,2048]{1,0:T(8,128)(2,1)S(1)}, bf16[512,2048]{1,0:T(8,128)(2,1)S(1)}, u32[]{:S(2)}, u32[]{:S(2)}) collective-permute-start(bf16[512,2048]{1,0:T(8,128)(2,1)S(1)} %copy-done.102), channel_id=1, source_target_pairs={{0,1},{1,0},{2,3},{3,2},{4,5},{5,4},{6,7},{7,6},{8,9},{9,8},{10,11... | collective-permute-start | bytes 6291464 | tf_op jit(solution)/shard_map/ppermute | solution.py:195
  1079.8 155.5 %collective-permute-start.142 = (bf16[512,2048]{1,0:T(8,128)(2,1)}, bf16[512,2048]{1,0:T(8,128)(2,1)S(1)}, u32[]{:S(2)}, u32[]{:S(2)}) collective-permute-start(bf16[512,2048]{1,0:T(8,128)(2,1)} %add_convert_fusion.2), channel_id=1, source_target_pairs={{0,2},{1,3},{2,0},{3,1},{4,6},{5,7},{6,4},{7,5},{8,10},{9,11},{10,... | collective-permute-start | bytes 6291464 | tf_op jit(solution)/shard_map/ppermute | solution.py:195
  1107.0 98.6 %collective-permute-start.105 = (f32[512,256]{1,0:T(8,128)S(1)}, f32[512,256]{1,0:T(8,128)}, u32[]{:S(2)}, u32[]{:S(2)}) collective-permute-start(f32[512,256]{1,0:T(8,128)S(1)} %convolution_add_fusion.1), channel_id=1, source_target_pairs={{0,2},{1,3},{2,0},{3,1},{4,6},{5,7},{6,4},{7,5},{8,10},{9,11},{10,... | collective-permute-start | bytes 1572872 | tf_op jit(solution)/shard_map/ppermute | solution.py:195
  1116.5 96.2 %collective-permute-start.86 = (bf16[512,1024]{1,0:T(8,128)(2,1)}, bf16[512,1024]{1,0:T(8,128)(2,1)S(1)}, u32[]{:S(2)}, u32[]{:S(2)}) collective-permute-start(bf16[512,1024]{1,0:T(8,128)(2,1)} %convolution_convert_fusion.16), channel_id=1, source_target_pairs={{0,1},{1,0},{2,3},{3,2},{4,5},{5,4},{6,7},{7,6},{8,9},{9,8},{10,11... | collective-permute-start | bytes 3145736 | tf_op jit(solution)/shard_map/ppermute | solution.py:195
  1152.0 84.6 %collective-permute-start.116 = (bf16[1024,512]{1,0:T(8,128)(2,1)}, bf16[1024,512]{1,0:T(8,128)(2,1)}, u32[]{:S(2)}, u32[]{:S(2)}) collective-permute-start(bf16[1024,512]{1,0:T(8,128)(2,1)} %add_convert_fusion.12), channel_id=1, source_target_pairs={{0,4},{4,0},{1,5},{5,1},{2,6},{6,2},{3,7},{7,3},{8,12},{12,8},{9,1... | collective-permute-start | bytes 3145736 | tf_op jit(solution)/shard_map/ppermute | solution.py:195
  1212.7 111.5 %collective-permute-start.155 = (bf16[2048,512]{1,0:T(8,128)(2,1)}, bf16[2048,512]{1,0:T(8,128)(2,1)}, u32[]{:S(2)}, u32[]{:S(2)}) collective-permute-start(bf16[2048,512]{1,0:T(8,128)(2,1)} %get-tuple-element.168), channel_id=1, source_target_pairs={{0,8},{24,16},{1,9},{25,17},{2,10},{26,18},{3,11},{27,19},{4,12},{... | collective-permute-start | bytes 6291464 | tf_op jit(solution)/shard_map/ppermute | solution.py:369
  1236.6 94.5 %collective-permute-start.163 = (bf16[2048,512]{1,0:T(8,128)(2,1)}, bf16[2048,512]{1,0:T(8,128)(2,1)}, u32[]{:S(2)}, u32[]{:S(2)}) collective-permute-start(bf16[2048,512]{1,0:T(8,128)(2,1)} %get-tuple-element.166), channel_id=1, source_target_pairs={{0,8},{24,16},{1,9},{25,17},{2,10},{26,18},{3,11},{27,19},{4,12},{... | collective-permute-start | bytes 6291464 | tf_op jit(solution)/shard_map/ppermute | solution.py:369
  1263.6 192.2 %collective-permute-start.79 = (bf16[256,512]{1,0:T(8,128)(2,1)}, bf16[256,512]{1,0:T(8,128)(2,1)}, u32[]{:S(2)}, u32[]{:S(2)}) collective-permute-start(bf16[256,512]{1,0:T(8,128)(2,1)} %get-tuple-element.70), channel_id=1, source_target_pairs={{0,7},{1,6},{2,5},{3,4},{4,3},{5,2},{6,1},{7,0},{8,15},{9,14},{10,... | collective-permute-start | bytes 786440 | tf_op jit(solution)/shard_map/ppermute | solution.py:205
  1317.6 90.0 %collective-permute-start.143 = (bf16[512,2048]{1,0:T(8,128)(2,1)}, bf16[512,2048]{1,0:T(8,128)(2,1)}, u32[]{:S(2)}, u32[]{:S(2)}) collective-permute-start(bf16[512,2048]{1,0:T(8,128)(2,1)} %get-tuple-element.160), channel_id=1, source_target_pairs={{0,8},{24,16},{1,9},{25,17},{2,10},{26,18},{3,11},{27,19},{4,12},{... | collective-permute-start | bytes 6291464 | tf_op jit(solution)/shard_map/ppermute | solution.py:369
  1324.3 105.8 %collective-permute-start.121 = (bf16[1024,512]{1,0:T(8,128)(2,1)}, bf16[1024,512]{1,0:T(8,128)(2,1)}, u32[]{:S(2)}, u32[]{:S(2)}) collective-permute-start(bf16[1024,512]{1,0:T(8,128)(2,1)} %get-tuple-element.158), channel_id=1, source_target_pairs={{0,8},{24,16},{1,9},{25,17},{2,10},{26,18},{3,11},{27,19},{4,12},{... | collective-permute-start | bytes 3145736 | tf_op jit(solution)/shard_map/ppermute | solution.py:369
  1331.1 121.5 %collective-permute-start.93 = (bf16[512,1024]{1,0:T(8,128)(2,1)}, bf16[512,1024]{1,0:T(8,128)(2,1)}, u32[]{:S(2)}, u32[]{:S(2)}) collective-permute-start(bf16[512,1024]{1,0:T(8,128)(2,1)} %get-tuple-element.156), channel_id=1, source_target_pairs={{0,8},{24,16},{1,9},{25,17},{2,10},{26,18},{3,11},{27,19},{4,12},{... | collective-permute-start | bytes 3145736 | tf_op jit(solution)/shard_map/ppermute | solution.py:369
  1362.7 98.3 %collective-permute-start.108 = (f32[512,256]{1,0:T(8,128)}, f32[512,256]{1,0:T(8,128)}, u32[]{:S(2)}, u32[]{:S(2)}) collective-permute-start(f32[512,256]{1,0:T(8,128)} %add.634), channel_id=1, source_target_pairs={{0,8},{8,0},{16,24},{24,16},{1,9},{9,1},{17,25},{25,17},{2,10},{10... | collective-permute-start | bytes 1572872 | tf_op jit(solution)/shard_map/ppermute | solution.py:195
  1462.8 89.7 %collective-permute-start.158 = (bf16[1024,512]{1,0:T(8,128)(2,1)S(1)}, bf16[1024,512]{1,0:T(8,128)(2,1)S(1)}, u32[]{:S(2)}, u32[]{:S(2)}) collective-permute-start(bf16[1024,512]{1,0:T(8,128)(2,1)S(1)} %add_convert_fusion.7), channel_id=1, source_target_pairs={{8,16},{16,8},{9,17},{17,9},{10,18},{18,10},{11,19},{19,11},{12,20... | collective-permute-start | bytes 3145736 | tf_op jit(solution)/shard_map/ppermute | solution.py:377
  1471.2 127.6 %collective-permute-start.157 = (bf16[1024,512]{1,0:T(8,128)(2,1)S(1)}, bf16[1024,512]{1,0:T(8,128)(2,1)S(1)}, u32[]{:S(2)}, u32[]{:S(2)}) collective-permute-start(bf16[1024,512]{1,0:T(8,128)(2,1)S(1)} %add_convert_fusion.7), channel_id=1, source_target_pairs={{8,0},{16,24},{9,1},{17,25},{10,2},{18,26},{11,3},{19,27},{12,4},{... | collective-permute-start | bytes 3145736 | tf_op jit(solution)/shard_map/ppermute | solution.py:378
  1643.1 90.1 %collective-permute-start.145 = (bf16[256,2048]{1,0:T(8,128)(2,1)S(1)}, bf16[256,2048]{1,0:T(8,128)(2,1)S(1)}, u32[]{:S(2)}, u32[]{:S(2)}) collective-permute-start(bf16[256,2048]{1,0:T(8,128)(2,1)S(1)} %add_convert_fusion.8), channel_id=1, source_target_pairs={{8,0},{16,24},{9,1},{17,25},{10,2},{18,26},{11,3},{19,27},{12,4},{... | collective-permute-start | bytes 3145736 | tf_op jit(solution)/shard_map/ppermute | solution.py:378
  1644.4 86.6 %collective-permute-start.139 = (bf16[256,2048]{1,0:T(8,128)(2,1)S(1)}, bf16[256,2048]{1,0:T(8,128)(2,1)S(1)}, u32[]{:S(2)}, u32[]{:S(2)}) collective-permute-start(bf16[256,2048]{1,0:T(8,128)(2,1)S(1)} %collective-permute-done.138), channel_id=1, source_target_pairs={{8,0},{16,24},{9,1},{17,25},{10,2},{18,26},{11,3},{19,27},{12,4},{... | collective-permute-start | bytes 3145736 | tf_op jit(solution)/shard_map/ppermute | solution.py:379
  1645.7 96.5 %collective-permute-start.147 = (bf16[256,2048]{1,0:T(8,128)(2,1)S(1)}, bf16[256,2048]{1,0:T(8,128)(2,1)S(1)}, u32[]{:S(2)}, u32[]{:S(2)}) collective-permute-start(bf16[256,2048]{1,0:T(8,128)(2,1)S(1)} %collective-permute-done.146), channel_id=1, source_target_pairs={{8,0},{16,24},{9,1},{17,25},{10,2},{18,26},{11,3},{19,27},{12,4},{... | collective-permute-start | bytes 3145736 | tf_op jit(solution)/shard_map/ppermute | solution.py:379
  (263 other events, 8074.2 us)

commit v2 on v1

--- a/solution.py
+++ b/solution.py
@@ -214,31 +214,52 @@
     return (key[0] ^ mask, key[1]) if axis == "row" else (key[0], key[1] ^ mask)
 
 
-def gather_pieces(x, steps):
-    pieces = {(0, 0): x}
+def grow(parts, axis, masks):
+    for mask in masks:
+        parts = parts + [send(part, axis, mask) for part in parts]
+    return parts
+
+
+class Fold:
+    def __init__(self, left, right):
+        self.left, self.right, self.arrived = left, right, []
+        self.limits = [left.shape[1], right.shape[1]]
+
+    def part(self, rows, cols):
+        made = dot_tn(self.left[:, rows[0] : rows[1]], self.right[:, cols[0] : cols[1]])
+        for other in self.arrived:
+            made = made + other[rows[0] : rows[1], cols[0] : cols[1]].astype(f32)
+        return made
+
+    def step(self, dim, axis, mask, *needed):
+        if needed:
+            self.left = after(self.left, *needed)
+        half = self.limits[dim] // 2
+        spans = [(0, self.limits[0]), (0, self.limits[1])]
+        spans[dim] = (half, self.limits[dim])
+        leaving = self.part(*spans).astype(bf16)
+        self.arrived = [lax.slice_in_dim(other, 0, half, axis=dim) for other in self.arrived]
+        self.arrived.append(send(leaving, axis, mask))
+        self.limits[dim] = half
+        return leaving
+
+    def home(self, skip=0):
+        kept = self.arrived
+        self.arrived = kept[: len(kept) - skip]
+        made = self.part((0, self.limits[0]), (0, self.limits[1]))
+        self.arrived = kept
+        return made
+
+
+def halve_sum(x, steps):
     for axis, mask in steps:
-        for key in list(pieces):
-            pieces[other_key(key, axis, mask)] = send(pieces[key], axis, mask)
-    return pieces
-
-
-def reduce_pieces(pieces, steps, wire):
-    pieces = dict(pieces)
-    for axis, mask in steps:
-        at = 0 if axis == "row" else 1
-        for key in [key for key in pieces if key[at] & mask]:
-            arrived = send(pieces.pop(key).astype(wire), axis, mask)
-            home = other_key(key, axis, mask)
-            pieces[home] = pieces[home].astype(f32) + arrived.astype(f32)
-    return pieces[(0, 0)]
-
-
-def join(pieces, rows, cols):
-    strips = [
-        jnp.concatenate([pieces[(i, j)] for i in range(rows)], 1) if rows > 1 else pieces[(0, j)]
-        for j in range(cols)
-    ]
-    return jnp.concatenate(strips, 0) if cols > 1 else strips[0]
+        half = x.shape[0] // 2
+        x = x[:half] + send(x[half:], axis, mask)
+    return x
+
+
+def after(x, *needed):
+    return lax.optimization_barrier((x,) + needed)[0]
 
 
 def everywhere(x, axes):
@@ -291,46 +312,91 @@
     return lax.dot_general(a, b, TN, preferred_element_type=f32)
 
 
-def chunk_rows(chunk, i, j):
+def flips():
+    if lax.axis_size("row") == 2:
+        return [lax.axis_index("row") ^ i for i in range(2)]
+    return [0, 1]
+
+
+def pick(halves, bit):
+    rows = halves.shape[0] // 2
+    return [
+        lax.dynamic_slice_in_dim(halves, jnp.where(bit == stay, 0, rows), rows, 0)
+        for stay in (0, 1)
+    ]
+
+
+def place_bits(mask):
+    count_col = lax.axis_size("col")
+    col = lax.axis_index("col")
+    return [jnp.where((col ^ ((count_col - 1) * flip)) & mask, 1, 0) for flip in flips()]
+
+
+def to_tokens_direct(block, chunk):
     count_row, count_col = lax.axis_size("row"), lax.axis_size("col")
-    r, c = lax.axis_index("row"), lax.axis_index("col") ^ j
-    if count_row == 2:
-        owner = (r ^ i) * count_col + c
-        return jnp.where(r == 0, owner, 2 * count_col - 1 - owner) * chunk
-    return (c if i == 0 else 2 * count_col - 1 - c) * chunk
-
-
-def chunk_send(x, i, j):
+    out = {}
+    for i in range(2):
+        for j in range(count_col):
+            flip = lax.axis_index("row") if count_row == 2 else i
+            place = lax.axis_index("col") ^ j ^ ((count_col - 1) * flip)
+            part = lax.dynamic_slice_in_dim(block, (i * count_col + place) * chunk, chunk, 0)
+            if count_row == 2:
+                out[(i, j)] = send_pair(part, i, j) if i or j else part
+            else:
+                out[(i, j)] = send(part, "col", j) if j else part
+    return out
+
+
+def to_tokens(block, chunk, waits):
+    half = block.shape[0] // 2
+    lower, upper = block[:half], block[half:]
     if lax.axis_size("row") == 2:
-        return send_pair(x, i, j) if i or j else x
-    return send(x, "col", j) if j else x
-
-
-def to_tokens(block, chunk):
-    count_col = lax.axis_size("col")
-    return [
-        [
-            chunk_send(lax.dynamic_slice_in_dim(block, chunk_rows(chunk, i, j), chunk, 0), i, j)
-            for j in range(count_col)
-        ]
+        upper = send(after(upper, waits[0]), "row", 1)
+    groups = {(0, 0): lower, (1, 0): upper}
+    for mask, wait in zip(masks_of("col"), waits[1:]):
+        groups[(1, 0)] = after(groups[(1, 0)], wait)
+        bits = place_bits(mask)
+        leaving = []
+        for key in list(groups):
+            groups[key], gone = pick(groups[key], bits[key[0]])
+            leaving.append(gone)
+        arrived = send(jnp.concatenate(leaving, 0), "col", mask)
+        rows = leaving[0].shape[0]
+        for k, key in enumerate(list(groups)):
+            groups[(key[0], key[1] ^ mask)] = arrived[k * rows : (k + 1) * rows]
+    return groups
+
+
+def assemble(groups, order):
+    return jnp.concatenate(
+        [jnp.concatenate([groups[(i, j)] for j in order], 1) for i in range(2)], 0
+    )
+
+
+def from_tokens(tokens, chunk, width, order):
+    low = tokens.astype(bf16)
+    groups = {
+        (i, j): low[i * chunk : (i + 1) * chunk, k * width : (k + 1) * width]
         for i in range(2)
-    ]
-
-
-def assemble(pieces):
-    return jnp.concatenate([jnp.concatenate(strip, 1) for strip in pieces], 0)
-
-
-def from_tokens(tokens, chunk, width, rows):
-    out = jnp.zeros((rows, width), f32)
-    low = tokens.astype(bf16)
-    for i in range(2):
-        for j in range(lax.axis_size("col")):
-            part = low[i * chunk : (i + 1) * chunk, j * width : (j + 1) * width]
-            out = lax.dynamic_update_slice_in_dim(
-                out, chunk_send(part, i, j).astype(f32), chunk_rows(chunk, i, j), 0
+        for k, j in enumerate(order)
+    }
+    for mask in masks_of("col")[::-1]:
+        bits = place_bits(mask)
+        leaving = [key for key in groups if key[1] & mask]
+        rows = groups[leaving[0]].shape[0]
+        arrived = send(jnp.concatenate([groups[key] for key in leaving], 0), "col", mask)
+        for k, key in enumerate(leaving):
+            del groups[key]
+            kept = groups[(key[0], key[1] ^ mask)]
+            came = arrived[k * rows : (k + 1) * rows]
+            swap = bits[key[0]] == 1
+            groups[(key[0], key[1] ^ mask)] = jnp.concatenate(
+                [jnp.where(swap, came, kept), jnp.where(swap, kept, came)], 0
             )
-    return out
+    upper = groups[(1, 0)]
+    if lax.axis_size("row") == 2:
+        upper = send(upper, "row", 1)
+    return jnp.concatenate([groups[(0, 0)], upper], 0).astype(f32)
 
 
 def token_starts(chunk):
@@ -357,32 +423,38 @@
         owner_row = half
         which = (local >= count_col).astype(jnp.int32)
         owner_col = jnp.where(which == 0, local, 2 * count_col - 1 - local)
-    return ((owner_row ^ r) * count_col + (owner_col ^ c)) * 2 + which
-
-
-def over_dp(total, wire):
-    size = lax.axis_size("dp")
-    if size != 4:
-        return everywhere(total, ["dp"])
+    place = jnp.zeros_like(group)
+    for k, (axis, mask) in enumerate(gather_steps()):
+        relative = owner_row ^ r if axis == "row" else owner_col ^ c
+        place = place + jnp.where(relative & mask, 1 << k, 0)
+    return place * 2 + which
+
+
+def gather_steps():
+    col = [("col", mask) for mask in masks_of("col")]
+    return col[:-1] + [("row", mask) for mask in masks_of("row")] + col[-1:]
+
+
+def inward(total, wire):
+    if lax.axis_size("dp") != 4:
+        return total
+    return lax.ppermute(total.astype(wire), "dp", [(0, 1), (3, 2)])
+
+
+def across_middle(total, arrived, wire):
+    if lax.axis_size("dp") != 4:
+        return (total, total)
+    held = (total + arrived.astype(f32)).astype(wire)
+    return (held, lax.ppermute(held, "dp", [(1, 2), (2, 1)]))
+
+
+def outward(held, arrived, wire):
+    if lax.axis_size("dp") != 4:
+        return everywhere(held, ["dp"])
+    final = (held.astype(f32) + arrived.astype(f32)).astype(wire)
     z = lax.axis_index("dp")
-    half = total.shape[0] // 2
-    total = total + lax.ppermute(total.astype(wire), "dp", [(0, 1), (3, 2)]).astype(f32)
-    own_at = jnp.where(z < 2, 0, half)
-    far_at = half - own_at
-    middle = [(1, 2), (2, 1)]
-    outward = [(1, 0), (2, 3)]
-    far = lax.dynamic_slice_in_dim(total, far_at, half, 0).astype(wire)
-    own = lax.dynamic_slice_in_dim(total, own_at, half, 0)
-    own = (own + lax.ppermute(far, "dp", middle).astype(f32)).astype(wire)
-    far = lax.ppermute(own, "dp", middle)
-    own_out = lax.ppermute(own, "dp", outward)
-    far_out = lax.ppermute(far, "dp", outward)
-    inside = (z == 1) | (z == 2)
-    own = jnp.where(inside, own, own_out).astype(f32)
-    far = jnp.where(inside, far, far_out).astype(f32)
-    first = jnp.where(z < 2, own, far)
-    second = jnp.where(z < 2, far, own)
-    return jnp.concatenate([first, second], 0)
+    end = lax.ppermute(final, "dp", [(1, 0), (2, 3)])
+    return jnp.where((z == 1) | (z == 2), final, end).astype(f32)
 
 
 def per_device(
@@ -412,56 +484,32 @@
     rows_a, width = layer_input.shape
     wide = w_query.shape[1]
     chunk = rows_a // (2 * count_col)
-    col_in = [("col", m) for m in masks_of("col")]
-    row_in = [("row", m) for m in masks_of("row")]
-    col_out, row_out = col_in[::-1], row_in[::-1]
-    near, across = col_in[-1:], col_in[:-1]
-    all_in = across + row_in + near
-    all_out = near + row_out + across[::-1]
+    col_far, near = masks_of("col")[:-1], masks_of("col")[-1]
+    row_masks = masks_of("row")
+    all_out = gather_steps()[::-1]
+    order = [0]
+    for mask in masks_of("col"):
+        order = order + [j ^ mask for j in order]
+    split = D // 2
     valid_flat = valid_mask.reshape(-1)
     block_flat = block_ids.reshape(-1)
 
-    x_pieces = to_tokens(layer_input, chunk)
-    vectors = gather_pieces(
-        jnp.stack([norm1_gain, norm1_shift, b_attn_out, norm2_gain, norm2_shift, b_fc_out]), col_in
-    )
-    vectors = jnp.concatenate([vectors[(0, j)] for j in range(count_col)], 1)
+    x_groups = to_tokens_direct(layer_input, chunk)
+    keyval_near = jnp.concatenate(grow([w_keyval], "col", col_far), 0)
+    keyval_far = send(keyval_near, "col", near)
+    query_parts = [
+        jnp.concatenate(parts, 0)
+        for parts in zip(*[grow([part], "row", row_masks) for part in grow([w_query], "col", col_far)])
+    ]
+    query_near = jnp.concatenate(query_parts, 0)
+    query_far = send(query_near, "col", near)
+    vectors = jnp.stack(
+        [norm1_gain, norm1_shift, b_attn_out, norm2_gain, norm2_shift, b_fc_out]
+    )
+    vectors = jnp.concatenate(grow([vectors], "col", col_far), 1)
+    vectors = jnp.concatenate([vectors, send(vectors, "col", near)], 1)
     gain1, shift1, bias_o, gain2, shift2, bias_out = [vectors[k : k + 1] for k in range(6)]
-    bias_q = gather_pieces(b_query[None, :], row_in)
-    bias_q = jnp.concatenate([bias_q[(i, 0)] for i in range(count_row)], 1)
-    keyval_w = join(gather_pieces(w_keyval, col_in), 1, count_col)
-    query_w = join(gather_pieces(w_query, all_in), count_row, count_col)
-    attn_pieces = gather_pieces(w_attn_out, all_in)
-    attn_w = jnp.concatenate(
-        [
-            jnp.concatenate([attn_pieces[(i, j)] for j in range(count_col)], 1)
-            for i in range(count_row)
-        ],
-        0,
-    )
-    fc_in_pieces = gather_pieces(w_fc_in, col_in)
-    fc_in_w = jnp.concatenate([fc_in_pieces[(0, j)] for j in range(count_col)], 0)
-    fc_out_pieces = gather_pieces(w_fc_out, col_in)
-    fc_out_w = jnp.concatenate([fc_out_pieces[(0, j)] for j in range(count_col)], 1)
-    late_pieces = [
-        [
-            chunk_send(
-                jnp.concatenate(
-                    [
-                        lax.dynamic_slice_in_dim(block, chunk_rows(chunk, i, j), chunk, 0)
-                        for block in (teacher, out_cotangent)
-                    ],
-                    0,
-                ),
-                i,
-                j,
-            )
-            for j in range(count_col)
-        ]
-        for i in range(2)
-    ]
-    target = assemble([[piece[:chunk] for piece in strip] for strip in late_pieces])
-    cotangent = assemble([[piece[chunk:] for piece in strip] for strip in late_pieces])
+    bias_q = jnp.concatenate(grow([b_query[None, :]], "row", row_masks), 1)
 
     starts = token_starts(chunk)
     block_own = jnp.concatenate(
@@ -474,155 +522,245 @@
     reach = jnp.sum((block_flat[None, :] <= block_own[:, None]).astype(jnp.int32), 1)
     limits = jnp.minimum(reach, valid_length)
     slots = key_slots()
-    valid_count = everywhere(jnp.full((8, 128), valid_length.astype(f32)), ["dp"])[0, 0]
-
-    residual = assemble(x_pieces).astype(f32)
+
+    residual = assemble(x_groups, order).astype(f32)
     normal1, inverse1, normed1 = norm_forward(residual, gain1, shift1)
-    keyval = dot_nn(normed1, keyval_w)
+    keyval = dot_nn(normed1[:, :split], keyval_near) + dot_nn(normed1[:, split:], keyval_far)
     keyval = jnp.concatenate(
         [keyval[:, :HEAD].astype(bf16), (keyval[:, HEAD:] + b_value).astype(bf16)], 1
     )
-    keyval_pieces = gather_pieces(keyval, all_in)
-    keyval_all = jnp.concatenate(
-        [keyval_pieces[(i, j)] for i in range(count_row) for j in range(count_col)], 0
-    )
+    keyval_far_rows = grow([keyval], "col", col_far)
+    keyval_all = jnp.concatenate(keyval_far_rows, 0)
+    keyval_all = jnp.concatenate(grow([keyval_all], "row", row_masks), 0)
+    keyval_all = jnp.concatenate([keyval_all, send(keyval_all, "col", near)], 0)
+    attn_cols = grow([after(w_attn_out, keyval_far_rows[-1])], "col", col_far)
+    fc_in_rows = grow([after(w_fc_in, attn_cols[-1])], "col", col_far)
     keys, values = keyval_all[:, :HEAD], keyval_all[:, HEAD:]
-    queries = (dot_nn(normed1, query_w) + bias_q).astype(bf16)
+    queries = jnp.concatenate(
+        [
+            dot_nn(normed1[:, :split], query_near[i * split : (i + 1) * split])
+            + dot_nn(normed1[:, split:], query_far[i * split : (i + 1) * split])
+            for i in range(count_row)
+        ],
+        1,
+    )
+    queries = (queries + bias_q).astype(bf16)
+    attn_near = jnp.concatenate(
+        grow([after(jnp.concatenate(attn_cols, 1), queries)], "row", row_masks), 0
+    )
+    attn_far = send(attn_near, "col", near)
+    fc_out_cols = grow([after(w_fc_out, queries)], "col", col_far)
     attended, log_totals = attend_forward(queries, keys, values, limits, slots, chunk)
-    middle = residual + (dot_nn(attended, attn_w) + bias_o)
+    middle = residual + (
+        jnp.concatenate([dot_nn(attended, attn_near), dot_nn(attended, attn_far)], 1) + bias_o
+    )
     normal2, inverse2, normed2 = norm_forward(middle, gain2, shift2)
     own = normed2.shape[0]
+    fc_in_near = jnp.concatenate(fc_in_rows[:-1] + [after(fc_in_rows[-1], attended)], 0)
+    fc_in_far = send(fc_in_near, "col", near)
+    fc_out_near = jnp.concatenate(fc_out_cols, 1)
+    fc_out_far = send(fc_out_near, "col", near)
+
+    def col_product(x, first, second):
+        return dot_nn(x[:, :split], first) + dot_nn(x[:, split:], second)
+
+    def col_product_back(x, first, second):
+        return dot_nt(x[:, :split], first) + dot_nt(x[:, split:], second)
 
     def row_gather(x):
-        pieces = gather_pieces(x, row_in)
-        return jnp.concatenate([pieces[(i, 0)] for i in range(count_row)], 0)
+        return jnp.concatenate(grow([x], "row", row_masks), 0)
 
     def row_sum(x):
-        pieces = {(i, 0): x[i * own : (i + 1) * own] for i in range(count_row)}
-        return reduce_pieces(pieces, row_out, bf16)
+        for mask in row_masks[::-1]:
+            half = x.shape[0] // 2
+            x = x[:half] + send(x[half:].astype(bf16), "row", mask).astype(f32)
+        return x
 
     normed2_all = row_gather(normed2)
-    pre_act = dot_nn(normed2_all, fc_in_w) + b_fc_in
+    pre_act = col_product(normed2_all, fc_in_near, fc_in_far) + b_fc_in
     act = gelu_tanh(pre_act).astype(bf16)
-    layer_output = middle + (row_sum(dot_nn(act, fc_out_w)) + bias_out)
+    fc_out_parts = jnp.concatenate([dot_nn(act, fc_out_near), dot_nn(act, fc_out_far)], 1)
+    layer_output = middle + (row_sum(fc_out_parts) + bias_out)
+    valid_count = jnp.full((8, 128), valid_length.astype(f32))
+    valid_count = everywhere(after(valid_count, attended), ["dp"])[0, 0]
+    late_groups = [
+        to_tokens(block, chunk, [attended, normed2_all, act])
+        for block in (teacher, out_cotangent)
+    ]
+    target = assemble(late_groups[0], order)
+    cotangent = assemble(late_groups[1], order)
     errors = layer_output - target.astype(f32)
     loss_part = jnp.sum(valid_own * errors * errors)
     ratio = rows_a * count_row * count_dp / valid_count
     grad_out = cotangent.astype(f32) + ratio * valid_own * errors
-    output_block = from_tokens(layer_output, chunk, width, rows_a)
     grad_mlp = grad_out.astype(bf16)
     grad_fc_out_bias = jnp.sum(grad_mlp, 0, dtype=f32)
     grad_mlp_all = row_gather(grad_mlp)
+    output_block = from_tokens(after(layer_output, grad_mlp_all), chunk, width, order)
 
     parts = 2
     hidden = act.shape[1] // parts
-    fc_out_grads = []
-    for f in range(parts):
-        pieces = {
-            (0, j): dot_tn(
-                act[:, f * hidden : (f + 1) * hidden],
-                grad_mlp_all[:, j * width : (j + 1) * width],
-            )
-            for j in range(count_col)
-        }
-        fc_out_grads.append(over_dp(reduce_pieces(pieces, col_out, bf16), bf16))
-    grad_fc_out = jnp.concatenate(fc_out_grads, 0)
-
-    grad_pre = (dot_nt(grad_mlp_all, fc_out_w) * gelu_slope(pre_act)).astype(bf16)
+    spans = [slice(f * hidden, (f + 1) * hidden) for f in range(parts)]
+    out_folds = [Fold(act[:, span], grad_mlp_all) for span in spans]
+    sent = []
+    for mask in [near] + col_far[::-1]:
+        for fold in out_folds:
+            sent = [fold.step(1, "col", mask, *sent)]
+    grad_pre = (
+        col_product_back(after(grad_mlp_all, *sent), fc_out_near, fc_out_far)
+        * gelu_slope(pre_act)
+    ).astype(bf16)
     grad_fc_in_bias = jnp.sum(grad_pre, 0, dtype=f32)
-    grad_normed2 = row_sum(dot_nt(grad_pre, fc_in_w))
-    fc_in_grads = []
-    for f in range(parts):
-        pieces = {
-            (0, j): dot_tn(
-                normed2_all[:, j * width : (j + 1) * width],
-                grad_pre[:, f * hidden : (f + 1) * hidden],
-            )
-            for j in range(count_col)
-        }
-        fc_in_grads.append(over_dp(reduce_pieces(pieces, col_out, bf16), bf16))
-    grad_fc_in = jnp.concatenate(fc_in_grads, 1)
+    homes = [fold.home(1) for fold in out_folds]
+    total_0 = homes[0] + out_folds[0].arrived[-1].astype(f32)
+    low_0 = total_0.astype(bf16)
+    grad_pre = after(grad_pre, low_0, homes[1])
+    normed2_grads = jnp.concatenate([dot_nt(grad_pre, fc_in_near), dot_nt(grad_pre, fc_in_far)], 1)
+    leaving = normed2_grads[own * count_row // 2 :].astype(bf16)
+    arrived = send(leaving, "row", row_masks[-1])
+    in_folds = [Fold(normed2_all, grad_pre[:, span]) for span in spans]
+    sent = [in_folds[0].step(0, "col", near, leaving)]
+    total_1 = homes[1] + after(out_folds[1].arrived[-1], *sent).astype(f32)
+    low_1 = total_1.astype(bf16)
+    sent = [in_folds[1].step(0, "col", near, low_1)]
+    for mask in col_far[::-1]:
+        for fold in in_folds:
+            sent = [fold.step(0, "col", mask, *sent)]
+    homes_in = [fold.home(1) for fold in in_folds]
+    grad_normed2 = normed2_grads[: own * count_row // 2] + after(
+        arrived, *sent, *homes_in
+    ).astype(f32)
+    for mask in row_masks[:-1][::-1]:
+        half = grad_normed2.shape[0] // 2
+        grad_normed2 = grad_normed2[:half] + send(
+            grad_normed2[half:].astype(bf16), "row", mask
+        ).astype(f32)
 
     gain2_part = jnp.sum(grad_normed2 * normal2, 0)
     shift2_part = jnp.sum(grad_normed2, 0)
     grad_middle = grad_out + norm_backward(grad_normed2, normal2, inverse2, gain2)
     grad_attn = grad_middle.astype(bf16)
     grad_attn_bias = jnp.sum(grad_attn, 0, dtype=f32)
-    pieces = {
-        (i, j): dot_tn(
-            attended[:, i * wide : (i + 1) * wide], grad_attn[:, j * width : (j + 1) * width]
-        )
-        for i in range(count_row)
-        for j in range(count_col)
-    }
-    grad_attn_out = over_dp(reduce_pieces(pieces, all_out, bf16), bf16)
-    grad_attended = dot_nt(grad_attn, attn_w).astype(bf16)
+    low_2 = (homes_in[0] + in_folds[0].arrived[-1].astype(f32)).astype(bf16)
+    sum_0, sum_1 = lax.psum((low_0, low_1), "dp")
+
+    attn_fold = Fold(attended, after(grad_attn, low_2))
+    sent = attn_fold.step(1, "col", near)
+    grad_attended = col_product_back(after(grad_attn, sent), attn_near, attn_far).astype(bf16)
+    for mask in row_masks[::-1]:
+        sent = attn_fold.step(0, "row", mask, sent)
 
     heads = queries.shape[1] // HEAD
     delta = jnp.sum(
         (attended.astype(f32) * grad_attended.astype(f32)).reshape(own, heads, HEAD), -1
     ).T
     grad_queries, grad_keys, grad_values = attend_backward(
-        queries, grad_attended, keys, values, limits, slots, log_totals, delta, chunk
+        queries,
+        after(grad_attended, low_2),
+        keys,
+        values,
+        limits,
+        slots,
+        log_totals,
+        delta,
+        chunk,
     )
     grad_keyval = jnp.concatenate([grad_keys, grad_values], 1)
-    pieces = {
-        (i, j): grad_keyval[(i * count_col + j) * own : (i * count_col + j + 1) * own]
-        for i in range(count_row)
-        for j in range(count_col)
-    }
-    grad_keyval_low = reduce_pieces(pieces, all_out, f32).astype(bf16)
+    low_3 = homes_in[1] + after(in_folds[1].arrived[-1], grad_queries).astype(f32)
+    low_3 = low_3.astype(bf16)
+    low_2, low_3 = lax.optimization_barrier((low_2, low_3, sum_0, sum_1))[:2]
+    sum_2, sum_3 = lax.psum((low_2, low_3), "dp")
+    grad_keyval_low = halve_sum(grad_keyval, all_out).astype(bf16)
+
+    query_fold = Fold(normed1, grad_queries)
+    sent = query_fold.step(0, "col", near)
+    for mask in col_far[::-1]:
+        sent_attn = attn_fold.step(1, "col", mask, sent)
+    query_grads = jnp.concatenate([
+        sum(
+            dot_nt(
+                after(grad_queries, sent, sent_attn)[:, i * wide : (i + 1) * wide],
+                weights[i * split : (i + 1) * split],
+            )
+            for i in range(count_row)
+        )
+        for weights in (query_near, query_far)
+    ], 1)
+    for mask in row_masks[::-1]:
+        sent = query_fold.step(1, "row", mask, sent)
+    total_4 = attn_fold.home()
+    in_4 = inward(total_4.astype(bf16), bf16)
     grad_value_bias = jnp.sum(grad_keyval_low[:, HEAD:], 0, dtype=f32)
     grad_query_bias = jnp.sum(grad_queries, 0, dtype=f32)
-    pieces = {
-        (i, j): dot_tn(
-            normed1[:, j * width : (j + 1) * width], grad_queries[:, i * wide : (i + 1) * wide]
-        )
-        for i in range(count_row)
-        for j in range(count_col)
-    }
-    grad_query_w = over_dp(reduce_pieces(pieces, all_out, bf16), bf16)
-    pieces = {
-        (0, j): dot_tn(normed1[:, j * width : (j + 1) * width], grad_keyval_low)
-        for j in range(count_col)
-    }
-    grad_keyval_w = everywhere(reduce_pieces(pieces, col_out, f32), ["row", "dp"])
-    grad_normed1 = dot_nt(grad_queries, query_w) + dot_nt(grad_keyval_low, keyval_w)
+    for mask in col_far[::-1]:
+        sent = query_fold.step(0, "col", mask, sent)
+
+    grad_keyval_w = everywhere(
+        halve_sum(dot_tn(normed1, grad_keyval_low), [step for step in all_out if step[0] == "col"]),
+        ["row", "dp"],
+    )
+    grad_normed1 = query_grads + jnp.concatenate(
+        [dot_nt(grad_keyval_low, keyval_near), dot_nt(grad_keyval_low, keyval_far)], 1
+    )
     gain1_part = jnp.sum(grad_normed1 * normal1, 0)
     shift1_part = jnp.sum(grad_normed1, 0)
     input_grad = grad_middle + norm_backward(grad_normed1, normal1, inverse1, gain1)
-    input_block = from_tokens(input_grad, chunk, width, rows_a)
-
-    def feature_sums(parts_list):
-        stacked = jnp.stack(parts_list)
-        pieces = {(0, j): stacked[:, j * width : (j + 1) * width] for j in range(count_col)}
-        return everywhere(reduce_pieces(pieces, col_out, f32), ["row", "dp"])
-
-    early = feature_sums([gain2_part, shift2_part, grad_fc_out_bias, grad_attn_bias])
-    late = feature_sums([gain1_part, shift1_part])
-    loss_sum = everywhere(jnp.full((8, 128), loss_part), ["row", "col", "dp"])[0, 0]
-    fc_in_bias_sum = everywhere(grad_fc_in_bias[None, :], ["col", "dp"])[0]
-    pieces = {(i, 0): grad_query_bias[None, i * wide : (i + 1) * wide] for i in range(count_row)}
-    query_bias_sum = everywhere(reduce_pieces(pieces, row_out, f32), ["col", "dp"])[0]
-    value_bias_sum = everywhere(grad_value_bias[None, :], ["row", "col", "dp"])[0]
+    input_block = from_tokens(input_grad, chunk, width, order)
+
+    held_4, mid_4 = across_middle(total_4, in_4, bf16)
+    total_5 = query_fold.home()
+    in_5 = inward(total_5.astype(bf16), bf16)
+    grad_attn_out = outward(held_4, mid_4, bf16)
+    held_5, mid_5 = across_middle(total_5, in_5, bf16)
+    grad_query_w = outward(held_5, mid_5, bf16)
+    grad_fc_out = jnp.concatenate([sum_0, sum_1], 0).astype(f32)
+    grad_fc_in = jnp.concatenate([sum_2, sum_3], 1).astype(f32)
+
+    unit = min(width, wide)
+    per = width // unit
+    feature_rows = jnp.stack(
+        [gain1_part, shift1_part, gain2_part, shift2_part, grad_fc_out_bias, grad_attn_bias]
+    )
+    tail = jnp.concatenate([grad_value_bias, loss_part[None], jnp.zeros((unit - HEAD - 1,), f32)])
+    shared = jnp.concatenate([tail, grad_query_bias, grad_fc_in_bias]).reshape(-1, unit)
+    features = feature_rows.reshape(6, count_col, per, unit).transpose(1, 0, 2, 3)
+    features = features.reshape(-1, unit)
+    for mask in masks_of("col")[::-1]:
+        half = features.shape[0] // 2
+        came = send(jnp.concatenate([features[half:], shared], 0), "col", mask)
+        features = features[:half] + came[:half]
+        shared = shared + came[half:]
+    ahead, each = 6 * per + 1, wide // unit
+    pack = jnp.concatenate([features, shared], 0)
+    query_sum = halve_sum(
+        pack[ahead : ahead + count_row * each], [("row", mask) for mask in row_masks[::-1]]
+    )
+    hidden_rows = pack[ahead + count_row * each :]
+    pack = jnp.concatenate([everywhere(pack[:ahead], ["row"]), query_sum, hidden_rows], 0)
+    pack = everywhere(pack, ["dp"])
+    vector_sums = [pack[k * per : (k + 1) * per].reshape(-1) for k in range(6)]
+    value_bias_sum = pack[6 * per, :HEAD]
+    loss_sum = pack[6 * per, HEAD]
+    query_bias_sum = pack[ahead : ahead + each].reshape(-1)
+    fc_in_bias_sum = pack[ahead + each :].reshape(-1)
     return (
         output_block,
         loss_sum / (valid_count * D),
         input_block,
-        late[0],
-        late[1],
+        vector_sums[0],
+        vector_sums[1],
         grad_query_w,
         query_bias_sum,
         grad_keyval_w,
         value_bias_sum,
         grad_attn_out,
-        early[3],
-        early[0],
-        early[1],
+        vector_sums[5],
+        vector_sums[2],
+        vector_sums[3],
         grad_fc_in,
         fc_in_bias_sum,
         grad_fc_out,
-        early[2],
+        vector_sums[4],
     )
 
 

time: 1760 us -> 1300 us (0.74)
  waiting for transfers between devices: 987 us -> 589 us
  starting transfers between devices: 156 us -> 77.6 us
    ppermute x30 -> x6, waiting for transfers between devices: 345 us -> 46.7 us  [the longest x2 25.3 us: outward(): end = lax.ppermute(final, 'dp', [(1, 0), (2, 3)])]
    ppermute x28 -> x7, waiting for transfers between devices: 203 us -> 19.8 us  [send_pair(): return lax.ppermute(x, ('row', 'col'), pairs)]
    psum x0 -> x2, waiting for transfers between devices: none -> 66.2 us  [the longest x1 60.5 us: per_device(): sum_0, sum_1 = lax.psum((low_0, low_1), 'dp')]
    convert_element_type x8 -> x16, other arithmetic: 4.45 us -> 47.6 us  [the longest x1 6.97 us: per_device(): grad_fc_out = jnp.concatenate([sum_0, sum_1], 0).astype(f32)]
    ppermute x30 -> x6, starting transfers between devices: 47.9 us -> 10.3 us  [the longest x2 6.22 us: inward(): return lax.ppermute(total.astype(wire), 'dp', [(0, 1), (3, 2)])]
    ppermute x110 -> x65, starting transfers between devices: 85.9 us -> 60.3 us  [send(): return lax.ppermute(x, axis, [(i, i ^ mask) for i in range(size)])]
    dot_general x36 -> x21, matrix products: 127 us -> 107 us  [dot_tn(): return lax.dot_general(a, b, TN, preferred_element_type=f32)]
    ppermute x110 -> x65, waiting for transfers between devices: 440 us -> 456 us  [send(): return lax.ppermute(x, axis, [(i, i ^ mask) for i in range(size)])]
  transfers between devices with their start and end apart: 168 -> 80, of which waited for: 67 -> 36; matrix products, arithmetic and copies ran while one was open for 25% -> 33% of each run, Pallas kernels for 6% -> 3%
where the time goes in v2:
time: 1300 us; the launch traced here: 1290 us
  waiting for transfers between devices  589 us (45%)
  matrix products  273 us (21%)
  other arithmetic  159 us (12%)
  Pallas kernels  105 us (8%)
  starting transfers between devices  77.6 us (6%)
  local copies, waits for them, and re-layouts  68.6 us (5%)
  between operations  20.4 us (2%)
    ppermute x65, waiting for transfers between devices, send(): return lax.ppermute(x, axis, [(i, i ^ mask) for i in range(size)])  456 us
    dot_general x21, matrix products, dot_tn(): return lax.dot_general(a, b, TN, preferred_element_type=f32)  107 us
    dot_general x12, matrix products, dot_nt(): return lax.dot_general(a, b, NT, preferred_element_type=f32)  85.3 us
    dot_general x12, matrix products, dot_nn(): return lax.dot_general(a, b, NN, preferred_element_type=f32)  81.1 us
    pallas_call x1, Pallas kernels, attend_backward(): pl.pallas_call(functools.partial(bwd_kernel, heads=heads, tq=tq, chunk=ch...  62.6 us
    psum x1, waiting for transfers between devices, per_device(): sum_0, sum_1 = lax.psum((low_0, low_1), 'dp')  60.5 us
    ppermute x65, starting transfers between devices, send(): return lax.ppermute(x, axis, [(i, i ^ mask) for i in range(size)])  60.3 us
    pallas_call x1, Pallas kernels, attend_forward(): pl.pallas_call(functools.partial(fwd_kernel, heads=heads, tq=tq, chunk=ch...  42.6 us
  transfers between devices with their start and end apart: 80, of which 36 were waited for; matrix products, arithmetic and copies ran while one was open for 33% of the time, Pallas kernels for 3%

profile of v2, /device:TPU:0, one launch (start us, length us, event | category | flops | bytes accessed | tf_op | source)
XLA Modules:
  0.0 1292.6 jit_solution(1834313653475135837)
XLA Ops:
  11.8 21.9 %collective-permute-done.9 = bf16[512,1024]{1,0:T(8,128)(2,1)S(1)} collective-permute-done((bf16[512,1024]{1,0:T(8,128)(2,1)}, bf16[512,1024]{1,0:T(8,128)(2,1)S(1)}, u32[]{:S(2)}, u32[]{:S(2)}) %collective-permute-start.9) | collective-permute-done | bytes 1048608 | tf_op jit(solution)/shard_map/ppermute | solution.py:195
  42.2 15.9 %collective-permute-done.11 = bf16[512,1024]{1,0:T(8,128)(2,1)S(1)} collective-permute-done((bf16[512,1024]{1,0:T(8,128)(2,1)S(1)}, bf16[512,1024]{1,0:T(8,128)(2,1)S(1)}, u32[]{:S(2)}, u32[]{:S(2)}) %collective-permute-start.11) | collective-permute-done | bytes 1048608 | tf_op jit(solution)/shard_map/ppermute | solution.py:195
  58.1 8.9 pad_maximum_fusion.4
  92.7 15.0 %convert_reduce_fusion.2 = (f32[512]{0:T(512)S(1)}, f32[512]{0:T(512)S(1)}, bf16[512,2048]{1,0:T(8,128)(2,1)S(1)}) fusion(bf16[256,512]{1,0:T(8,128)(2,1)S(1)} %collective-permute-done.6, bf16[256,512]{1,0:T(8,128)(2,1)S(1)} %collective-permute-done.5, bf16[256,512]{1,0:T(8,128)(2,1)S(1)} %collective-permute-done.4, ...), kind=kLoop, calls=%fused_computation.17 | loop fusion | flops 20970496 | bytes 4198400 | tf_op jit(solution)/shard_map/reduce_sum | solution.py:287
  110.5 8.5 collective-permute-done.16
  127.1 17.2 %collective-permute-done.19 = bf16[1024,512]{1,0:T(8,128)(2,1)} collective-permute-done((bf16[1024,512]{1,0:T(8,128)(2,1)}, bf16[1024,512]{1,0:T(8,128)(2,1)}, u32[]{:S(2)}, u32[]{:S(2)}) %collective-permute-start.19) | collective-permute-done | bytes 1048608 | tf_op jit(solution)/shard_map/ppermute | solution.py:195
  174.1 31.3 %collective-permute-done.20 = bf16[1024,1024]{1,0:T(8,128)(2,1)S(1)} collective-permute-done((bf16[1024,1024]{1,0:T(8,128)(2,1)}, bf16[1024,1024]{1,0:T(8,128)(2,1)S(1)}, u32[]{:S(2)}, u32[]{:S(2)}) %collective-permute-start.20) | collective-permute-done | bytes 2097184 | tf_op jit(solution)/shard_map/ppermute | solution.py:195
  207.1 42.6 %attend_forward.1 = (bf16[512,2048]{1,0:T(8,128)(2,1)S(1)}, f32[16,512]{1,0:T(8,128)S(1)}) custom-call(s32[4]{0:T(128)S(1)} %get-tuple-element.242.full_ref, s32[4]{0:T(128)S(1)} %get-tuple-element.241.count_ref, s32[16]{0:T(128)S(1)} %xor_add_fusion.slot_ref, bf16[512,2048]{1,0:T(8,128)(2,1)} %fusion.28.q_ref, ...), custom_call_target="tpu_custom_call" | custom-call | tf_op jit(solution)/shard_map/attend_forward/pallas_call | solution.py:147
  281.0 68.9 %collective-permute-done.25 = bf16[4096,512]{1,0:T(8,128)(2,1)} collective-permute-done((bf16[4096,512]{1,0:T(8,128)(2,1)}, bf16[4096,512]{1,0:T(8,128)(2,1)}, u32[]{:S(2)}, u32[]{:S(2)}) %collective-permute-start.25) | collective-permute-done | bytes 4194336 | tf_op jit(solution)/shard_map/ppermute | solution.py:195
  363.5 14.4 %fusion.50 = f32[1024,4096]{1,0:T(8,128)} fusion(bf16[1024,4096]{1,0:T(8,128)(2,1)} %collective-permute-done.24, bf16[512,2048]{1,0:T(8,128)(2,1)S(1)} %add_convert_fusion.11, bf16[512,2048]{1,0:T(8,128)(2,1)S(1)} %collective-permute-done.22), kind=kOutput, calls=%fused_computation.109 | convolution fusion | flops 8594128896 | bytes 29360128 | tf_op jit(solution)/shard_map/dot_general | solution.py:304
  377.9 24.3 %fusion.4 = (bf16[1024,4096]{1,0:T(8,128)(2,1)}, f32[1024,4096]{1,0:T(8,128)}) fusion(f32[4096]{0:T(1024)S(1)} %copy-done.117, f32[1024,4096]{1,0:T(8,128)} %fusion.50, bf16[1024,4096]{1,0:T(8,128)(2,1)} %constant_dynamic-update-slice_fusion.8, bf16[512,2048]{1,0:T(8,128)(2,1)S(1)} %add_convert_fusion.11, bf16[512,2048]{1,0:T(8,128)(2,1)} %copy-done.81), kind=kOutput, calls=%fused_computation.5 | convolution fusion | flops 8640266240 | bytes 54542336 | tf_op jit(solution)/shard_map/dot_general | solution.py:304
  402.2 12.7 fusion.153
  417.9 11.4 fusion.154
  449.2 29.3 %collective-permute-done.27 = bf16[512,2048]{1,0:T(8,128)(2,1)} collective-permute-done((bf16[512,2048]{1,0:T(8,128)(2,1)}, bf16[512,2048]{1,0:T(8,128)(2,1)}, u32[]{:S(2)}, u32[]{:S(2)}) %collective-permute-start.27) | collective-permute-done | bytes 2097184 | tf_op jit(solution)/shard_map/ppermute | solution.py:195
  478.6 18.1 %convert_reduce_fusion.5 = (f32[2048]{0:T(1024)}, bf16[512,2048]{1,0:T(8,128)(2,1)S(1)}, f32[512,2048]{1,0:T(8,128)}, f32[512,2048]{1,0:T(8,128)}) fusion(bf16[256,512]{1,0:T(8,128)(2,1)S(1)} %get-tuple-element.192, bf16[256,512]{1,0:T(8,128)(2,1)S(1)} %get-tuple-element.193, bf16[256,512]{1,0:T(8,128)(2,1)S(1)} %get-tuple-element.209, ...), kind=kLoop, calls=%fused_computation.67 | loop fusion | flops 45086720 | bytes 29378560 | tf_op jit(solution)/shard_map/reduce_sum | solution.py:597
  500.9 41.5 %collective-permute-done.36 = bf16[512,2048]{1,0:T(8,128)(2,1)S(1)} collective-permute-done((bf16[512,2048]{1,0:T(8,128)(2,1)S(1)}, bf16[512,2048]{1,0:T(8,128)(2,1)S(1)}, u32[]{:S(2)}, u32[]{:S(2)}) %collective-permute-start.36) | collective-permute-done | bytes 2097184 | tf_op jit(solution)/shard_map/ppermute | solution.py:195
  581.5 14.7 %fusion.55 = f32[1024,4096]{1,0:T(8,128)} fusion(bf16[4096,1024]{1,0:T(8,128)(2,1)} %collective-permute-done.26, bf16[1024,2048]{1,0:T(8,128)(2,1)S(1)} %pad_maximum_fusion), kind=kOutput, calls=%fused_computation.128 | convolution fusion | flops 8589934592 | bytes 27262976 | tf_op jit(solution)/shard_map/dot_general | solution.py:308
  596.1 26.6 %convert_reduce_fusion = (f32[4096]{0:T(1024)}, bf16[1024,4096]{1,0:T(8,128)(2,1)}) fusion(f32[1024,4096]{1,0:T(8,128)} %get-tuple-element.234, f32[1024,4096]{1,0:T(8,128)} %fusion.55, bf16[4096,1024]{1,0:T(8,128)(2,1)} %constant_dynamic-update-slice_fusion.10, bf16[1024,2048]{1,0:T(8,128)(2,1)} %copy-done.52), kind=kOutput, calls=%fused_computation.6 | convolution fusion | flops 8678010880 | bytes 52445184 | tf_op jit(solution)/shard_map/dot_general | solution.py:308
  628.7 11.5 fusion.155
  640.2 12.8 fusion.156
  704.4 19.0 %collective-permute-done.43 = bf16[512,2048]{1,0:T(8,128)(2,1)} collective-permute-done((bf16[512,2048]{1,0:T(8,128)(2,1)S(1)}, bf16[512,2048]{1,0:T(8,128)(2,1)}, u32[]{:S(2)}, u32[]{:S(2)}) %collective-permute-start.43) | collective-permute-done | bytes 2097184 | tf_op jit(solution)/shard_map/ppermute | solution.py:195
  758.8 62.6 %attend_backward.1 = (bf16[512,2048]{1,0:T(8,128)(2,1)S(1)}, f32[4096,128]{1,0:T(8,128)}, f32[4096,128]{1,0:T(8,128)}) custom-call(s32[4]{0:T(128)S(1)} %copy-done.16, s32[4]{0:T(128)S(1)} %copy-done.14, s32[16]{0:T(128)S(1)} %copy-done.18, bf16[512,2048]{1,0:T(8,128)(2,1)} %fusion.28.q_ref, bf16[512,2048]{1,0:T(8,128)(2,1)} %copy-done.49, ...), custom_call_target="tpu_custom_call" | custom-call | tf_op jit(solution)/shard_map/attend_backward/pallas_call | solution.py:176
  847.3 13.0 %collective-permute-done.38 = bf16[1024,512]{1,0:T(8,128)(2,1)S(1)} collective-permute-done((bf16[1024,512]{1,0:T(8,128)(2,1)S(1)}, bf16[1024,512]{1,0:T(8,128)(2,1)S(1)}, u32[]{:S(2)}, u32[]{:S(2)}) %collective-permute-start.38) | collective-permute-done | bytes 1048608 | tf_op jit(solution)/shard_map/ppermute | solution.py:195
  883.5 10.1 collective-permute-done.39
  897.5 27.0 %collective-permute-done.52 = f32[512,256]{1,0:T(8,128)S(1)} collective-permute-done((f32[512,256]{1,0:T(8,128)S(1)}, f32[512,256]{1,0:T(8,128)S(1)}, u32[]{:S(2)}, u32[]{:S(2)}) %collective-permute-start.52) | collective-permute-done | bytes 524320 | tf_op jit(solution)/shard_map/ppermute | solution.py:195
  926.8 60.5 %all-reduce.7.cloned.1.call-done = (bf16[2048,512]{1,0:T(8,128)(2,1)}, bf16[2048,512]{1,0:T(8,128)(2,1)}) async-done(((bf16[2048,512]{1,0:T(8,128)(2,1)}, bf16[2048,512]{1,0:T(8,128)(2,1)}), (bf16[2048,512]{1,0:T(8,128)(2,1)}, bf16[2048,512]{1,0:T(8,128)(2,1)})) %all-reduce.7.cloned.1.call-update) | async-done | bytes 4194320 | tf_op jit(solution)/shard_map/psum | solution.py:645
  1025.2 77.1 %collective-permute-done.70 = f32[512,256]{1,0:T(8,128)S(1)} collective-permute-done((f32[512,256]{1,0:T(8,128)S(1)}, f32[512,256]{1,0:T(8,128)S(1)}, u32[]{:S(2)}, u32[]{:S(2)}) %collective-permute-start.70) | collective-permute-done | bytes 524320 | tf_op jit(solution)/shard_map/ppermute | solution.py:195
  1135.0 20.5 %collective-permute-done.54 = f32[19,512]{1,0:T(8,128)S(1)} collective-permute-done((f32[19,512]{1,0:T(8,128)S(1)}, f32[19,512]{1,0:T(8,128)S(1)}, u32[]{:S(2)}, u32[]{:S(2)}) %collective-permute-start.54) | collective-permute-done | bytes 38944 | tf_op jit(solution)/shard_map/ppermute | solution.py:195
  1207.4 18.8 %collective-permute-done.65 = bf16[512,1024]{1,0:T(8,128)(2,1)S(1)} collective-permute-done((bf16[512,1024]{1,0:T(8,128)(2,1)}, bf16[512,1024]{1,0:T(8,128)(2,1)S(1)}, u32[]{:S(2)}, u32[]{:S(2)}) %collective-permute-start.65) | collective-permute-done | bytes 1048608 | tf_op jit(solution)/shard_map/ppermute | solution.py:441
  1239.8 13.8 %collective-permute-done.61 = bf16[1024,512]{1,0:T(8,128)(2,1)S(1)} collective-permute-done((bf16[1024,512]{1,0:T(8,128)(2,1)S(1)}, bf16[1024,512]{1,0:T(8,128)(2,1)S(1)}, u32[]{:S(2)}, u32[]{:S(2)}) %collective-permute-start.61) | collective-permute-done | bytes 1048608 | tf_op jit(solution)/shard_map/ppermute | solution.py:195
  1256.2 8.5 collective-permute-done.76
  1266.2 16.7 %collective-permute-done.67 = bf16[512,1024]{1,0:T(8,128)(2,1)S(1)} collective-permute-done((bf16[512,1024]{1,0:T(8,128)(2,1)S(1)}, bf16[512,1024]{1,0:T(8,128)(2,1)S(1)}, u32[]{:S(2)}, u32[]{:S(2)}) %collective-permute-start.67) | collective-permute-done | bytes 1048608 | tf_op jit(solution)/shard_map/ppermute | solution.py:456
  (590 shorter events, 477.1 us)
Async XLA Ops:
  7.2 980.1 %all-reduce.7.cloned.1.call-start = ((), (), s32[]{:S(2)}) async-start(), calls=%async_computation.1 | async-start | bytes 8388608 | tf_op jit(solution)/shard_map/psum | solution.py:645
  67.0 81.8 %collective-permute-start.12 = (bf16[2048,1024]{1,0:T(8,128)(2,1)}, bf16[2048,1024]{1,0:T(8,128)(2,1)}, u32[]{:S(2)}, u32[]{:S(2)}) collective-permute-start(bf16[2048,1024]{1,0:T(8,128)(2,1)} %pad_maximum_fusion.4), channel_id=1, source_target_pairs={{0,1},{1,0},{2,3},{3,2},{4,5},{5,4},{6,7},{7,6},{8,9},{9,8},{10,11... | collective-permute-start | bytes 12582920 | tf_op jit(solution)/shard_map/ppermute | solution.py:195
  144.3 105.5 %collective-permute-start.23 = (bf16[512,4096]{1,0:T(8,128)(2,1)}, bf16[512,4096]{1,0:T(8,128)(2,1)}, u32[]{:S(2)}, u32[]{:S(2)}) collective-permute-start(bf16[512,4096]{1,0:T(8,128)(2,1)} %param.30), channel_id=1, source_target_pairs={{0,2},{1,3},{2,0},{3,1},{4,6},{5,7},{6,4},{7,5},{8,10},{9,11},{10,... | collective-permute-start | bytes 12582920 | tf_op jit(solution)/shard_map/ppermute | solution.py:195
  158.9 46.5 %collective-permute-start.20 = (bf16[1024,1024]{1,0:T(8,128)(2,1)}, bf16[1024,1024]{1,0:T(8,128)(2,1)S(1)}, u32[]{:S(2)}, u32[]{:S(2)}) collective-permute-start(bf16[1024,1024]{1,0:T(8,128)(2,1)} %pad_maximum_fusion.6), channel_id=1, source_target_pairs={{0,4},{4,0},{1,5},{5,1},{2,6},{6,2},{3,7},{7,3},{8,12},{12,8},{9,1... | collective-permute-start | bytes 6291464 | tf_op jit(solution)/shard_map/ppermute | solution.py:195
  206.9 56.1 %collective-permute-start.21 = (bf16[2048,1024]{1,0:T(8,128)(2,1)}, bf16[2048,1024]{1,0:T(8,128)(2,1)}, u32[]{:S(2)}, u32[]{:S(2)}) collective-permute-start(bf16[2048,1024]{1,0:T(8,128)(2,1)} %constant_dynamic-update-slice_fusion.6), channel_id=1, source_target_pairs={{0,1},{1,0},{2,3},{3,2},{4,5},{5,4},{6,7},{7,6},{8,9},{9,8},{10,11... | collective-permute-start | bytes 12582920 | tf_op jit(solution)/shard_map/ppermute | solution.py:195
  255.2 108.3 %collective-permute-start.24 = (bf16[1024,4096]{1,0:T(8,128)(2,1)}, bf16[1024,4096]{1,0:T(8,128)(2,1)}, u32[]{:S(2)}, u32[]{:S(2)}) collective-permute-start(bf16[1024,4096]{1,0:T(8,128)(2,1)} %constant_dynamic-update-slice_fusion.8), channel_id=1, source_target_pairs={{0,1},{1,0},{2,3},{3,2},{4,5},{5,4},{6,7},{7,6},{8,9},{9,8},{10,11... | collective-permute-start | bytes 25165832 | tf_op jit(solution)/shard_map/ppermute | solution.py:195
  257.0 92.9 %collective-permute-start.25 = (bf16[4096,512]{1,0:T(8,128)(2,1)}, bf16[4096,512]{1,0:T(8,128)(2,1)}, u32[]{:S(2)}, u32[]{:S(2)}) collective-permute-start(bf16[4096,512]{1,0:T(8,128)(2,1)} %param.32), channel_id=1, source_target_pairs={{0,2},{1,3},{2,0},{3,1},{4,6},{5,7},{6,4},{7,5},{8,10},{9,11},{10,... | collective-permute-start | bytes 12582920 | tf_op jit(solution)/shard_map/ppermute | solution.py:195
  269.4 85.0 %collective-permute-start.22 = (bf16[512,2048]{1,0:T(8,128)(2,1)S(1)}, bf16[512,2048]{1,0:T(8,128)(2,1)S(1)}, u32[]{:S(2)}, u32[]{:S(2)}) collective-permute-start(bf16[512,2048]{1,0:T(8,128)(2,1)S(1)} %add_convert_fusion.11), channel_id=1, source_target_pairs={{0,4},{4,0},{1,5},{5,1},{2,6},{6,2},{3,7},{7,3},{8,12},{12,8},{9,1... | collective-permute-start | bytes 6291464 | tf_op jit(solution)/shard_map/ppermute | solution.py:195
  274.3 82.6 %collective-permute-start.28 = (bf16[1024,512]{1,0:T(8,128)(2,1)S(1)}, bf16[1024,512]{1,0:T(8,128)(2,1)S(1)}, u32[]{:S(2)}, u32[]{:S(2)}) collective-permute-start(bf16[1024,512]{1,0:T(8,128)(2,1)S(1)} %get-tuple-element.63), channel_id=1, source_target_pairs={{0,4},{4,0},{1,5},{5,1},{2,6},{6,2},{3,7},{7,3},{8,12},{12,8},{9,1... | collective-permute-start | bytes 3145736 | tf_op jit(solution)/shard_map/ppermute | solution.py:195
  279.4 82.4 %collective-permute-start.33 = (bf16[1024,512]{1,0:T(8,128)(2,1)S(1)}, bf16[1024,512]{1,0:T(8,128)(2,1)S(1)}, u32[]{:S(2)}, u32[]{:S(2)}) collective-permute-start(bf16[1024,512]{1,0:T(8,128)(2,1)S(1)} %get-tuple-element.67), channel_id=1, source_target_pairs={{0,4},{4,0},{1,5},{5,1},{2,6},{6,2},{3,7},{7,3},{8,12},{12,8},{9,1... | collective-permute-start | bytes 3145736 | tf_op jit(solution)/shard_map/ppermute | solution.py:195
  354.4 63.5 %collective-permute-start.26 = (bf16[4096,1024]{1,0:T(8,128)(2,1)}, bf16[4096,1024]{1,0:T(8,128)(2,1)}, u32[]{:S(2)}, u32[]{:S(2)}) collective-permute-start(bf16[4096,1024]{1,0:T(8,128)(2,1)} %constant_dynamic-update-slice_fusion.10), channel_id=1, source_target_pairs={{0,1},{1,0},{2,3},{3,2},{4,5},{5,4},{6,7},{7,6},{8,9},{9,8},{10,11... | collective-permute-start | bytes 25165832 | tf_op jit(solution)/shard_map/ppermute | solution.py:195
  358.1 57.7 %collective-permute-start.29 = (bf16[1024,512]{1,0:T(8,128)(2,1)}, bf16[1024,512]{1,0:T(8,128)(2,1)}, u32[]{:S(2)}, u32[]{:S(2)}) collective-permute-start(bf16[1024,512]{1,0:T(8,128)(2,1)} %pad_maximum_fusion.8), channel_id=1, source_target_pairs={{0,2},{1,3},{2,0},{3,1},{4,6},{5,7},{6,4},{7,5},{8,10},{9,11},{10,... | collective-permute-start | bytes 3145736 | tf_op jit(solution)/shard_map/ppermute | solution.py:195
  362.9 71.6 %collective-permute-start.34 = (bf16[1024,512]{1,0:T(8,128)(2,1)}, bf16[1024,512]{1,0:T(8,128)(2,1)}, u32[]{:S(2)}, u32[]{:S(2)}) collective-permute-start(bf16[1024,512]{1,0:T(8,128)(2,1)} %pad_maximum_fusion.10), channel_id=1, source_target_pairs={{0,2},{1,3},{2,0},{3,1},{4,6},{5,7},{6,4},{7,5},{8,10},{9,11},{10,... | collective-permute-start | bytes 3145736 | tf_op jit(solution)/shard_map/ppermute | solution.py:195
  432.0 46.5 %collective-permute-start.27 = (bf16[512,2048]{1,0:T(8,128)(2,1)}, bf16[512,2048]{1,0:T(8,128)(2,1)}, u32[]{:S(2)}, u32[]{:S(2)}) collective-permute-start(bf16[512,2048]{1,0:T(8,128)(2,1)} %fusion.27), channel_id=1, source_target_pairs={{0,4},{4,0},{1,5},{5,1},{2,6},{6,2},{3,7},{7,3},{8,12},{12,8},{9,1... | collective-permute-start | bytes 6291464 | tf_op jit(solution)/shard_map/ppermute | solution.py:195
  496.7 45.7 %collective-permute-start.36 = (bf16[512,2048]{1,0:T(8,128)(2,1)S(1)}, bf16[512,2048]{1,0:T(8,128)(2,1)S(1)}, u32[]{:S(2)}, u32[]{:S(2)}) collective-permute-start(bf16[512,2048]{1,0:T(8,128)(2,1)S(1)} %get-tuple-element.119), channel_id=1, source_target_pairs={{0,4},{4,0},{1,5},{5,1},{2,6},{6,2},{3,7},{7,3},{8,12},{12,8},{9,1... | collective-permute-start | bytes 6291464 | tf_op jit(solution)/shard_map/ppermute | solution.py:195
  567.9 54.8 %collective-permute-start.42 = (bf16[2048,512]{1,0:T(8,128)(2,1)}, bf16[2048,512]{1,0:T(8,128)(2,1)S(1)}, u32[]{:S(2)}, u32[]{:S(2)}) collective-permute-start(bf16[2048,512]{1,0:T(8,128)(2,1)} %add_convert_fusion.10), channel_id=1, source_target_pairs={{0,2},{1,3},{2,0},{3,1},{4,6},{5,7},{6,4},{7,5},{8,10},{9,11},{10,... | collective-permute-start | bytes 6291464 | tf_op jit(solution)/shard_map/ppermute | solution.py:195
  574.4 89.1 %collective-permute-start.44 = (bf16[2048,512]{1,0:T(8,128)(2,1)}, bf16[2048,512]{1,0:T(8,128)(2,1)}, u32[]{:S(2)}, u32[]{:S(2)}) collective-permute-start(bf16[2048,512]{1,0:T(8,128)(2,1)} %add_convert_fusion.9), channel_id=1, source_target_pairs={{0,2},{1,3},{2,0},{3,1},{4,6},{5,7},{6,4},{7,5},{8,10},{9,11},{10,... | collective-permute-start | bytes 6291464 | tf_op jit(solution)/shard_map/ppermute | solution.py:195
  675.7 47.7 %collective-permute-start.43 = (bf16[512,2048]{1,0:T(8,128)(2,1)S(1)}, bf16[512,2048]{1,0:T(8,128)(2,1)}, u32[]{:S(2)}, u32[]{:S(2)}) collective-permute-start(bf16[512,2048]{1,0:T(8,128)(2,1)S(1)} %fusion.26), channel_id=1, source_target_pairs={{0,4},{4,0},{1,5},{5,1},{2,6},{6,2},{3,7},{7,3},{8,12},{12,8},{9,1... | collective-permute-start | bytes 6291464 | tf_op jit(solution)/shard_map/ppermute | solution.py:195
  685.6 47.9 %collective-permute-start.47 = (bf16[512,2048]{1,0:T(8,128)(2,1)}, bf16[512,2048]{1,0:T(8,128)(2,1)}, u32[]{:S(2)}, u32[]{:S(2)}) collective-permute-start(bf16[512,2048]{1,0:T(8,128)(2,1)} %add_convert_fusion.6), channel_id=1, source_target_pairs={{0,2},{1,3},{2,0},{3,1},{4,6},{5,7},{6,4},{7,5},{8,10},{9,11},{10,... | collective-permute-start | bytes 6291464 | tf_op jit(solution)/shard_map/ppermute | solution.py:195
  833.5 356.4 %all-reduce.5.cloned.1.call-start = ((), (), s32[]{:S(2)}) async-start(), calls=%async_computation | async-start | bytes 8388608 | tf_op jit(solution)/shard_map/psum | solution.py:672
  836.0 158.3 %collective-permute-start.48 = (bf16[2048,1024]{1,0:T(8,128)(2,1)}, bf16[2048,1024]{1,0:T(8,128)(2,1)}, u32[]{:S(2)}, u32[]{:S(2)}) collective-permute-start(bf16[2048,1024]{1,0:T(8,128)(2,1)} %convolution_convert_fusion.1), channel_id=1, source_target_pairs={{0,1},{1,0},{2,3},{3,2},{4,5},{5,4},{6,7},{7,6},{8,9},{9,8},{10,11... | collective-permute-start | bytes 12582920 | tf_op jit(solution)/shard_map/ppermute | solution.py:195
  841.8 158.3 %collective-permute-start.62 = (bf16[1024,2048]{1,0:T(8,128)(2,1)}, bf16[1024,2048]{1,0:T(8,128)(2,1)}, u32[]{:S(2)}, u32[]{:S(2)}) collective-permute-start(bf16[1024,2048]{1,0:T(8,128)(2,1)} %convolution_convert_fusion), channel_id=1, source_target_pairs={{0,1},{1,0},{2,3},{3,2},{4,5},{5,4},{6,7},{7,6},{8,9},{9,8},{10,11... | collective-permute-start | bytes 12582920 | tf_op jit(solution)/shard_map/ppermute | solution.py:195
  866.3 128.0 %collective-permute-start.77 = (bf16[512,2048]{1,0:T(8,128)(2,1)}, bf16[512,2048]{1,0:T(8,128)(2,1)}, u32[]{:S(2)}, u32[]{:S(2)}) collective-permute-start(bf16[512,2048]{1,0:T(8,128)(2,1)} %add_convert_fusion.5), channel_id=1, source_target_pairs={{0,2},{1,3},{2,0},{3,1},{4,6},{5,7},{6,4},{7,5},{8,10},{9,11},{10,... | collective-permute-start | bytes 6291464 | tf_op jit(solution)/shard_map/ppermute | solution.py:195
  873.4 51.1 %collective-permute-start.52 = (f32[512,256]{1,0:T(8,128)S(1)}, f32[512,256]{1,0:T(8,128)S(1)}, u32[]{:S(2)}, u32[]{:S(2)}) collective-permute-start(f32[512,256]{1,0:T(8,128)S(1)} %slice.684), channel_id=1, source_target_pairs={{0,2},{1,3},{2,0},{3,1},{4,6},{5,7},{6,4},{7,5},{8,10},{9,11},{10,... | collective-permute-start | bytes 1572872 | tf_op jit(solution)/shard_map/ppermute | solution.py:195
  926.7 78.4 %collective-permute-start.68 = (f32[1024,256]{1,0:T(8,128)S(1)}, f32[1024,256]{1,0:T(8,128)}, u32[]{:S(2)}, u32[]{:S(2)}) collective-permute-start(f32[1024,256]{1,0:T(8,128)S(1)} %slice.721), channel_id=1, source_target_pairs={{0,1},{1,0},{2,3},{3,2},{4,5},{5,4},{6,7},{7,6},{8,9},{9,8},{10,11... | collective-permute-start | bytes 3145736 | tf_op jit(solution)/shard_map/ppermute | solution.py:195
  998.7 105.9 %collective-permute-start.49 = (bf16[1024,1024]{1,0:T(8,128)(2,1)}, bf16[1024,1024]{1,0:T(8,128)(2,1)}, u32[]{:S(2)}, u32[]{:S(2)}) collective-permute-start(bf16[1024,1024]{1,0:T(8,128)(2,1)} %add_convert_fusion.2), channel_id=1, source_target_pairs={{0,4},{4,0},{1,5},{5,1},{2,6},{6,2},{3,7},{7,3},{8,12},{12,8},{9,1... | collective-permute-start | bytes 6291464 | tf_op jit(solution)/shard_map/ppermute | solution.py:195
  1004.5 105.0 %collective-permute-start.63 = (bf16[1024,1024]{1,0:T(8,128)(2,1)}, bf16[1024,1024]{1,0:T(8,128)(2,1)}, u32[]{:S(2)}, u32[]{:S(2)}) collective-permute-start(bf16[1024,1024]{1,0:T(8,128)(2,1)} %add_convert_fusion.1), channel_id=1, source_target_pairs={{0,4},{4,0},{1,5},{5,1},{2,6},{6,2},{3,7},{7,3},{8,12},{12,8},{9,1... | collective-permute-start | bytes 6291464 | tf_op jit(solution)/shard_map/ppermute | solution.py:195
  1021.7 80.6 %collective-permute-start.70 = (f32[512,256]{1,0:T(8,128)S(1)}, f32[512,256]{1,0:T(8,128)S(1)}, u32[]{:S(2)}, u32[]{:S(2)}) collective-permute-start(f32[512,256]{1,0:T(8,128)S(1)} %slice_add_fusion.3), channel_id=1, source_target_pairs={{0,4},{4,0},{1,5},{5,1},{2,6},{6,2},{3,7},{7,3},{8,12},{12,8},{9,1... | collective-permute-start | bytes 1572872 | tf_op jit(solution)/shard_map/ppermute | solution.py:195
  1103.1 93.6 %collective-permute-start.71 = (f32[512,256]{1,0:T(8,128)}, f32[512,256]{1,0:T(8,128)}, u32[]{:S(2)}, u32[]{:S(2)}) collective-permute-start(f32[512,256]{1,0:T(8,128)} %add.496), channel_id=1, source_target_pairs={{0,16},{8,24},{16,0},{24,8},{1,17},{9,25},{17,1},{25,9},{2,18},{10... | collective-permute-start | bytes 1572872 | tf_op jit(solution)/shard_map/ppermute | solution.py:195
  1108.1 61.0 %collective-permute-start.73 = (bf16[1024,512]{1,0:T(8,128)(2,1)}, bf16[1024,512]{1,0:T(8,128)(2,1)}, u32[]{:S(2)}, u32[]{:S(2)}) collective-permute-start(bf16[1024,512]{1,0:T(8,128)(2,1)} %add_convert_fusion.17), channel_id=1, source_target_pairs={{0,2},{1,3},{2,0},{3,1},{4,6},{5,7},{6,4},{7,5},{8,10},{9,11},{10,... | collective-permute-start | bytes 3145736 | tf_op jit(solution)/shard_map/ppermute | solution.py:195
  1113.0 65.5 %collective-permute-start.64 = (bf16[512,1024]{1,0:T(8,128)(2,1)}, bf16[512,1024]{1,0:T(8,128)(2,1)S(1)}, u32[]{:S(2)}, u32[]{:S(2)}) collective-permute-start(bf16[512,1024]{1,0:T(8,128)(2,1)} %add_convert_fusion.16), channel_id=1, source_target_pairs={{0,2},{1,3},{2,0},{3,1},{4,6},{5,7},{6,4},{7,5},{8,10},{9,11},{10,... | collective-permute-start | bytes 3145736 | tf_op jit(solution)/shard_map/ppermute | solution.py:195
  1236.5 46.4 %collective-permute-start.67 = (bf16[512,1024]{1,0:T(8,128)(2,1)S(1)}, bf16[512,1024]{1,0:T(8,128)(2,1)S(1)}, u32[]{:S(2)}, u32[]{:S(2)}) collective-permute-start(bf16[512,1024]{1,0:T(8,128)(2,1)S(1)} %add_convert_fusion.14), channel_id=1, source_target_pairs={{8,0},{16,24},{9,1},{17,25},{10,2},{18,26},{11,3},{19,27},{12,4},{... | collective-permute-start | bytes 3145736 | tf_op jit(solution)/shard_map/ppermute | solution.py:456
  (172 other events, 3596.0 us)
Sparse Core Ops, SparseCore 0:
  833.6 153.6 all-reduce.6
  1012.6 177.2 all-reduce.4

commit v3 on v2

--- a/solution.py
+++ b/solution.py
@@ -220,16 +220,41 @@
     return parts
 
 
+def product_kernel(*refs):
+    left, right, *others, out = refs
+    made = lax.dot_general(left[...], right[...], TN, preferred_element_type=f32)
+    for other in others:
+        made = made + other[...].astype(f32)
+    out[...] = made.astype(out.dtype)
+
+
+def token_product(left, right, rows, cols, base, others, kind):
+    tokens = left.shape[0]
+    tall, broad = min(512, rows[1] - rows[0]), min(1024, cols[1] - cols[0])
+    left_at, right_at = (base[0] + rows[0]) // tall, (base[1] + cols[0]) // broad
+    row_at, col_at = rows[0] // tall, cols[0] // broad
+    return pl.pallas_call(
+        product_kernel,
+        grid=((rows[1] - rows[0]) // tall, (cols[1] - cols[0]) // broad),
+        in_specs=[
+            pl.BlockSpec((tokens, tall), lambda i, j: (0, left_at + i)),
+            pl.BlockSpec((tokens, broad), lambda i, j: (0, right_at + j)),
+        ]
+        + [pl.BlockSpec((tall, broad), lambda i, j: (row_at + i, col_at + j)) for _ in others],
+        out_specs=pl.BlockSpec((tall, broad), lambda i, j: (i, j)),
+        out_shape=jax.ShapeDtypeStruct((rows[1] - rows[0], cols[1] - cols[0]), kind),
+        name="token_product",
+        compiler_params=pltpu.CompilerParams(vmem_limit_bytes=48 << 20),
+    )(left, right, *others)
+
+
 class Fold:
-    def __init__(self, left, right):
-        self.left, self.right, self.arrived = left, right, []
-        self.limits = [left.shape[1], right.shape[1]]
-
-    def part(self, rows, cols):
-        made = dot_tn(self.left[:, rows[0] : rows[1]], self.right[:, cols[0] : cols[1]])
-        for other in self.arrived:
-            made = made + other[rows[0] : rows[1], cols[0] : cols[1]].astype(f32)
-        return made
+    def __init__(self, left, right, base=(0, 0), size=None):
+        self.left, self.right, self.base, self.arrived = left, right, base, []
+        self.limits = list(size or (left.shape[1], right.shape[1]))
+
+    def part(self, rows, cols, kind):
+        return token_product(self.left, self.right, rows, cols, self.base, self.arrived, kind)
 
     def step(self, dim, axis, mask, *needed):
         if needed:
@@ -237,16 +262,15 @@
         half = self.limits[dim] // 2
         spans = [(0, self.limits[0]), (0, self.limits[1])]
         spans[dim] = (half, self.limits[dim])
-        leaving = self.part(*spans).astype(bf16)
-        self.arrived = [lax.slice_in_dim(other, 0, half, axis=dim) for other in self.arrived]
-        self.arrived.append(send(leaving, axis, mask))
+        leaving = self.part(*spans, bf16)
+        self.arrived = self.arrived + [send(leaving, axis, mask)]
         self.limits[dim] = half
         return leaving
 
     def home(self, skip=0):
         kept = self.arrived
         self.arrived = kept[: len(kept) - skip]
-        made = self.part((0, self.limits[0]), (0, self.limits[1]))
+        made = self.part((0, self.limits[0]), (0, self.limits[1]), f32)
         self.arrived = kept
         return made
 
@@ -450,10 +474,17 @@
 
 def outward(held, arrived, wire):
     if lax.axis_size("dp") != 4:
-        return everywhere(held, ["dp"])
+        final = everywhere(held.astype(f32), ["dp"])
+        return (final, final)
     final = (held.astype(f32) + arrived.astype(f32)).astype(wire)
+    return (final, lax.ppermute(final, "dp", [(1, 0), (2, 3)]))
+
+
+def settled(pair):
+    final, end = pair
+    if lax.axis_size("dp") != 4:
+        return final
     z = lax.axis_index("dp")
-    end = lax.ppermute(final, "dp", [(1, 0), (2, 3)])
     return jnp.where((z == 1) | (z == 2), final, end).astype(f32)
 
 
@@ -499,7 +530,12 @@
     keyval_far = send(keyval_near, "col", near)
     query_parts = [
         jnp.concatenate(parts, 0)
-        for parts in zip(*[grow([part], "row", row_masks) for part in grow([w_query], "col", col_far)])
+        for parts in zip(
+            *[
+                grow([part], "row", row_masks)
+                for part in grow([after(w_query, *x_groups.values())], "col", col_far)
+            ]
+        )
     ]
     query_near = jnp.concatenate(query_parts, 0)
     query_far = send(query_near, "col", near)
@@ -545,12 +581,11 @@
         1,
     )
     queries = (queries + bias_q).astype(bf16)
-    attn_near = jnp.concatenate(
-        grow([after(jnp.concatenate(attn_cols, 1), queries)], "row", row_masks), 0
-    )
-    attn_far = send(attn_near, "col", near)
+    attn_rows = grow([after(jnp.concatenate(attn_cols, 1), queries)], "row", row_masks)
     fc_out_cols = grow([after(w_fc_out, queries)], "col", col_far)
     attended, log_totals = attend_forward(queries, keys, values, limits, slots, chunk)
+    attn_near = jnp.concatenate(attn_rows[:-1] + [after(attn_rows[-1], attended)], 0)
+    attn_far = send(attn_near, "col", near)
     middle = residual + (
         jnp.concatenate([dot_nn(attended, attn_near), dot_nn(attended, attn_far)], 1) + bias_o
     )
@@ -558,8 +593,6 @@
     own = normed2.shape[0]
     fc_in_near = jnp.concatenate(fc_in_rows[:-1] + [after(fc_in_rows[-1], attended)], 0)
     fc_in_far = send(fc_in_near, "col", near)
-    fc_out_near = jnp.concatenate(fc_out_cols, 1)
-    fc_out_far = send(fc_out_near, "col", near)
 
     def col_product(x, first, second):
         return dot_nn(x[:, :split], first) + dot_nn(x[:, split:], second)
@@ -579,12 +612,16 @@
     normed2_all = row_gather(normed2)
     pre_act = col_product(normed2_all, fc_in_near, fc_in_far) + b_fc_in
     act = gelu_tanh(pre_act).astype(bf16)
-    fc_out_parts = jnp.concatenate([dot_nn(act, fc_out_near), dot_nn(act, fc_out_far)], 1)
-    layer_output = middle + (row_sum(fc_out_parts) + bias_out)
+    fc_out_near = jnp.concatenate(fc_out_cols[:-1] + [after(fc_out_cols[-1], act)], 1)
+    fc_out_far = send(fc_out_near, "col", near)
+    fc_out_first = dot_nn(act, fc_out_near)
+    fc_out_parts = jnp.concatenate([fc_out_first, dot_nn(act, fc_out_far)], 1)
+    fc_out_sum = row_sum(fc_out_parts)
+    layer_output = middle + (fc_out_sum + bias_out)
     valid_count = jnp.full((8, 128), valid_length.astype(f32))
     valid_count = everywhere(after(valid_count, attended), ["dp"])[0, 0]
     late_groups = [
-        to_tokens(block, chunk, [attended, normed2_all, act])
+        to_tokens(block, chunk, [act, fc_out_first, fc_out_sum])
         for block in (teacher, out_cotangent)
     ]
     target = assemble(late_groups[0], order)
@@ -596,12 +633,12 @@
     grad_mlp = grad_out.astype(bf16)
     grad_fc_out_bias = jnp.sum(grad_mlp, 0, dtype=f32)
     grad_mlp_all = row_gather(grad_mlp)
-    output_block = from_tokens(after(layer_output, grad_mlp_all), chunk, width, order)
 
     parts = 2
     hidden = act.shape[1] // parts
-    spans = [slice(f * hidden, (f + 1) * hidden) for f in range(parts)]
-    out_folds = [Fold(act[:, span], grad_mlp_all) for span in spans]
+    out_folds = [
+        Fold(act, grad_mlp_all, (f * hidden, 0), (hidden, D)) for f in range(parts)
+    ]
     sent = []
     for mask in [near] + col_far[::-1]:
         for fold in out_folds:
@@ -614,15 +651,20 @@
     homes = [fold.home(1) for fold in out_folds]
     total_0 = homes[0] + out_folds[0].arrived[-1].astype(f32)
     low_0 = total_0.astype(bf16)
+    in_0 = inward(low_0, bf16)
     grad_pre = after(grad_pre, low_0, homes[1])
     normed2_grads = jnp.concatenate([dot_nt(grad_pre, fc_in_near), dot_nt(grad_pre, fc_in_far)], 1)
     leaving = normed2_grads[own * count_row // 2 :].astype(bf16)
     arrived = send(leaving, "row", row_masks[-1])
-    in_folds = [Fold(normed2_all, grad_pre[:, span]) for span in spans]
-    sent = [in_folds[0].step(0, "col", near, leaving)]
-    total_1 = homes[1] + after(out_folds[1].arrived[-1], *sent).astype(f32)
+    in_folds = [
+        Fold(normed2_all, grad_pre, (0, f * hidden), (D, hidden)) for f in range(parts)
+    ]
+    sent = in_folds[0].step(0, "col", near, leaving)
+    total_1 = homes[1] + after(out_folds[1].arrived[-1], sent).astype(f32)
     low_1 = total_1.astype(bf16)
-    sent = [in_folds[1].step(0, "col", near, low_1)]
+    in_1 = inward(low_1, bf16)
+    held_0, mid_0 = across_middle(total_0, after(in_0, sent), bf16)
+    sent = [in_folds[1].step(0, "col", near, low_1, held_0)]
     for mask in col_far[::-1]:
         for fold in in_folds:
             sent = [fold.step(0, "col", mask, *sent)]
@@ -641,10 +683,16 @@
     grad_middle = grad_out + norm_backward(grad_normed2, normal2, inverse2, gain2)
     grad_attn = grad_middle.astype(bf16)
     grad_attn_bias = jnp.sum(grad_attn, 0, dtype=f32)
-    low_2 = (homes_in[0] + in_folds[0].arrived[-1].astype(f32)).astype(bf16)
-    sum_0, sum_1 = lax.psum((low_0, low_1), "dp")
-
-    attn_fold = Fold(attended, after(grad_attn, low_2))
+    total_2 = homes_in[0] + in_folds[0].arrived[-1].astype(f32)
+    low_2 = total_2.astype(bf16)
+    in_2 = inward(low_2, bf16)
+    out_0 = outward(held_0, after(mid_0, grad_attn), bf16)
+    held_1, mid_1 = across_middle(total_1, after(in_1, grad_attn), bf16)
+    total_3 = homes_in[1] + after(in_folds[1].arrived[-1], grad_attn).astype(f32)
+    low_3 = total_3.astype(bf16)
+    in_3 = inward(low_3, bf16)
+
+    attn_fold = Fold(attended, after(grad_attn, low_2, out_0[0], held_1))
     sent = attn_fold.step(1, "col", near)
     grad_attended = col_product_back(after(grad_attn, sent), attn_near, attn_far).astype(bf16)
     for mask in row_masks[::-1]:
@@ -656,7 +704,7 @@
     ).T
     grad_queries, grad_keys, grad_values = attend_backward(
         queries,
-        after(grad_attended, low_2),
+        after(grad_attended, low_3, sent),
         keys,
         values,
         limits,
@@ -666,16 +714,14 @@
         chunk,
     )
     grad_keyval = jnp.concatenate([grad_keys, grad_values], 1)
-    low_3 = homes_in[1] + after(in_folds[1].arrived[-1], grad_queries).astype(f32)
-    low_3 = low_3.astype(bf16)
-    low_2, low_3 = lax.optimization_barrier((low_2, low_3, sum_0, sum_1))[:2]
-    sum_2, sum_3 = lax.psum((low_2, low_3), "dp")
-    grad_keyval_low = halve_sum(grad_keyval, all_out).astype(bf16)
+    out_1 = outward(held_1, after(mid_1, grad_queries), bf16)
+    held_2, mid_2 = across_middle(total_2, after(in_2, grad_queries), bf16)
+    held_3, mid_3 = across_middle(total_3, after(in_3, grad_queries), bf16)
 
     query_fold = Fold(normed1, grad_queries)
-    sent = query_fold.step(0, "col", near)
     for mask in col_far[::-1]:
-        sent_attn = attn_fold.step(1, "col", mask, sent)
+        sent_attn = attn_fold.step(1, "col", mask, grad_queries)
+    sent = query_fold.step(0, "col", near, sent_attn)
     query_grads = jnp.concatenate([
         sum(
             dot_nt(
@@ -687,13 +733,17 @@
         for weights in (query_near, query_far)
     ], 1)
     for mask in row_masks[::-1]:
-        sent = query_fold.step(1, "row", mask, sent)
+        sent = query_fold.step(1, "row", mask, sent, out_1[0], held_2)
+    grad_keyval_low = halve_sum(after(grad_keyval, sent), all_out).astype(bf16)
+    output_block = from_tokens(after(layer_output, sent), chunk, width, order)
     total_4 = attn_fold.home()
-    in_4 = inward(total_4.astype(bf16), bf16)
+    low_4 = total_4.astype(bf16)
+    in_4 = inward(low_4, bf16)
+    out_2 = outward(held_2, after(mid_2, low_4), bf16)
     grad_value_bias = jnp.sum(grad_keyval_low[:, HEAD:], 0, dtype=f32)
     grad_query_bias = jnp.sum(grad_queries, 0, dtype=f32)
     for mask in col_far[::-1]:
-        sent = query_fold.step(0, "col", mask, sent)
+        sent = query_fold.step(0, "col", mask, sent, held_3, low_4)
 
     grad_keyval_w = everywhere(
         halve_sum(dot_tn(normed1, grad_keyval_low), [step for step in all_out if step[0] == "col"]),
@@ -707,14 +757,17 @@
     input_grad = grad_middle + norm_backward(grad_normed1, normal1, inverse1, gain1)
     input_block = from_tokens(input_grad, chunk, width, order)
 
-    held_4, mid_4 = across_middle(total_4, in_4, bf16)
+    held_4, mid_4 = across_middle(total_4, after(in_4, sent), bf16)
+    out_3 = outward(held_3, after(mid_3, sent), bf16)
     total_5 = query_fold.home()
-    in_5 = inward(total_5.astype(bf16), bf16)
-    grad_attn_out = outward(held_4, mid_4, bf16)
+    in_5 = inward(after(total_5, out_3[0]).astype(bf16), bf16)
+    out_4 = outward(held_4, mid_4, bf16)
     held_5, mid_5 = across_middle(total_5, in_5, bf16)
-    grad_query_w = outward(held_5, mid_5, bf16)
-    grad_fc_out = jnp.concatenate([sum_0, sum_1], 0).astype(f32)
-    grad_fc_in = jnp.concatenate([sum_2, sum_3], 1).astype(f32)
+    out_5 = outward(held_5, mid_5, bf16)
+    grad_query_w, grad_attn_out = settled(out_5), settled(out_4)
+    out_0 = (out_0[0], after(out_0[1], grad_queries))
+    grad_fc_out = jnp.concatenate([settled(out_0), settled(out_1)], 0)
+    grad_fc_in = jnp.concatenate([settled(out_2), settled(out_3)], 1)
 
     unit = min(width, wide)
     per = width // unit

time: 1300 us -> 1220 us (0.938)
  waiting for transfers between devices: 589 us -> 416 us
  matrix products: 273 us -> 164 us
  Pallas kernels: 105 us -> 206 us
  starting transfers between devices: 77.6 us -> 150 us
  other arithmetic: 159 us -> 199 us
  between operations: 20.4 us -> 7.24 us
    dot_general x21 -> x1, matrix products: 107 us -> 0.74 us  [dot_tn(): return lax.dot_general(a, b, TN, preferred_element_type=f32)]
    ppermute x65, waiting for transfers between devices: 456 us -> 350 us  [send(): return lax.ppermute(x, axis, [(i, i ^ mask) for i in range(size)])]
    pallas_call x0 -> x20, Pallas kernels: none -> 104 us  [token_product(): pl.pallas_call(product_kernel, grid=((rows[1] - rows[0]) // tall, (cols[1...]
    psum x2 -> x0, waiting for transfers between devices: 66.2 us -> none  [the longest x1 60.5 us: per_device(): sum_0, sum_1 = lax.psum((low_0, low_1), 'dp')]
    ppermute x2 -> x6, starting transfers between devices: 6.22 us -> 50.7 us  [inward(): return lax.ppermute(total.astype(wire), 'dp', [(0, 1), (3, 2)])]
    ppermute x2 -> x6, waiting for transfers between devices: 21.4 us -> 3.6 us  [inward(): return lax.ppermute(total.astype(wire), 'dp', [(0, 1), (3, 2)])]
    ppermute x2 -> x6, waiting for transfers between devices: 25.3 us -> 43 us  [outward(): return (final, lax.ppermute(final, 'dp', [(1, 0), (2, 3)]))]
    convert_element_type x2 -> x6, other arithmetic: 0.68 us -> 18.2 us  [outward(): final = (held.astype(f32) + arrived.astype(f32)).astype(wire)]
  transfers between devices with their start and end apart: 80 -> 90, of which waited for: 36 -> 41; matrix products, arithmetic and copies ran while one was open for 33% -> 31% of each run, Pallas kernels for 3% -> 16%
where the time goes in v3:
time: 1220 us
  waiting for transfers between devices  416 us (34%)
  Pallas kernels  206 us (17%)
  other arithmetic  199 us (16%)
  matrix products  164 us (13%)
  starting transfers between devices  150 us (12%)
  local copies, waits for them, and re-layouts  76.5 us (6%)
    ppermute x65, waiting for transfers between devices, send(): return lax.ppermute(x, axis, [(i, i ^ mask) for i in range(size)])  350 us
    pallas_call x20, Pallas kernels, token_product(): pl.pallas_call(product_kernel, grid=((rows[1] - rows[0]) // tall, (cols[1...  104 us
    dot_general x12, matrix products, dot_nt(): return lax.dot_general(a, b, NT, preferred_element_type=f32)  85.9 us
    dot_general x12, matrix products, dot_nn(): return lax.dot_general(a, b, NN, preferred_element_type=f32)  77.7 us
    ppermute x65, starting transfers between devices, send(): return lax.ppermute(x, axis, [(i, i ^ mask) for i in range(size)])  72.6 us
    pallas_call x1, Pallas kernels, attend_backward(): pl.pallas_call(functools.partial(bwd_kernel, heads=heads, tq=tq, chunk=ch...  60.8 us
    ppermute x6, starting transfers between devices, inward(): return lax.ppermute(total.astype(wire), 'dp', [(0, 1), (3, 2)])  50.7 us
    ppermute x6, waiting for transfers between devices, outward(): return (final, lax.ppermute(final, 'dp', [(1, 0), (2, 3)]))  43 us
  transfers between devices with their start and end apart: 90, of which 41 were waited for; matrix products, arithmetic and copies ran while one was open for 31% of the time, Pallas kernels for 16%

profile of v3, /device:TPU:0, one launch (start us, length us, event | category | flops | bytes accessed | tf_op | source)
XLA Modules:
  0.0 1218.7 jit_solution(10264790729171406091)
XLA Ops:
  34.1 23.8 %collective-permute-done.9 = bf16[512,1024]{1,0:T(8,128)(2,1)S(1)} collective-permute-done((bf16[512,1024]{1,0:T(8,128)(2,1)S(1)}, bf16[512,1024]{1,0:T(8,128)(2,1)S(1)}, u32[]{:S(2)}, u32[]{:S(2)}) %collective-permute-start.9) | collective-permute-done | bytes 1048608 | tf_op jit(solution)/shard_map/ppermute | solution.py:195
  70.1 12.9 %collective-permute-done.11 = bf16[512,1024]{1,0:T(8,128)(2,1)S(1)} collective-permute-done((bf16[512,1024]{1,0:T(8,128)(2,1)S(1)}, bf16[512,1024]{1,0:T(8,128)(2,1)S(1)}, u32[]{:S(2)}, u32[]{:S(2)}) %collective-permute-start.11) | collective-permute-done | bytes 1048608 | tf_op jit(solution)/shard_map/ppermute | solution.py:195
  91.3 15.2 %convert_reduce_fusion.2 = (f32[512]{0:T(512)S(1)}, f32[512]{0:T(512)S(1)}, bf16[512,2048]{1,0:T(8,128)(2,1)S(1)}) fusion(bf16[256,512]{1,0:T(8,128)(2,1)S(1)} %copy-done.105, bf16[256,512]{1,0:T(8,128)(2,1)S(1)} %copy-done.103, bf16[256,512]{1,0:T(8,128)(2,1)S(1)} %copy-done.101, bf16[256,512]{1,0:T(8,128)(2,1)S(1)} %copy-done.99, ...), kind=kLoop, calls=%fused_computation.17 | loop fusion | flops 20970496 | bytes 4198400 | tf_op jit(solution)/shard_map/reduce_sum | solution.py:311
  122.6 9.8 collective-permute-done.17
  132.6 10.9 collective-permute-done.19
  155.8 41.4 %attend_forward.1 = (bf16[512,2048]{1,0:T(8,128)(2,1)S(1)}, f32[16,512]{1,0:T(8,128)S(1)}) custom-call(s32[4]{0:T(128)S(1)} %get-tuple-element.260.full_ref, s32[4]{0:T(128)S(1)} %get-tuple-element.259.count_ref, s32[16]{0:T(128)S(1)} %xor_add_fusion.slot_ref, bf16[512,2048]{1,0:T(8,128)(2,1)} %fusion.26.q_ref, ...), custom_call_target="tpu_custom_call" | custom-call | tf_op jit(solution)/shard_map/attend_forward/pallas_call | solution.py:147
  197.1 37.6 %collective-permute-done.23 = bf16[512,4096]{1,0:T(8,128)(2,1)} collective-permute-done((bf16[512,4096]{1,0:T(8,128)(2,1)S(1)}, bf16[512,4096]{1,0:T(8,128)(2,1)}, u32[]{:S(2)}, u32[]{:S(2)}) %collective-permute-start.23) | collective-permute-done | bytes 4194336 | tf_op jit(solution)/shard_map/ppermute | solution.py:195
  242.9 16.0 %collective-permute-done.21 = bf16[2048,1024]{1,0:T(8,128)(2,1)S(1)} collective-permute-done((bf16[2048,1024]{1,0:T(8,128)(2,1)S(1)}, bf16[2048,1024]{1,0:T(8,128)(2,1)S(1)}, u32[]{:S(2)}, u32[]{:S(2)}) %collective-permute-start.21) | collective-permute-done | bytes 4194336 | tf_op jit(solution)/shard_map/ppermute | solution.py:195
  269.9 41.0 %collective-permute-done.22 = bf16[512,2048]{1,0:T(8,128)(2,1)S(1)} collective-permute-done((bf16[512,2048]{1,0:T(8,128)(2,1)S(1)}, bf16[512,2048]{1,0:T(8,128)(2,1)S(1)}, u32[]{:S(2)}, u32[]{:S(2)}) %collective-permute-start.22) | collective-permute-done | bytes 2097184 | tf_op jit(solution)/shard_map/ppermute | solution.py:195
  312.2 14.4 %fusion.34 = f32[1024,4096]{1,0:T(8,128)} fusion(bf16[1024,4096]{1,0:T(8,128)(2,1)} %collective-permute-done.24, bf16[512,2048]{1,0:T(8,128)(2,1)S(1)} %add_convert_fusion.9, bf16[512,2048]{1,0:T(8,128)(2,1)S(1)} %collective-permute-done.22), kind=kOutput, calls=%fused_computation.90 | convolution fusion | flops 8594128896 | bytes 29360128 | tf_op jit(solution)/shard_map/dot_general | solution.py:328
  326.6 24.3 %fusion.4 = (bf16[1024,4096]{1,0:T(8,128)(2,1)}, f32[1024,4096]{1,0:T(8,128)}) fusion(f32[4096]{0:T(1024)S(1)} %copy-done.139, f32[1024,4096]{1,0:T(8,128)} %fusion.34, bf16[1024,4096]{1,0:T(8,128)(2,1)} %constant_dynamic-update-slice_fusion.8, bf16[512,2048]{1,0:T(8,128)(2,1)S(1)} %add_convert_fusion.9, bf16[512,2048]{1,0:T(8,128)(2,1)} %copy-done.78), kind=kOutput, calls=%fused_computation.5 | convolution fusion | flops 8640266240 | bytes 54542336 | tf_op jit(solution)/shard_map/dot_general | solution.py:328
  367.5 15.1 %fusion.88 = f32[1024,1024]{0,1:T(8,128)} fusion(bf16[1024,4096]{1,0:T(8,128)(2,1)} %get-tuple-element.89.refs_0_, bf16[4096,1024]{1,0:T(8,128)(2,1)} %constant_dynamic-update-slice_fusion.10), kind=kOutput, calls=%fused_computation.313 | convolution fusion | flops 8589934592 | bytes 20971520 | tf_op jit(solution)/shard_map/dot_general | solution.py:328
  395.4 13.3 %fusion.89 = f32[1024,1024]{1,0:T(8,128)S(1)} fusion(bf16[1024,4096]{1,0:T(8,128)(2,1)} %get-tuple-element.89.refs_0_, bf16[4096,1024]{1,0:T(8,128)(2,1)} %collective-permute-done.26), kind=kOutput, calls=%fused_computation.314 | convolution fusion | flops 8589934592 | bytes 20971520 | tf_op jit(solution)/shard_map/dot_general | solution.py:328
  419.5 19.9 %collective-permute-done.29 = bf16[1024,512]{1,0:T(8,128)(2,1)} collective-permute-done((bf16[1024,512]{1,0:T(8,128)(2,1)}, bf16[1024,512]{1,0:T(8,128)(2,1)}, u32[]{:S(2)}, u32[]{:S(2)}) %collective-permute-start.29) | collective-permute-done | bytes 1048608 | tf_op jit(solution)/shard_map/ppermute | solution.py:195
  441.3 18.4 %collective-permute-done.34 = bf16[1024,512]{1,0:T(8,128)(2,1)} collective-permute-done((bf16[1024,512]{1,0:T(8,128)(2,1)}, bf16[1024,512]{1,0:T(8,128)(2,1)}, u32[]{:S(2)}, u32[]{:S(2)}) %collective-permute-start.34) | collective-permute-done | bytes 1048608 | tf_op jit(solution)/shard_map/ppermute | solution.py:195
  482.6 18.1 %convert_reduce_fusion.5 = (f32[2048]{0:T(1024)}, bf16[512,2048]{1,0:T(8,128)(2,1)S(1)}, f32[512,2048]{1,0:T(8,128)}, f32[512,2048]{1,0:T(8,128)}) fusion(bf16[256,512]{1,0:T(8,128)(2,1)S(1)} %get-tuple-element.214, bf16[256,512]{1,0:T(8,128)(2,1)S(1)} %get-tuple-element.215, bf16[256,512]{1,0:T(8,128)(2,1)S(1)} %get-tuple-element.231, ...), kind=kLoop, calls=%fused_computation.61 | loop fusion | flops 41940992 | bytes 23087104 | tf_op jit(solution)/shard_map/reduce_sum | solution.py:634
  502.3 43.8 %collective-permute-done.36 = bf16[512,2048]{1,0:T(8,128)(2,1)S(1)} collective-permute-done((bf16[512,2048]{1,0:T(8,128)(2,1)S(1)}, bf16[512,2048]{1,0:T(8,128)(2,1)S(1)}, u32[]{:S(2)}, u32[]{:S(2)}) %collective-permute-start.36) | collective-permute-done | bytes 2097184 | tf_op jit(solution)/shard_map/ppermute | solution.py:195
  598.6 14.5 %fusion.36 = f32[1024,4096]{1,0:T(8,128)} fusion(bf16[4096,1024]{1,0:T(8,128)(2,1)} %collective-permute-done.26, bf16[1024,2048]{1,0:T(8,128)(2,1)S(1)} %copy-done.32), kind=kOutput, calls=%fused_computation.102 | convolution fusion | flops 8589934592 | bytes 27262976 | tf_op jit(solution)/shard_map/dot_general | solution.py:332
  613.1 26.6 %convert_reduce_fusion = (f32[4096]{0:T(1024)}, bf16[1024,4096]{1,0:T(8,128)(2,1)}) fusion(f32[1024,4096]{1,0:T(8,128)} %get-tuple-element.256, f32[1024,4096]{1,0:T(8,128)} %fusion.36, bf16[4096,1024]{1,0:T(8,128)(2,1)} %constant_dynamic-update-slice_fusion.10, bf16[1024,2048]{1,0:T(8,128)(2,1)} %pad_maximum_fusion.4.refs_1_), kind=kOutput, calls=%fused_computation.6 | convolution fusion | flops 8678010880 | bytes 52445184 | tf_op jit(solution)/shard_map/dot_general | solution.py:332
  649.6 11.4 fusion.90
  661.1 12.8 %fusion.91 = f32[1024,1024]{1,0:T(8,128)S(1)} fusion(bf16[1024,4096]{1,0:T(8,128)(2,1)S(1)} %copy-done.31, bf16[1024,4096]{1,0:T(8,128)(2,1)} %collective-permute-done.24), kind=kOutput, calls=%fused_computation.316 | convolution fusion | flops 8589934592 | bytes 20971520 | tf_op jit(solution)/shard_map/dot_general | solution.py:332
  697.5 9.3 token_product.27
  741.5 13.5 %collective-permute-done.40 = bf16[512,2048]{1,0:T(8,128)(2,1)} collective-permute-done((bf16[512,2048]{1,0:T(8,128)(2,1)S(1)}, bf16[512,2048]{1,0:T(8,128)(2,1)}, u32[]{:S(2)}, u32[]{:S(2)}) %collective-permute-start.40) | collective-permute-done | bytes 2097184 | tf_op jit(solution)/shard_map/ppermute | solution.py:195
  782.5 9.4 fusion.5
  841.0 60.8 %attend_backward.1 = (bf16[512,2048]{1,0:T(8,128)(2,1)S(1)}, f32[4096,128]{1,0:T(8,128)}, f32[4096,128]{1,0:T(8,128)}) custom-call(s32[4]{0:T(128)S(1)} %copy-done.28, s32[4]{0:T(128)S(1)} %copy-done.26, s32[16]{0:T(128)S(1)} %copy-done.30, bf16[512,2048]{1,0:T(8,128)(2,1)} %fusion.26.q_ref, bf16[512,2048]{1,0:T(8,128)(2,1)} %copy-done.53, ...), custom_call_target="tpu_custom_call" | custom-call | tf_op jit(solution)/shard_map/attend_backward/pallas_call | solution.py:176
  937.8 19.7 %collective-permute-done.89 = bf16[2048,512]{1,0:T(8,128)(2,1)} collective-permute-done((bf16[2048,512]{1,0:T(8,128)(2,1)}, bf16[2048,512]{1,0:T(8,128)(2,1)}, u32[]{:S(2)}, u32[]{:S(2)}) %collective-permute-start.89) | collective-permute-done | bytes 2097184 | tf_op jit(solution)/shard_map/ppermute | solution.py:480
  986.4 17.7 %collective-permute-start.82 = (bf16[1024,512]{1,0:T(8,128)(2,1)S(1)}, bf16[1024,512]{1,0:T(8,128)(2,1)}, u32[]{:S(2)}, u32[]{:S(2)}) collective-permute-start(bf16[1024,512]{1,0:T(8,128)(2,1)S(1)} %convert_element_type.278), channel_id=1, source_target_pairs={{0,8},{24,16},{1,9},{25,17},{2,10},{26,18},{3,11},{27,19},{4,12},{... | collective-permute-start | bytes 3145736 | tf_op jit(solution)/shard_map/ppermute | solution.py:465
  1010.2 15.1 %collective-permute-done.86 = bf16[512,2048]{1,0:T(8,128)(2,1)} collective-permute-done((bf16[512,2048]{1,0:T(8,128)(2,1)}, bf16[512,2048]{1,0:T(8,128)(2,1)}, u32[]{:S(2)}, u32[]{:S(2)}) %collective-permute-start.86) | collective-permute-done | bytes 2097184 | tf_op jit(solution)/shard_map/ppermute | solution.py:480
  1042.3 9.3 collective-permute-done.55
  1141.8 10.1 collective-permute-done.78
  1156.0 9.0 collective-permute-done.79
  1179.3 13.6 %collective-permute-done.80 = f32[512,256]{1,0:T(8,128)S(1)} collective-permute-done((f32[512,256]{1,0:T(8,128)S(1)}, f32[512,256]{1,0:T(8,128)S(1)}, u32[]{:S(2)}, u32[]{:S(2)}) %collective-permute-start.80) | collective-permute-done | bytes 524320 | tf_op jit(solution)/shard_map/ppermute | solution.py:195
  (653 shorter events, 582.8 us)
Async XLA Ops:
  60.0 60.9 %collective-permute-start.13 = (f32[1,1024]{1,0:T(1,128)S(1)}, f32[1,1024]{1,0:T(1,128)S(1)}, u32[]{:S(2)}, u32[]{:S(2)}) collective-permute-start(f32[1,1024]{1,0:T(1,128)S(1)} %bitcast.112), channel_id=1, source_target_pairs={{0,4},{4,0},{1,5},{5,1},{2,6},{6,2},{3,7},{7,3},{8,12},{12,8},{9,1... | collective-permute-start | bytes 12296 | tf_op jit(solution)/shard_map/ppermute | solution.py:195
  91.1 55.6 %collective-permute-start.12 = (bf16[2048,1024]{1,0:T(8,128)(2,1)S(1)}, bf16[2048,1024]{1,0:T(8,128)(2,1)S(1)}, u32[]{:S(2)}, u32[]{:S(2)}) collective-permute-start(bf16[2048,1024]{1,0:T(8,128)(2,1)S(1)} %pad_maximum_fusion.3), channel_id=1, source_target_pairs={{0,1},{1,0},{2,3},{3,2},{4,5},{5,4},{6,7},{7,6},{8,9},{9,8},{10,11... | collective-permute-start | bytes 12582920 | tf_op jit(solution)/shard_map/ppermute | solution.py:195
  143.4 91.3 %collective-permute-start.23 = (bf16[512,4096]{1,0:T(8,128)(2,1)S(1)}, bf16[512,4096]{1,0:T(8,128)(2,1)}, u32[]{:S(2)}, u32[]{:S(2)}) collective-permute-start(bf16[512,4096]{1,0:T(8,128)(2,1)S(1)} %copy-done.54), channel_id=1, source_target_pairs={{0,2},{1,3},{2,0},{3,1},{4,6},{5,7},{6,4},{7,5},{8,10},{9,11},{10,... | collective-permute-start | bytes 12582920 | tf_op jit(solution)/shard_map/ppermute | solution.py:195
  153.7 86.0 %collective-permute-start.20 = (bf16[1024,1024]{1,0:T(8,128)(2,1)S(1)}, bf16[1024,1024]{1,0:T(8,128)(2,1)S(1)}, u32[]{:S(2)}, u32[]{:S(2)}) collective-permute-start(bf16[1024,1024]{1,0:T(8,128)(2,1)S(1)} %pad_maximum_fusion.7), channel_id=1, source_target_pairs={{0,4},{4,0},{1,5},{5,1},{2,6},{6,2},{3,7},{7,3},{8,12},{12,8},{9,1... | collective-permute-start | bytes 6291464 | tf_op jit(solution)/shard_map/ppermute | solution.py:195
  239.5 71.4 %collective-permute-start.24 = (bf16[1024,4096]{1,0:T(8,128)(2,1)}, bf16[1024,4096]{1,0:T(8,128)(2,1)}, u32[]{:S(2)}, u32[]{:S(2)}) collective-permute-start(bf16[1024,4096]{1,0:T(8,128)(2,1)} %constant_dynamic-update-slice_fusion.8), channel_id=1, source_target_pairs={{0,1},{1,0},{2,3},{3,2},{4,5},{5,4},{6,7},{7,6},{8,9},{9,8},{10,11... | collective-permute-start | bytes 25165832 | tf_op jit(solution)/shard_map/ppermute | solution.py:195
  263.1 47.7 %collective-permute-start.22 = (bf16[512,2048]{1,0:T(8,128)(2,1)S(1)}, bf16[512,2048]{1,0:T(8,128)(2,1)S(1)}, u32[]{:S(2)}, u32[]{:S(2)}) collective-permute-start(bf16[512,2048]{1,0:T(8,128)(2,1)S(1)} %add_convert_fusion.9), channel_id=1, source_target_pairs={{0,4},{4,0},{1,5},{5,1},{2,6},{6,2},{3,7},{7,3},{8,12},{12,8},{9,1... | collective-permute-start | bytes 6291464 | tf_op jit(solution)/shard_map/ppermute | solution.py:195
  264.7 92.7 %collective-permute-start.25 = (bf16[4096,512]{1,0:T(8,128)(2,1)}, bf16[4096,512]{1,0:T(8,128)(2,1)}, u32[]{:S(2)}, u32[]{:S(2)}) collective-permute-start(bf16[4096,512]{1,0:T(8,128)(2,1)} %param.32), channel_id=1, source_target_pairs={{0,2},{1,3},{2,0},{3,1},{4,6},{5,7},{6,4},{7,5},{8,10},{9,11},{10,... | collective-permute-start | bytes 12582920 | tf_op jit(solution)/shard_map/ppermute | solution.py:195
  411.4 50.6 %collective-permute-start.27 = (bf16[512,2048]{1,0:T(8,128)(2,1)}, bf16[512,2048]{1,0:T(8,128)(2,1)}, u32[]{:S(2)}, u32[]{:S(2)}) collective-permute-start(bf16[512,2048]{1,0:T(8,128)(2,1)} %fusion.25), channel_id=1, source_target_pairs={{0,4},{4,0},{1,5},{5,1},{2,6},{6,2},{3,7},{7,3},{8,12},{12,8},{9,1... | collective-permute-start | bytes 6291464 | tf_op jit(solution)/shard_map/ppermute | solution.py:195
  576.0 63.7 %collective-permute-start.39 = (bf16[2048,512]{1,0:T(8,128)(2,1)}, bf16[2048,512]{1,0:T(8,128)(2,1)}, u32[]{:S(2)}, u32[]{:S(2)}) collective-permute-start(bf16[2048,512]{1,0:T(8,128)(2,1)} %token_product.22), channel_id=1, source_target_pairs={{0,2},{1,3},{2,0},{3,1},{4,6},{5,7},{6,4},{7,5},{8,10},{9,11},{10,... | collective-permute-start | bytes 6291464 | tf_op jit(solution)/shard_map/ppermute | solution.py:195
  581.9 103.8 %collective-permute-start.41 = (bf16[2048,512]{1,0:T(8,128)(2,1)S(1)}, bf16[2048,512]{1,0:T(8,128)(2,1)}, u32[]{:S(2)}, u32[]{:S(2)}) collective-permute-start(bf16[2048,512]{1,0:T(8,128)(2,1)S(1)} %token_product.23), channel_id=1, source_target_pairs={{0,2},{1,3},{2,0},{3,1},{4,6},{5,7},{6,4},{7,5},{8,10},{9,11},{10,... | collective-permute-start | bytes 6291464 | tf_op jit(solution)/shard_map/ppermute | solution.py:195
  644.8 48.3 %collective-permute-start.42 = (bf16[2048,512]{1,0:T(8,128)(2,1)}, bf16[2048,512]{1,0:T(8,128)(2,1)}, u32[]{:S(2)}, u32[]{:S(2)}) collective-permute-start(bf16[2048,512]{1,0:T(8,128)(2,1)} %fusion.27), channel_id=1, source_target_pairs={{0,8},{24,16},{1,9},{25,17},{2,10},{26,18},{3,11},{27,19},{4,12},{... | collective-permute-start | bytes 6291464 | tf_op jit(solution)/shard_map/ppermute | solution.py:465
  706.8 48.1 %collective-permute-start.40 = (bf16[512,2048]{1,0:T(8,128)(2,1)S(1)}, bf16[512,2048]{1,0:T(8,128)(2,1)}, u32[]{:S(2)}, u32[]{:S(2)}) collective-permute-start(bf16[512,2048]{1,0:T(8,128)(2,1)S(1)} %copy-done.74), channel_id=1, source_target_pairs={{0,4},{4,0},{1,5},{5,1},{2,6},{6,2},{3,7},{7,3},{8,12},{12,8},{9,1... | collective-permute-start | bytes 6291464 | tf_op jit(solution)/shard_map/ppermute | solution.py:195
  708.3 55.2 %collective-permute-start.47 = (bf16[2048,512]{1,0:T(8,128)(2,1)}, bf16[2048,512]{1,0:T(8,128)(2,1)}, u32[]{:S(2)}, u32[]{:S(2)}) collective-permute-start(bf16[2048,512]{1,0:T(8,128)(2,1)} %fusion.28), channel_id=1, source_target_pairs={{0,8},{24,16},{1,9},{25,17},{2,10},{26,18},{3,11},{27,19},{4,12},{... | collective-permute-start | bytes 6291464 | tf_op jit(solution)/shard_map/ppermute | solution.py:465
  714.5 49.1 %collective-permute-start.46 = (bf16[2048,512]{1,0:T(8,128)(2,1)}, bf16[2048,512]{1,0:T(8,128)(2,1)}, u32[]{:S(2)}, u32[]{:S(2)}) collective-permute-start(bf16[2048,512]{1,0:T(8,128)(2,1)} %add_convert_fusion.8), channel_id=1, source_target_pairs={{8,16},{16,8},{9,17},{17,9},{10,18},{18,10},{11,19},{19,11},{12,20... | collective-permute-start | bytes 6291464 | tf_op jit(solution)/shard_map/ppermute | solution.py:472
  722.3 50.6 %collective-permute-start.45 = (bf16[512,2048]{1,0:T(8,128)(2,1)}, bf16[512,2048]{1,0:T(8,128)(2,1)}, u32[]{:S(2)}, u32[]{:S(2)}) collective-permute-start(bf16[512,2048]{1,0:T(8,128)(2,1)} %token_product.28), channel_id=1, source_target_pairs={{0,2},{1,3},{2,0},{3,1},{4,6},{5,7},{6,4},{7,5},{8,10},{9,11},{10,... | collective-permute-start | bytes 6291464 | tf_op jit(solution)/shard_map/ppermute | solution.py:195
  781.9 48.4 %collective-permute-start.48 = (bf16[512,2048]{1,0:T(8,128)(2,1)}, bf16[512,2048]{1,0:T(8,128)(2,1)}, u32[]{:S(2)}, u32[]{:S(2)}) collective-permute-start(bf16[512,2048]{1,0:T(8,128)(2,1)} %copy-done.22), channel_id=1, source_target_pairs={{0,2},{1,3},{2,0},{3,1},{4,6},{5,7},{6,4},{7,5},{8,10},{9,11},{10,... | collective-permute-start | bytes 6291464 | tf_op jit(solution)/shard_map/ppermute | solution.py:195
  791.9 114.9 %collective-permute-start.88 = (bf16[2048,512]{1,0:T(8,128)(2,1)}, bf16[2048,512]{1,0:T(8,128)(2,1)}, u32[]{:S(2)}, u32[]{:S(2)}) collective-permute-start(bf16[2048,512]{1,0:T(8,128)(2,1)} %add_convert_fusion.7), channel_id=1, source_target_pairs={{8,0},{16,24},{9,1},{17,25},{10,2},{18,26},{11,3},{19,27},{12,4},{... | collective-permute-start | bytes 6291464 | tf_op jit(solution)/shard_map/ppermute | solution.py:480
  793.3 108.5 %collective-permute-start.51 = (bf16[2048,512]{1,0:T(8,128)(2,1)}, bf16[2048,512]{1,0:T(8,128)(2,1)}, u32[]{:S(2)}, u32[]{:S(2)}) collective-permute-start(bf16[2048,512]{1,0:T(8,128)(2,1)} %add_convert_fusion.6), channel_id=1, source_target_pairs={{8,16},{16,8},{9,17},{17,9},{10,18},{18,10},{11,19},{19,11},{12,20... | collective-permute-start | bytes 6291464 | tf_op jit(solution)/shard_map/ppermute | solution.py:472
  795.4 112.8 %collective-permute-start.52 = (bf16[512,2048]{1,0:T(8,128)(2,1)}, bf16[512,2048]{1,0:T(8,128)(2,1)}, u32[]{:S(2)}, u32[]{:S(2)}) collective-permute-start(bf16[512,2048]{1,0:T(8,128)(2,1)} %fusion.29), channel_id=1, source_target_pairs={{0,8},{24,16},{1,9},{25,17},{2,10},{26,18},{3,11},{27,19},{4,12},{... | collective-permute-start | bytes 6291464 | tf_op jit(solution)/shard_map/ppermute | solution.py:465
  812.9 95.3 %collective-permute-start.50 = (bf16[1024,1024]{1,0:T(8,128)(2,1)}, bf16[1024,1024]{1,0:T(8,128)(2,1)}, u32[]{:S(2)}, u32[]{:S(2)}) collective-permute-start(bf16[1024,1024]{1,0:T(8,128)(2,1)} %token_product.33), channel_id=1, source_target_pairs={{0,4},{4,0},{1,5},{5,1},{2,6},{6,2},{3,7},{7,3},{8,12},{12,8},{9,1... | collective-permute-start | bytes 6291464 | tf_op jit(solution)/shard_map/ppermute | solution.py:195
  835.3 92.5 %collective-permute-start.69 = (bf16[512,2048]{1,0:T(8,128)(2,1)}, bf16[512,2048]{1,0:T(8,128)(2,1)}, u32[]{:S(2)}, u32[]{:S(2)}) collective-permute-start(bf16[512,2048]{1,0:T(8,128)(2,1)} %fusion.30), channel_id=1, source_target_pairs={{0,8},{24,16},{1,9},{25,17},{2,10},{26,18},{3,11},{27,19},{4,12},{... | collective-permute-start | bytes 6291464 | tf_op jit(solution)/shard_map/ppermute | solution.py:465
  906.8 50.8 %collective-permute-start.89 = (bf16[2048,512]{1,0:T(8,128)(2,1)}, bf16[2048,512]{1,0:T(8,128)(2,1)}, u32[]{:S(2)}, u32[]{:S(2)}) collective-permute-start(bf16[2048,512]{1,0:T(8,128)(2,1)} %add_convert_fusion.4), channel_id=1, source_target_pairs={{8,0},{16,24},{9,1},{17,25},{10,2},{18,26},{11,3},{19,27},{12,4},{... | collective-permute-start | bytes 6291464 | tf_op jit(solution)/shard_map/ppermute | solution.py:480
  915.3 53.5 %collective-permute-start.53 = (bf16[1024,2048]{1,0:T(8,128)(2,1)}, bf16[1024,2048]{1,0:T(8,128)(2,1)}, u32[]{:S(2)}, u32[]{:S(2)}) collective-permute-start(bf16[1024,2048]{1,0:T(8,128)(2,1)} %token_product.35), channel_id=1, source_target_pairs={{0,1},{1,0},{2,3},{3,2},{4,5},{5,4},{6,7},{7,6},{8,9},{9,8},{10,11... | collective-permute-start | bytes 12582920 | tf_op jit(solution)/shard_map/ppermute | solution.py:195
  933.2 108.3 %collective-permute-start.73 = (bf16[512,2048]{1,0:T(8,128)(2,1)S(1)}, bf16[512,2048]{1,0:T(8,128)(2,1)}, u32[]{:S(2)}, u32[]{:S(2)}) collective-permute-start(bf16[512,2048]{1,0:T(8,128)(2,1)S(1)} %add_convert_fusion.2), channel_id=1, source_target_pairs={{8,16},{16,8},{9,17},{17,9},{10,18},{18,10},{11,19},{19,11},{12,20... | collective-permute-start | bytes 6291464 | tf_op jit(solution)/shard_map/ppermute | solution.py:472
  967.3 57.9 %collective-permute-start.86 = (bf16[512,2048]{1,0:T(8,128)(2,1)}, bf16[512,2048]{1,0:T(8,128)(2,1)}, u32[]{:S(2)}, u32[]{:S(2)}) collective-permute-start(bf16[512,2048]{1,0:T(8,128)(2,1)} %add_convert_fusion), channel_id=1, source_target_pairs={{8,0},{16,24},{9,1},{17,25},{10,2},{18,26},{11,3},{19,27},{12,4},{... | collective-permute-start | bytes 6291464 | tf_op jit(solution)/shard_map/ppermute | solution.py:480
  978.8 51.6 %collective-permute-start.71 = (bf16[1024,1024]{1,0:T(8,128)(2,1)S(1)}, bf16[1024,1024]{1,0:T(8,128)(2,1)}, u32[]{:S(2)}, u32[]{:S(2)}) collective-permute-start(bf16[1024,1024]{1,0:T(8,128)(2,1)S(1)} %token_product.36), channel_id=1, source_target_pairs={{0,4},{4,0},{1,5},{5,1},{2,6},{6,2},{3,7},{7,3},{8,12},{12,8},{9,1... | collective-permute-start | bytes 6291464 | tf_op jit(solution)/shard_map/ppermute | solution.py:195
  981.8 51.1 %collective-permute-start.57 = (f32[2048,256]{1,0:T(8,128)}, f32[2048,256]{1,0:T(8,128)}, u32[]{:S(2)}, u32[]{:S(2)}) collective-permute-start(f32[2048,256]{1,0:T(8,128)} %slice.390), channel_id=1, source_target_pairs={{0,1},{1,0},{2,3},{3,2},{4,5},{5,4},{6,7},{7,6},{8,9},{9,8},{10,11... | collective-permute-start | bytes 6291464 | tf_op jit(solution)/shard_map/ppermute | solution.py:195
  986.4 46.5 %collective-permute-start.82 = (bf16[1024,512]{1,0:T(8,128)(2,1)S(1)}, bf16[1024,512]{1,0:T(8,128)(2,1)}, u32[]{:S(2)}, u32[]{:S(2)}) collective-permute-start(bf16[1024,512]{1,0:T(8,128)(2,1)S(1)} %convert_element_type.278), channel_id=1, source_target_pairs={{0,8},{24,16},{1,9},{25,17},{2,10},{26,18},{3,11},{27,19},{4,12},{... | collective-permute-start | bytes 3145736 | tf_op jit(solution)/shard_map/ppermute | solution.py:465
  1062.2 90.1 %collective-permute-start.87 = (bf16[512,2048]{1,0:T(8,128)(2,1)}, bf16[512,2048]{1,0:T(8,128)(2,1)}, u32[]{:S(2)}, u32[]{:S(2)}) collective-permute-start(bf16[512,2048]{1,0:T(8,128)(2,1)} %add_convert_fusion.1), channel_id=1, source_target_pairs={{8,0},{16,24},{9,1},{17,25},{10,2},{18,26},{11,3},{19,27},{12,4},{... | collective-permute-start | bytes 6291464 | tf_op jit(solution)/shard_map/ppermute | solution.py:480
  1066.5 126.5 %collective-permute-start.84 = (bf16[1024,512]{1,0:T(8,128)(2,1)S(1)}, bf16[1024,512]{1,0:T(8,128)(2,1)}, u32[]{:S(2)}, u32[]{:S(2)}) collective-permute-start(bf16[1024,512]{1,0:T(8,128)(2,1)S(1)} %add_convert_fusion.10), channel_id=1, source_target_pairs={{8,0},{16,24},{9,1},{17,25},{10,2},{18,26},{11,3},{19,27},{12,4},{... | collective-permute-start | bytes 3145736 | tf_op jit(solution)/shard_map/ppermute | solution.py:480
  1077.9 60.7 %collective-permute-start.74 = (bf16[512,1024]{1,0:T(8,128)(2,1)}, bf16[512,1024]{1,0:T(8,128)(2,1)}, u32[]{:S(2)}, u32[]{:S(2)}) collective-permute-start(bf16[512,1024]{1,0:T(8,128)(2,1)} %convert_element_type.282), channel_id=1, source_target_pairs={{0,8},{24,16},{1,9},{25,17},{2,10},{26,18},{3,11},{27,19},{4,12},{... | collective-permute-start | bytes 3145736 | tf_op jit(solution)/shard_map/ppermute | solution.py:465
  1154.6 49.4 %collective-permute-start.76 = (bf16[512,1024]{1,0:T(8,128)(2,1)S(1)}, bf16[512,1024]{1,0:T(8,128)(2,1)S(1)}, u32[]{:S(2)}, u32[]{:S(2)}) collective-permute-start(bf16[512,1024]{1,0:T(8,128)(2,1)S(1)} %add_convert_fusion.12), channel_id=1, source_target_pairs={{8,0},{16,24},{9,1},{17,25},{10,2},{18,26},{11,3},{19,27},{12,4},{... | collective-permute-start | bytes 3145736 | tf_op jit(solution)/shard_map/ppermute | solution.py:480
  (199 other events, 4035.8 us)

commit v4 on v3

--- a/solution.py
+++ b/solution.py
@@ -528,17 +528,6 @@
     x_groups = to_tokens_direct(layer_input, chunk)
     keyval_near = jnp.concatenate(grow([w_keyval], "col", col_far), 0)
     keyval_far = send(keyval_near, "col", near)
-    query_parts = [
-        jnp.concatenate(parts, 0)
-        for parts in zip(
-            *[
-                grow([part], "row", row_masks)
-                for part in grow([after(w_query, *x_groups.values())], "col", col_far)
-            ]
-        )
-    ]
-    query_near = jnp.concatenate(query_parts, 0)
-    query_far = send(query_near, "col", near)
     vectors = jnp.stack(
         [norm1_gain, norm1_shift, b_attn_out, norm2_gain, norm2_shift, b_fc_out]
     )
@@ -561,11 +550,19 @@
 
     residual = assemble(x_groups, order).astype(f32)
     normal1, inverse1, normed1 = norm_forward(residual, gain1, shift1)
+    query_cols = grow([after(w_query, *x_groups.values())], "col", col_far)
+    query_cols = query_cols[:1] + [after(part, normed1) for part in query_cols[1:]]
     keyval = dot_nn(normed1[:, :split], keyval_near) + dot_nn(normed1[:, split:], keyval_far)
     keyval = jnp.concatenate(
         [keyval[:, :HEAD].astype(bf16), (keyval[:, HEAD:] + b_value).astype(bf16)], 1
     )
     keyval_far_rows = grow([keyval], "col", col_far)
+    query_rows = [grow([part], "row", row_masks) for part in query_cols]
+    query_parts = [
+        jnp.concatenate([after(part, keyval) for part in parts], 0) for parts in zip(*query_rows)
+    ]
+    query_near = jnp.concatenate(query_parts, 0)
+    query_far = send(query_near, "col", near)
     keyval_all = jnp.concatenate(keyval_far_rows, 0)
     keyval_all = jnp.concatenate(grow([keyval_all], "row", row_masks), 0)
     keyval_all = jnp.concatenate([keyval_all, send(keyval_all, "col", near)], 0)
@@ -586,12 +583,12 @@
     attended, log_totals = attend_forward(queries, keys, values, limits, slots, chunk)
     attn_near = jnp.concatenate(attn_rows[:-1] + [after(attn_rows[-1], attended)], 0)
     attn_far = send(attn_near, "col", near)
-    middle = residual + (
-        jnp.concatenate([dot_nn(attended, attn_near), dot_nn(attended, attn_far)], 1) + bias_o
-    )
+    middle_first = dot_nn(attended, attn_near)
+    middle = jnp.concatenate([middle_first, dot_nn(attended, attn_far)], 1)
+    middle = residual + (middle + bias_o)
     normal2, inverse2, normed2 = norm_forward(middle, gain2, shift2)
     own = normed2.shape[0]
-    fc_in_near = jnp.concatenate(fc_in_rows[:-1] + [after(fc_in_rows[-1], attended)], 0)
+    fc_in_near = jnp.concatenate(fc_in_rows[:-1] + [after(fc_in_rows[-1], middle_first, attn_far)], 0)
     fc_in_far = send(fc_in_near, "col", near)
 
     def col_product(x, first, second):

time: 1220 us -> 1220 us (level)
    unnamed x293 -> x285, local copies, waits for them, and re-layouts: 34.5 us -> 41.8 us
  transfers between devices with their start and end apart: 90 -> 90, of which waited for: 41 -> 39; matrix products, arithmetic and copies ran while one was open for 31% -> 31% of each run, Pallas kernels for 16% -> 16%
where the time goes in v4:
time: 1220 us; the launch traced here: 1210 us
  waiting for transfers between devices  412 us (34%)
  Pallas kernels  207 us (17%)
  other arithmetic  195 us (16%)
  matrix products  169 us (14%)
  starting transfers between devices  141 us (12%)
  local copies, waits for them, and re-layouts  81.7 us (7%)
    ppermute x65, waiting for transfers between devices, send(): return lax.ppermute(x, axis, [(i, i ^ mask) for i in range(size)])  351 us
    pallas_call x20, Pallas kernels, token_product(): pl.pallas_call(product_kernel, grid=((rows[1] - rows[0]) // tall, (cols[1...  105 us
    dot_general x12, matrix products, dot_nt(): return lax.dot_general(a, b, NT, preferred_element_type=f32)  87.7 us
    dot_general x12, matrix products, dot_nn(): return lax.dot_general(a, b, NN, preferred_element_type=f32)  80.2 us
    ppermute x65, starting transfers between devices, send(): return lax.ppermute(x, axis, [(i, i ^ mask) for i in range(size)])  67.9 us
    pallas_call x1, Pallas kernels, attend_backward(): pl.pallas_call(functools.partial(bwd_kernel, heads=heads, tq=tq, chunk=ch...  60.8 us
    ppermute x6, starting transfers between devices, inward(): return lax.ppermute(total.astype(wire), 'dp', [(0, 1), (3, 2)])  47.7 us
    unnamed x285, local copies, waits for them, and re-layouts  41.8 us
  transfers between devices with their start and end apart: 90, of which 39 were waited for; matrix products, arithmetic and copies ran while one was open for 31% of the time, Pallas kernels for 16%

profile of v4, /device:TPU:0, one launch (start us, length us, event | category | flops | bytes accessed | tf_op | source)
XLA Modules:
  0.0 1212.9 jit_solution(6226142558297670917)
XLA Ops:
  8.7 10.2 collective-permute-done.7
  47.2 14.7 %convert_reduce_fusion.2 = (f32[512]{0:T(512)S(1)}, f32[512]{0:T(512)S(1)}, bf16[512,2048]{1,0:T(8,128)(2,1)S(1)}) fusion(bf16[256,512]{1,0:T(8,128)(2,1)S(1)} %collective-permute-done.6, bf16[256,512]{1,0:T(8,128)(2,1)S(1)} %collective-permute-done.5, bf16[256,512]{1,0:T(8,128)(2,1)S(1)} %collective-permute-done.4, ...), kind=kLoop, calls=%fused_computation.17 | loop fusion | flops 20970496 | bytes 4198400 | tf_op jit(solution)/shard_map/reduce_sum | solution.py:311
  74.6 20.5 %collective-permute-done.13 = bf16[512,1024]{1,0:T(8,128)(2,1)S(1)} collective-permute-done((bf16[512,1024]{1,0:T(8,128)(2,1)S(1)}, bf16[512,1024]{1,0:T(8,128)(2,1)S(1)}, u32[]{:S(2)}, u32[]{:S(2)}) %collective-permute-start.13) | collective-permute-done | bytes 1048608 | tf_op jit(solution)/shard_map/ppermute | solution.py:195
  111.7 9.8 collective-permute-done.17
  150.7 41.2 %attend_forward.1 = (bf16[512,2048]{1,0:T(8,128)(2,1)S(1)}, f32[16,512]{1,0:T(8,128)S(1)}) custom-call(s32[4]{0:T(128)S(1)} %get-tuple-element.270.full_ref, s32[4]{0:T(128)S(1)} %get-tuple-element.269.count_ref, s32[16]{0:T(128)S(1)} %xor_add_fusion.slot_ref, bf16[512,2048]{1,0:T(8,128)(2,1)} %fusion.26.q_ref, ...), custom_call_target="tpu_custom_call" | custom-call | tf_op jit(solution)/shard_map/attend_forward/pallas_call | solution.py:147
  202.0 37.7 %collective-permute-done.23 = bf16[512,4096]{1,0:T(8,128)(2,1)S(1)} collective-permute-done((bf16[512,4096]{1,0:T(8,128)(2,1)}, bf16[512,4096]{1,0:T(8,128)(2,1)S(1)}, u32[]{:S(2)}, u32[]{:S(2)}) %collective-permute-start.23) | collective-permute-done | bytes 4194336 | tf_op jit(solution)/shard_map/ppermute | solution.py:195
  254.7 41.7 %collective-permute-done.22 = bf16[512,2048]{1,0:T(8,128)(2,1)S(1)} collective-permute-done((bf16[512,2048]{1,0:T(8,128)(2,1)S(1)}, bf16[512,2048]{1,0:T(8,128)(2,1)S(1)}, u32[]{:S(2)}, u32[]{:S(2)}) %collective-permute-start.22) | collective-permute-done | bytes 2097184 | tf_op jit(solution)/shard_map/ppermute | solution.py:195
  301.2 12.7 %fusion.34 = f32[1024,4096]{1,0:T(8,128)} fusion(bf16[1024,4096]{1,0:T(8,128)(2,1)S(1)} %collective-permute-done.24, bf16[512,2048]{1,0:T(8,128)(2,1)S(1)} %add_convert_fusion.9, bf16[512,2048]{1,0:T(8,128)(2,1)S(1)} %collective-permute-done.22), kind=kOutput, calls=%fused_computation.90 | convolution fusion | flops 8594128896 | bytes 29360128 | tf_op jit(solution)/shard_map/dot_general | solution.py:328
  313.9 24.5 %fusion.4 = (bf16[1024,4096]{1,0:T(8,128)(2,1)}, f32[1024,4096]{1,0:T(8,128)}) fusion(f32[4096]{0:T(1024)S(1)} %copy-done.135, f32[1024,4096]{1,0:T(8,128)} %fusion.34, bf16[1024,4096]{1,0:T(8,128)(2,1)} %constant_dynamic-update-slice_fusion.8, bf16[512,2048]{1,0:T(8,128)(2,1)} %copy-done.57, bf16[512,2048]{1,0:T(8,128)(2,1)} %copy-done.87), kind=kOutput, calls=%fused_computation.5 | convolution fusion | flops 8640266240 | bytes 54542336 | tf_op jit(solution)/shard_map/dot_general | solution.py:328
  353.1 15.1 %fusion.92 = f32[1024,1024]{0,1:T(8,128)} fusion(bf16[1024,4096]{1,0:T(8,128)(2,1)} %get-tuple-element.99.refs_0_, bf16[4096,1024]{1,0:T(8,128)(2,1)} %constant_dynamic-update-slice_fusion.10), kind=kOutput, calls=%fused_computation.314 | convolution fusion | flops 8589934592 | bytes 20971520 | tf_op jit(solution)/shard_map/dot_general | solution.py:328
  380.1 13.3 %fusion.93 = f32[1024,1024]{1,0:T(8,128)S(1)} fusion(bf16[1024,4096]{1,0:T(8,128)(2,1)} %get-tuple-element.99.refs_0_, bf16[4096,1024]{1,0:T(8,128)(2,1)} %collective-permute-done.26), kind=kOutput, calls=%fused_computation.315 | convolution fusion | flops 8589934592 | bytes 20971520 | tf_op jit(solution)/shard_map/dot_general | solution.py:328
  404.0 21.0 %collective-permute-done.29 = bf16[1024,512]{1,0:T(8,128)(2,1)} collective-permute-done((bf16[1024,512]{1,0:T(8,128)(2,1)}, bf16[1024,512]{1,0:T(8,128)(2,1)}, u32[]{:S(2)}, u32[]{:S(2)}) %collective-permute-start.29) | collective-permute-done | bytes 1048608 | tf_op jit(solution)/shard_map/ppermute | solution.py:195
  426.9 18.4 %collective-permute-done.34 = bf16[1024,512]{1,0:T(8,128)(2,1)} collective-permute-done((bf16[1024,512]{1,0:T(8,128)(2,1)}, bf16[1024,512]{1,0:T(8,128)(2,1)}, u32[]{:S(2)}, u32[]{:S(2)}) %collective-permute-start.34) | collective-permute-done | bytes 1048608 | tf_op jit(solution)/shard_map/ppermute | solution.py:195
  468.1 18.1 %convert_reduce_fusion.5 = (f32[2048]{0:T(1024)}, bf16[512,2048]{1,0:T(8,128)(2,1)S(1)}, f32[512,2048]{1,0:T(8,128)}, f32[512,2048]{1,0:T(8,128)}) fusion(bf16[256,512]{1,0:T(8,128)(2,1)S(1)} %get-tuple-element.224, bf16[256,512]{1,0:T(8,128)(2,1)S(1)} %get-tuple-element.225, bf16[256,512]{1,0:T(8,128)(2,1)S(1)} %get-tuple-element.241, ...), kind=kLoop, calls=%fused_computation.61 | loop fusion | flops 41940992 | bytes 23087104 | tf_op jit(solution)/shard_map/reduce_sum | solution.py:631
  486.9 44.7 %collective-permute-done.36 = bf16[512,2048]{1,0:T(8,128)(2,1)S(1)} collective-permute-done((bf16[512,2048]{1,0:T(8,128)(2,1)S(1)}, bf16[512,2048]{1,0:T(8,128)(2,1)S(1)}, u32[]{:S(2)}, u32[]{:S(2)}) %collective-permute-start.36) | collective-permute-done | bytes 2097184 | tf_op jit(solution)/shard_map/ppermute | solution.py:195
  581.5 14.6 %fusion.36 = f32[1024,4096]{1,0:T(8,128)} fusion(bf16[4096,1024]{1,0:T(8,128)(2,1)} %collective-permute-done.26, bf16[1024,2048]{1,0:T(8,128)(2,1)S(1)} %copy-done.34), kind=kOutput, calls=%fused_computation.102 | convolution fusion | flops 8589934592 | bytes 27262976 | tf_op jit(solution)/shard_map/dot_general | solution.py:332
  596.1 26.6 %convert_reduce_fusion = (f32[4096]{0:T(1024)}, bf16[1024,4096]{1,0:T(8,128)(2,1)}) fusion(f32[1024,4096]{1,0:T(8,128)} %get-tuple-element.266, f32[1024,4096]{1,0:T(8,128)} %fusion.36, bf16[4096,1024]{1,0:T(8,128)(2,1)} %constant_dynamic-update-slice_fusion.10, bf16[1024,2048]{1,0:T(8,128)(2,1)} %pad_maximum_fusion.4.refs_1_), kind=kOutput, calls=%fused_computation.6 | convolution fusion | flops 8678010880 | bytes 52445184 | tf_op jit(solution)/shard_map/dot_general | solution.py:332
  632.6 11.5 fusion.94
  644.1 12.8 %fusion.95 = f32[1024,1024]{1,0:T(8,128)S(1)} fusion(bf16[1024,4096]{1,0:T(8,128)(2,1)S(1)} %copy-done.33, bf16[1024,4096]{1,0:T(8,128)(2,1)} %copy-done.132), kind=kOutput, calls=%fused_computation.317 | convolution fusion | flops 8589934592 | bytes 20971520 | tf_op jit(solution)/shard_map/dot_general | solution.py:332
  680.6 9.2 token_product.27
  724.2 13.9 %collective-permute-done.40 = bf16[512,2048]{1,0:T(8,128)(2,1)} collective-permute-done((bf16[512,2048]{1,0:T(8,128)(2,1)}, bf16[512,2048]{1,0:T(8,128)(2,1)}, u32[]{:S(2)}, u32[]{:S(2)}) %collective-permute-start.40) | collective-permute-done | bytes 2097184 | tf_op jit(solution)/shard_map/ppermute | solution.py:195
  765.1 9.9 fusion.5
  791.5 20.6 %collective-permute-done.48 = bf16[512,2048]{1,0:T(8,128)(2,1)} collective-permute-done((bf16[512,2048]{1,0:T(8,128)(2,1)}, bf16[512,2048]{1,0:T(8,128)(2,1)}, u32[]{:S(2)}, u32[]{:S(2)}) %collective-permute-start.48) | collective-permute-done | bytes 2097184 | tf_op jit(solution)/shard_map/ppermute | solution.py:195
  840.2 60.8 %attend_backward.1 = (bf16[512,2048]{1,0:T(8,128)(2,1)S(1)}, f32[4096,128]{1,0:T(8,128)}, f32[4096,128]{1,0:T(8,128)}) custom-call(s32[4]{0:T(128)S(1)} %copy-done.30, s32[4]{0:T(128)S(1)} %copy-done.28, s32[16]{0:T(128)S(1)} %copy-done.32, bf16[512,2048]{1,0:T(8,128)(2,1)} %fusion.26.q_ref, bf16[512,2048]{1,0:T(8,128)(2,1)} %copy-done.56, ...), custom_call_target="tpu_custom_call" | custom-call | tf_op jit(solution)/shard_map/attend_backward/pallas_call | solution.py:176
  937.8 18.5 %collective-permute-done.89 = bf16[2048,512]{1,0:T(8,128)(2,1)} collective-permute-done((bf16[2048,512]{1,0:T(8,128)(2,1)}, bf16[2048,512]{1,0:T(8,128)(2,1)}, u32[]{:S(2)}, u32[]{:S(2)}) %collective-permute-start.89) | collective-permute-done | bytes 2097184 | tf_op jit(solution)/shard_map/ppermute | solution.py:480
  988.9 16.4 %collective-permute-start.82 = (bf16[1024,512]{1,0:T(8,128)(2,1)S(1)}, bf16[1024,512]{1,0:T(8,128)(2,1)}, u32[]{:S(2)}, u32[]{:S(2)}) collective-permute-start(bf16[1024,512]{1,0:T(8,128)(2,1)S(1)} %convert_element_type.278), channel_id=1, source_target_pairs={{0,8},{24,16},{1,9},{25,17},{2,10},{26,18},{3,11},{27,19},{4,12},{... | collective-permute-start | bytes 3145736 | tf_op jit(solution)/shard_map/ppermute | solution.py:465
  1010.7 13.1 %collective-permute-done.86 = bf16[512,2048]{1,0:T(8,128)(2,1)} collective-permute-done((bf16[512,2048]{1,0:T(8,128)(2,1)}, bf16[512,2048]{1,0:T(8,128)(2,1)}, u32[]{:S(2)}, u32[]{:S(2)}) %collective-permute-start.86) | collective-permute-done | bytes 2097184 | tf_op jit(solution)/shard_map/ppermute | solution.py:480
  1039.0 11.3 collective-permute-done.55
  1063.8 9.0 collective-permute-done.72.refs_4_
  1109.3 9.3 collective-permute-start.64
  1135.9 10.1 collective-permute-done.78
  1174.6 12.4 %collective-permute-done.80 = f32[512,256]{1,0:T(8,128)S(1)} collective-permute-done((f32[512,256]{1,0:T(8,128)S(1)}, f32[512,256]{1,0:T(8,128)S(1)}, u32[]{:S(2)}, u32[]{:S(2)}) %collective-permute-start.80) | collective-permute-done | bytes 524320 | tf_op jit(solution)/shard_map/ppermute | solution.py:195
  (645 shorter events, 582.3 us)
Async XLA Ops:
  144.5 50.0 %collective-permute-start.20 = (bf16[1024,1024]{1,0:T(8,128)(2,1)}, bf16[1024,1024]{1,0:T(8,128)(2,1)}, u32[]{:S(2)}, u32[]{:S(2)}) collective-permute-start(bf16[1024,1024]{1,0:T(8,128)(2,1)} %pad_maximum_fusion.7), channel_id=1, source_target_pairs={{0,4},{4,0},{1,5},{5,1},{2,6},{6,2},{3,7},{7,3},{8,12},{12,8},{9,1... | collective-permute-start | bytes 6291464 | tf_op jit(solution)/shard_map/ppermute | solution.py:195
  148.5 91.2 %collective-permute-start.23 = (bf16[512,4096]{1,0:T(8,128)(2,1)}, bf16[512,4096]{1,0:T(8,128)(2,1)S(1)}, u32[]{:S(2)}, u32[]{:S(2)}) collective-permute-start(bf16[512,4096]{1,0:T(8,128)(2,1)} %param.30), channel_id=1, source_target_pairs={{0,2},{1,3},{2,0},{3,1},{4,6},{5,7},{6,4},{7,5},{8,10},{9,11},{10,... | collective-permute-start | bytes 12582920 | tf_op jit(solution)/shard_map/ppermute | solution.py:195
  196.3 43.4 %collective-permute-start.21 = (bf16[2048,1024]{1,0:T(8,128)(2,1)S(1)}, bf16[2048,1024]{1,0:T(8,128)(2,1)S(1)}, u32[]{:S(2)}, u32[]{:S(2)}) collective-permute-start(bf16[2048,1024]{1,0:T(8,128)(2,1)S(1)} %constant_dynamic-update-slice_fusion.6), channel_id=1, source_target_pairs={{0,1},{1,0},{2,3},{3,2},{4,5},{5,4},{6,7},{7,6},{8,9},{9,8},{10,11... | collective-permute-start | bytes 12582920 | tf_op jit(solution)/shard_map/ppermute | solution.py:195
  242.2 54.3 %collective-permute-start.24 = (bf16[1024,4096]{1,0:T(8,128)(2,1)}, bf16[1024,4096]{1,0:T(8,128)(2,1)S(1)}, u32[]{:S(2)}, u32[]{:S(2)}) collective-permute-start(bf16[1024,4096]{1,0:T(8,128)(2,1)} %constant_dynamic-update-slice_fusion.8), channel_id=1, source_target_pairs={{0,1},{1,0},{2,3},{3,2},{4,5},{5,4},{6,7},{7,6},{8,9},{9,8},{10,11... | collective-permute-start | bytes 25165832 | tf_op jit(solution)/shard_map/ppermute | solution.py:195
  249.1 47.3 %collective-permute-start.22 = (bf16[512,2048]{1,0:T(8,128)(2,1)S(1)}, bf16[512,2048]{1,0:T(8,128)(2,1)S(1)}, u32[]{:S(2)}, u32[]{:S(2)}) collective-permute-start(bf16[512,2048]{1,0:T(8,128)(2,1)S(1)} %add_convert_fusion.9), channel_id=1, source_target_pairs={{0,4},{4,0},{1,5},{5,1},{2,6},{6,2},{3,7},{7,3},{8,12},{12,8},{9,1... | collective-permute-start | bytes 6291464 | tf_op jit(solution)/shard_map/ppermute | solution.py:195
  249.7 92.2 %collective-permute-start.25 = (bf16[4096,512]{1,0:T(8,128)(2,1)}, bf16[4096,512]{1,0:T(8,128)(2,1)}, u32[]{:S(2)}, u32[]{:S(2)}) collective-permute-start(bf16[4096,512]{1,0:T(8,128)(2,1)} %param.32), channel_id=1, source_target_pairs={{0,2},{1,3},{2,0},{3,1},{4,6},{5,7},{6,4},{7,5},{8,10},{9,11},{10,... | collective-permute-start | bytes 12582920 | tf_op jit(solution)/shard_map/ppermute | solution.py:195
  396.0 51.5 %collective-permute-start.27 = (bf16[512,2048]{1,0:T(8,128)(2,1)}, bf16[512,2048]{1,0:T(8,128)(2,1)}, u32[]{:S(2)}, u32[]{:S(2)}) collective-permute-start(bf16[512,2048]{1,0:T(8,128)(2,1)} %fusion.25), channel_id=1, source_target_pairs={{0,4},{4,0},{1,5},{5,1},{2,6},{6,2},{3,7},{7,3},{8,12},{12,8},{9,1... | collective-permute-start | bytes 6291464 | tf_op jit(solution)/shard_map/ppermute | solution.py:195
  486.3 45.3 %collective-permute-start.36 = (bf16[512,2048]{1,0:T(8,128)(2,1)S(1)}, bf16[512,2048]{1,0:T(8,128)(2,1)S(1)}, u32[]{:S(2)}, u32[]{:S(2)}) collective-permute-start(bf16[512,2048]{1,0:T(8,128)(2,1)S(1)} %get-tuple-element.153), channel_id=1, source_target_pairs={{0,4},{4,0},{1,5},{5,1},{2,6},{6,2},{3,7},{7,3},{8,12},{12,8},{9,1... | collective-permute-start | bytes 6291464 | tf_op jit(solution)/shard_map/ppermute | solution.py:195
  558.0 64.7 %collective-permute-start.39 = (bf16[2048,512]{1,0:T(8,128)(2,1)}, bf16[2048,512]{1,0:T(8,128)(2,1)}, u32[]{:S(2)}, u32[]{:S(2)}) collective-permute-start(bf16[2048,512]{1,0:T(8,128)(2,1)} %token_product.22), channel_id=1, source_target_pairs={{0,2},{1,3},{2,0},{3,1},{4,6},{5,7},{6,4},{7,5},{8,10},{9,11},{10,... | collective-permute-start | bytes 6291464 | tf_op jit(solution)/shard_map/ppermute | solution.py:195
  565.0 103.7 %collective-permute-start.41 = (bf16[2048,512]{1,0:T(8,128)(2,1)}, bf16[2048,512]{1,0:T(8,128)(2,1)}, u32[]{:S(2)}, u32[]{:S(2)}) collective-permute-start(bf16[2048,512]{1,0:T(8,128)(2,1)} %token_product.23), channel_id=1, source_target_pairs={{0,2},{1,3},{2,0},{3,1},{4,6},{5,7},{6,4},{7,5},{8,10},{9,11},{10,... | collective-permute-start | bytes 6291464 | tf_op jit(solution)/shard_map/ppermute | solution.py:195
  627.8 48.4 %collective-permute-start.42 = (bf16[2048,512]{1,0:T(8,128)(2,1)}, bf16[2048,512]{1,0:T(8,128)(2,1)}, u32[]{:S(2)}, u32[]{:S(2)}) collective-permute-start(bf16[2048,512]{1,0:T(8,128)(2,1)} %fusion.27), channel_id=1, source_target_pairs={{0,8},{24,16},{1,9},{25,17},{2,10},{26,18},{3,11},{27,19},{4,12},{... | collective-permute-start | bytes 6291464 | tf_op jit(solution)/shard_map/ppermute | solution.py:465
  689.8 48.4 %collective-permute-start.40 = (bf16[512,2048]{1,0:T(8,128)(2,1)}, bf16[512,2048]{1,0:T(8,128)(2,1)}, u32[]{:S(2)}, u32[]{:S(2)}) collective-permute-start(bf16[512,2048]{1,0:T(8,128)(2,1)} %fusion.24), channel_id=1, source_target_pairs={{0,4},{4,0},{1,5},{5,1},{2,6},{6,2},{3,7},{7,3},{8,12},{12,8},{9,1... | collective-permute-start | bytes 6291464 | tf_op jit(solution)/shard_map/ppermute | solution.py:195
  690.4 56.4 %collective-permute-start.47 = (bf16[2048,512]{1,0:T(8,128)(2,1)}, bf16[2048,512]{1,0:T(8,128)(2,1)}, u32[]{:S(2)}, u32[]{:S(2)}) collective-permute-start(bf16[2048,512]{1,0:T(8,128)(2,1)} %fusion.28), channel_id=1, source_target_pairs={{0,8},{24,16},{1,9},{25,17},{2,10},{26,18},{3,11},{27,19},{4,12},{... | collective-permute-start | bytes 6291464 | tf_op jit(solution)/shard_map/ppermute | solution.py:465
  696.5 50.3 %collective-permute-start.46 = (bf16[2048,512]{1,0:T(8,128)(2,1)}, bf16[2048,512]{1,0:T(8,128)(2,1)}, u32[]{:S(2)}, u32[]{:S(2)}) collective-permute-start(bf16[2048,512]{1,0:T(8,128)(2,1)} %add_convert_fusion.8), channel_id=1, source_target_pairs={{8,16},{16,8},{9,17},{17,9},{10,18},{18,10},{11,19},{19,11},{12,20... | collective-permute-start | bytes 6291464 | tf_op jit(solution)/shard_map/ppermute | solution.py:472
  704.3 51.1 %collective-permute-start.45 = (bf16[512,2048]{1,0:T(8,128)(2,1)}, bf16[512,2048]{1,0:T(8,128)(2,1)}, u32[]{:S(2)}, u32[]{:S(2)}) collective-permute-start(bf16[512,2048]{1,0:T(8,128)(2,1)} %token_product.28), channel_id=1, source_target_pairs={{0,2},{1,3},{2,0},{3,1},{4,6},{5,7},{6,4},{7,5},{8,10},{9,11},{10,... | collective-permute-start | bytes 6291464 | tf_op jit(solution)/shard_map/ppermute | solution.py:195
  763.7 48.4 %collective-permute-start.49 = (bf16[2048,1024]{1,0:T(8,128)(2,1)}, bf16[2048,1024]{1,0:T(8,128)(2,1)}, u32[]{:S(2)}, u32[]{:S(2)}) collective-permute-start(bf16[2048,1024]{1,0:T(8,128)(2,1)} %token_product.32), channel_id=1, source_target_pairs={{0,1},{1,0},{2,3},{3,2},{4,5},{5,4},{6,7},{7,6},{8,9},{9,8},{10,11... | collective-permute-start | bytes 12582920 | tf_op jit(solution)/shard_map/ppermute | solution.py:195
  763.7 48.4 %collective-permute-start.48 = (bf16[512,2048]{1,0:T(8,128)(2,1)}, bf16[512,2048]{1,0:T(8,128)(2,1)}, u32[]{:S(2)}, u32[]{:S(2)}) collective-permute-start(bf16[512,2048]{1,0:T(8,128)(2,1)} %token_product.29), channel_id=1, source_target_pairs={{0,2},{1,3},{2,0},{3,1},{4,6},{5,7},{6,4},{7,5},{8,10},{9,11},{10,... | collective-permute-start | bytes 6291464 | tf_op jit(solution)/shard_map/ppermute | solution.py:195
  775.0 126.0 %collective-permute-start.88 = (bf16[2048,512]{1,0:T(8,128)(2,1)}, bf16[2048,512]{1,0:T(8,128)(2,1)}, u32[]{:S(2)}, u32[]{:S(2)}) collective-permute-start(bf16[2048,512]{1,0:T(8,128)(2,1)} %add_convert_fusion.7), channel_id=1, source_target_pairs={{8,0},{16,24},{9,1},{17,25},{10,2},{18,26},{11,3},{19,27},{12,4},{... | collective-permute-start | bytes 6291464 | tf_op jit(solution)/shard_map/ppermute | solution.py:480
  776.4 124.6 %collective-permute-start.51 = (bf16[2048,512]{1,0:T(8,128)(2,1)}, bf16[2048,512]{1,0:T(8,128)(2,1)}, u32[]{:S(2)}, u32[]{:S(2)}) collective-permute-start(bf16[2048,512]{1,0:T(8,128)(2,1)} %add_convert_fusion.6), channel_id=1, source_target_pairs={{8,16},{16,8},{9,17},{17,9},{10,18},{18,10},{11,19},{19,11},{12,20... | collective-permute-start | bytes 6291464 | tf_op jit(solution)/shard_map/ppermute | solution.py:472
  778.4 128.8 %collective-permute-start.52 = (bf16[512,2048]{1,0:T(8,128)(2,1)}, bf16[512,2048]{1,0:T(8,128)(2,1)}, u32[]{:S(2)}, u32[]{:S(2)}) collective-permute-start(bf16[512,2048]{1,0:T(8,128)(2,1)} %fusion.29), channel_id=1, source_target_pairs={{0,8},{24,16},{1,9},{25,17},{2,10},{26,18},{3,11},{27,19},{4,12},{... | collective-permute-start | bytes 6291464 | tf_op jit(solution)/shard_map/ppermute | solution.py:465
  816.2 91.1 %collective-permute-start.50 = (bf16[1024,1024]{1,0:T(8,128)(2,1)}, bf16[1024,1024]{1,0:T(8,128)(2,1)}, u32[]{:S(2)}, u32[]{:S(2)}) collective-permute-start(bf16[1024,1024]{1,0:T(8,128)(2,1)} %token_product.33), channel_id=1, source_target_pairs={{0,4},{4,0},{1,5},{5,1},{2,6},{6,2},{3,7},{7,3},{8,12},{12,8},{9,1... | collective-permute-start | bytes 6291464 | tf_op jit(solution)/shard_map/ppermute | solution.py:195
  820.6 100.2 %collective-permute-start.69 = (bf16[512,2048]{1,0:T(8,128)(2,1)}, bf16[512,2048]{1,0:T(8,128)(2,1)}, u32[]{:S(2)}, u32[]{:S(2)}) collective-permute-start(bf16[512,2048]{1,0:T(8,128)(2,1)} %fusion.30), channel_id=1, source_target_pairs={{0,8},{24,16},{1,9},{25,17},{2,10},{26,18},{3,11},{27,19},{4,12},{... | collective-permute-start | bytes 6291464 | tf_op jit(solution)/shard_map/ppermute | solution.py:465
  905.9 50.4 %collective-permute-start.89 = (bf16[2048,512]{1,0:T(8,128)(2,1)}, bf16[2048,512]{1,0:T(8,128)(2,1)}, u32[]{:S(2)}, u32[]{:S(2)}) collective-permute-start(bf16[2048,512]{1,0:T(8,128)(2,1)} %add_convert_fusion.4), channel_id=1, source_target_pairs={{8,0},{16,24},{9,1},{17,25},{10,2},{18,26},{11,3},{19,27},{12,4},{... | collective-permute-start | bytes 6291464 | tf_op jit(solution)/shard_map/ppermute | solution.py:480
  914.1 53.6 %collective-permute-start.53 = (bf16[1024,2048]{1,0:T(8,128)(2,1)}, bf16[1024,2048]{1,0:T(8,128)(2,1)}, u32[]{:S(2)}, u32[]{:S(2)}) collective-permute-start(bf16[1024,2048]{1,0:T(8,128)(2,1)} %token_product.35), channel_id=1, source_target_pairs={{0,1},{1,0},{2,3},{3,2},{4,5},{5,4},{6,7},{7,6},{8,9},{9,8},{10,11... | collective-permute-start | bytes 12582920 | tf_op jit(solution)/shard_map/ppermute | solution.py:195
  925.6 112.7 %collective-permute-start.73 = (bf16[512,2048]{1,0:T(8,128)(2,1)}, bf16[512,2048]{1,0:T(8,128)(2,1)}, u32[]{:S(2)}, u32[]{:S(2)}) collective-permute-start(bf16[512,2048]{1,0:T(8,128)(2,1)} %add_convert_fusion.2), channel_id=1, source_target_pairs={{8,16},{16,8},{9,17},{17,9},{10,18},{18,10},{11,19},{19,11},{12,20... | collective-permute-start | bytes 6291464 | tf_op jit(solution)/shard_map/ppermute | solution.py:472
  966.1 57.7 %collective-permute-start.86 = (bf16[512,2048]{1,0:T(8,128)(2,1)}, bf16[512,2048]{1,0:T(8,128)(2,1)}, u32[]{:S(2)}, u32[]{:S(2)}) collective-permute-start(bf16[512,2048]{1,0:T(8,128)(2,1)} %add_convert_fusion), channel_id=1, source_target_pairs={{8,0},{16,24},{9,1},{17,25},{10,2},{18,26},{11,3},{19,27},{12,4},{... | collective-permute-start | bytes 6291464 | tf_op jit(solution)/shard_map/ppermute | solution.py:480
  979.4 50.0 %collective-permute-start.71 = (bf16[1024,1024]{1,0:T(8,128)(2,1)S(1)}, bf16[1024,1024]{1,0:T(8,128)(2,1)}, u32[]{:S(2)}, u32[]{:S(2)}) collective-permute-start(bf16[1024,1024]{1,0:T(8,128)(2,1)S(1)} %token_product.36), channel_id=1, source_target_pairs={{0,4},{4,0},{1,5},{5,1},{2,6},{6,2},{3,7},{7,3},{8,12},{12,8},{9,1... | collective-permute-start | bytes 6291464 | tf_op jit(solution)/shard_map/ppermute | solution.py:195
  984.3 47.6 %collective-permute-start.57 = (f32[2048,256]{1,0:T(8,128)}, f32[2048,256]{1,0:T(8,128)}, u32[]{:S(2)}, u32[]{:S(2)}) collective-permute-start(f32[2048,256]{1,0:T(8,128)} %slice.390), channel_id=1, source_target_pairs={{0,1},{1,0},{2,3},{3,2},{4,5},{5,4},{6,7},{7,6},{8,9},{9,8},{10,11... | collective-permute-start | bytes 6291464 | tf_op jit(solution)/shard_map/ppermute | solution.py:195
  1058.2 89.5 %collective-permute-start.87 = (bf16[512,2048]{1,0:T(8,128)(2,1)}, bf16[512,2048]{1,0:T(8,128)(2,1)}, u32[]{:S(2)}, u32[]{:S(2)}) collective-permute-start(bf16[512,2048]{1,0:T(8,128)(2,1)} %add_convert_fusion.1), channel_id=1, source_target_pairs={{8,0},{16,24},{9,1},{17,25},{10,2},{18,26},{11,3},{19,27},{12,4},{... | collective-permute-start | bytes 6291464 | tf_op jit(solution)/shard_map/ppermute | solution.py:480
  1062.5 124.6 %collective-permute-start.84 = (bf16[1024,512]{1,0:T(8,128)(2,1)S(1)}, bf16[1024,512]{1,0:T(8,128)(2,1)}, u32[]{:S(2)}, u32[]{:S(2)}) collective-permute-start(bf16[1024,512]{1,0:T(8,128)(2,1)S(1)} %add_convert_fusion.10), channel_id=1, source_target_pairs={{8,0},{16,24},{9,1},{17,25},{10,2},{18,26},{11,3},{19,27},{12,4},{... | collective-permute-start | bytes 3145736 | tf_op jit(solution)/shard_map/ppermute | solution.py:480
  1076.9 55.8 %collective-permute-start.74 = (bf16[512,1024]{1,0:T(8,128)(2,1)}, bf16[512,1024]{1,0:T(8,128)(2,1)}, u32[]{:S(2)}, u32[]{:S(2)}) collective-permute-start(bf16[512,1024]{1,0:T(8,128)(2,1)} %convert_element_type.282), channel_id=1, source_target_pairs={{0,8},{24,16},{1,9},{25,17},{2,10},{26,18},{3,11},{27,19},{4,12},{... | collective-permute-start | bytes 3145736 | tf_op jit(solution)/shard_map/ppermute | solution.py:465
  1149.9 48.3 %collective-permute-start.76 = (bf16[512,1024]{1,0:T(8,128)(2,1)S(1)}, bf16[512,1024]{1,0:T(8,128)(2,1)S(1)}, u32[]{:S(2)}, u32[]{:S(2)}) collective-permute-start(bf16[512,1024]{1,0:T(8,128)(2,1)S(1)} %add_convert_fusion.12), channel_id=1, source_target_pairs={{8,0},{16,24},{9,1},{17,25},{10,2},{18,26},{11,3},{19,27},{12,4},{... | collective-permute-start | bytes 3145736 | tf_op jit(solution)/shard_map/ppermute | solution.py:480
  (195 other events, 3184.8 us)
